TPU v7x, 32 devices: a whole 2x2x4 slice. The times are simulated.
32 devices in a mesh: row: 8 (over z, core), col: 4 (over y, x).
Axes of the slice: x: 2, y: 2, z: 4, core: 2. Of those that a mesh axis runs over, the one named last changes fastest.
Arguments:
- atom_feats: bfloat16 [5120, 128], P(('row', 'col')), may hold values from -6 to 6
- atom_bias: float32 [4, 5120, 128], P(None, ('row', 'col')), may hold values from -5 to 360
- atom_counts: int32 [1280], replicated, may hold values from 1 to 24, 5120 in all
- valid_tokens: int32 [1], replicated, may hold values from 640 to 1280
- pair_in: bfloat16 [256, 1280, 128], P('row', 'col'), may hold values from -6 to 6
- atom_gain: float32 [128], replicated, may hold values from 0.5 to 1.5
- atom_proj: bfloat16 [128, 512], replicated, may hold values from -0.5 to 0.5
- atom_out: bfloat16 [128, 128], replicated, may hold values from -4 to 4
- atom_pool: bfloat16 [128, 384], replicated, may hold values from -0.5 to 0.5
- single_to_pair: bfloat16 [384, 256], replicated, may hold values from -0.3125 to 0.3125
- pair_gains: float32 [3, 128], replicated, may hold values from 0.5 to 1.5
- trans_in: bfloat16 [128, 1024], replicated, may hold values from -0.5 to 0.5
- trans_out: bfloat16 [512, 128], replicated, may hold values from -0.25 to 0.25
- tri_in: bfloat16 [128, 512], replicated, may hold values from -0.5 to 0.5
- tri_out: bfloat16 [128, 128], replicated, may hold values from -0.5 to 0.5
Outputs:
- single: bfloat16 [1280, 384], P('col')
- update: bfloat16 [256, 256, 128], P('row', 'col')
Inputs may be any that keep to these rules, and one draw needn't show every extreme that they name: `atom_counts`: the counts sum to 5120; some token has exactly 24 atoms.
All inputs are finite; a program needn't handle non-finite values.
Results may differ from a plain program's by a relative error of at most 0.0091.
Values may be sent and summed in bfloat16 or wider, within the bound.
No kernel may reach another device: no remote copies, remote signals or barrier semaphores. Data moves between devices by JAX's collectives and lax.ppermute only.
A program may use at most 128 MiB of HBM per device.

v0:
```python
import jax
import jax.numpy as jnp
from jax import lax
from jax.sharding import PartitionSpec as P

QBLOCK = 32
KEYS = 128
RIM = 48


EPS = 1e-05


def padded(shard, sides, width):
    for axis, dim in sides:
        size, length = (lax.axis_size(axis), shard.shape[dim])
        up = [(i, (i + 1) % size) for i in range(size - 1)]
        down = [(j, i) for i, j in up]
        last = lax.slice_in_dim(shard, length - width, length, axis=dim)
        initial = lax.slice_in_dim(shard, 0, width, axis=dim)
        before = lax.ppermute(last, axis, up)
        after = lax.ppermute(initial, axis, down)
        shard = jnp.concatenate([before, shard, after], axis=dim)
    return shard


def normalize(values, gain_row):
    values = values.astype(jnp.float32)
    average = jnp.mean(values, axis=-1, keepdims=True)
    centered = values - average
    variance = jnp.mean(centered * centered, axis=-1, keepdims=True)
    return centered * lax.rsqrt(variance + EPS) * gain_row


def attend(queries, key_vals, gating, atom_bias, first_atom, total_atoms):
    atom_rows, atom_width = queries.shape
    blocks = atom_rows // QBLOCK
    head_count = atom_bias.shape[0]
    head_size = atom_width // head_count
    windowed = jnp.stack(
        [key_vals[QBLOCK * block_id : QBLOCK * block_id + KEYS] for block_id in range(blocks)]
    )
    position = (
        first_atom
        - RIM
        + (jnp.arange(blocks, dtype=jnp.int32) * QBLOCK)[:, None]
        + jnp.arange(KEYS, dtype=jnp.int32)[None, :]
    )
    in_range = (position >= 0) & (position < total_atoms)
    query_heads = queries.reshape(blocks, QBLOCK, head_count, head_size)
    key_heads = windowed[:, :, :atom_width].reshape(blocks, KEYS, head_count, head_size)
    value_heads = windowed[:, :, atom_width:].reshape(blocks, KEYS, head_count, head_size)
    scores = jnp.einsum(
        "bqhd,bkhd->bhqk", query_heads, key_heads, preferred_element_type=jnp.float32
    ) * head_size ** (-0.5)
    bias_rows = atom_bias.reshape(head_count, blocks, QBLOCK, KEYS).transpose(1, 0, 2, 3)
    scores = jnp.where(in_range[:, None, None, :], scores + bias_rows, -1e30)
    row_max = jnp.max(scores, axis=-1, keepdims=True)
    exponent = jnp.exp(scores - row_max)
    weights = (exponent / jnp.sum(exponent, axis=-1, keepdims=True)).astype(jnp.bfloat16)
    blended = jnp.einsum(
        "bhqk,bkhd->bqhd", weights, value_heads, preferred_element_type=jnp.float32
    )
    return (blended.reshape(atom_rows, atom_width) * gating).astype(jnp.bfloat16)


def body(
    atom_feats,
    atom_bias,
    atom_counts,
    valid_tokens,
    pair_in,
    atom_gain,
    atom_proj,
    atom_out,
    atom_pool,
    single_to_pair,
    pair_gains,
    trans_in,
    trans_out,
    tri_in,
    tri_out,
):
    atom_rows, atom_width = atom_feats.shape
    position = lax.axis_index(("row", "col"))
    total_atoms = atom_rows * lax.axis_size(("row", "col"))
    first_atom = position * atom_rows
    normed = normalize(atom_feats, atom_gain).astype(jnp.bfloat16)
    projected = jnp.dot(normed, atom_proj, preferred_element_type=jnp.float32)
    queries = projected[:, :atom_width].astype(jnp.bfloat16)
    gating = jax.nn.sigmoid(projected[:, 3 * atom_width :])
    key_vals = projected[:, atom_width : 3 * atom_width].astype(jnp.bfloat16)
    key_vals = padded(key_vals, ((("row", "col"), 0),), RIM)
    gated = attend(queries, key_vals, gating, atom_bias, first_atom, total_atoms)
    updated = (
        atom_feats.astype(jnp.float32)
        + jnp.dot(gated, atom_out, preferred_element_type=jnp.float32)
    ).astype(jnp.bfloat16)
    hidden = jax.nn.relu(jnp.dot(updated, atom_pool, preferred_element_type=jnp.float32))
    tokens = atom_counts.shape[0]
    token_ends = jnp.cumsum(atom_counts)
    starts = token_ends - atom_counts
    atom_index = first_atom + jnp.arange(atom_rows, dtype=jnp.int32)
    owners = jnp.sum((starts[None, :] <= atom_index[:, None]).astype(jnp.int32), axis=1) - 1
    first_token = owners[0]
    offsets = owners - first_token
    onehot = (offsets[None, :] == jnp.arange(atom_rows, dtype=jnp.int32)[:, None]).astype(
        jnp.float32
    )
    window = jnp.dot(onehot, hidden, precision=lax.Precision.HIGHEST)
    table_sums = jnp.zeros((tokens + atom_rows, hidden.shape[1]), jnp.float32)
    table_sums = lax.dynamic_update_slice_in_dim(table_sums, window, first_token, 0)[:tokens]
    count_float = atom_counts.astype(jnp.float32)
    totals = lax.psum(table_sums, ("row", "col"))
    single_all = (totals / count_float[:, None]).astype(jnp.bfloat16)
    row_dev, tok_col, channels = pair_in.shape
    col_place = lax.axis_index("col")
    row_place = lax.axis_index("row")
    single = lax.dynamic_slice_in_dim(single_all, col_place * tok_col, tok_col)
    row_single = lax.dynamic_slice_in_dim(single_all, row_place * row_dev, row_dev)
    row_terms = jnp.dot(
        row_single, single_to_pair[:, :channels], preferred_element_type=jnp.float32
    )
    col_terms = jnp.dot(single, single_to_pair[:, channels:], preferred_element_type=jnp.float32)
    col_mask = (
        col_place * tok_col + jnp.arange(tok_col, dtype=jnp.int32) < valid_tokens[0]
    ).astype(jnp.float32)[:, None]

    def pair_row(operands):
        row_in, row_add = operands
        paired = (row_in.astype(jnp.float32) + row_add[None, :] + col_terms).astype(jnp.bfloat16)
        normed_row = normalize(paired, pair_gains[0]).astype(jnp.bfloat16)
        gate_up = jnp.dot(normed_row, trans_in, preferred_element_type=jnp.float32)
        inner = (jax.nn.silu(gate_up[:, : 4 * channels]) * gate_up[:, 4 * channels :]).astype(
            jnp.bfloat16
        )
        paired = (
            paired.astype(jnp.float32)
            + jnp.dot(inner, trans_out, preferred_element_type=jnp.float32)
        ).astype(jnp.bfloat16)
        normed_row = normalize(paired, pair_gains[1]).astype(jnp.bfloat16)
        tri_proj = jnp.dot(normed_row, tri_in, preferred_element_type=jnp.float32)
        left_row = (
            jax.nn.sigmoid(tri_proj[:, :channels]) * tri_proj[:, channels : 2 * channels] * col_mask
        ).astype(jnp.bfloat16)
        right_row = (
            jax.nn.sigmoid(tri_proj[:, 2 * channels : 3 * channels])
            * tri_proj[:, 3 * channels :]
            * col_mask
        ).astype(jnp.bfloat16)
        return (left_row, right_row)

    left_ops, right_ops = lax.map(pair_row, (pair_in, row_terms))
    partial_value = jnp.einsum(
        "ikc,jkc->ijc",
        left_ops,
        lax.all_gather(right_ops, "row", axis=0, tiled=True),
        preferred_element_type=jnp.float32,
    )
    summed = lax.psum_scatter(partial_value, "col", scatter_dimension=1, tiled=True)
    normed_out = normalize(summed, pair_gains[2]).astype(jnp.bfloat16)
    update = jnp.dot(normed_out.reshape(-1, channels), tri_out, preferred_element_type=jnp.float32)
    update = update.reshape(summed.shape).astype(jnp.bfloat16)
    return (single, update)


def solution(mesh):
    in_specs = (
        P(("row", "col"), None),
        P(None, ("row", "col"), None),
        P(),
        P(),
        P("row", "col", None),
        P(),
        P(),
        P(),
        P(),
        P(),
        P(),
        P(),
        P(),
        P(),
        P(),
    )
    out_specs = (P("col", None), P("row", "col", None))
    return jax.shard_map(body, mesh=mesh, in_specs=in_specs, out_specs=out_specs, check_vma=False)
```

profile of v0, /device:TPU:8, one launch (start us, length us, event | category | flops | bytes accessed | tf_op | source)
XLA Modules:
  0.0 657.0 jit_solution(9790463930272878575)
XLA Ops:
  10.2 3.4 collective-permute-start
  13.6 4.0 collective-permute-start.1
  26.6 1.8 dynamic_update_slice.10
  28.4 1.4 slice.138
  29.9 132.9 %all-reduce.2.cloned.1.call-done = f32[1280,384]{1,0:T(8,128)} async-done(((f32[1280,384]{1,0:T(8,128)}), f32[1280,384]{1,0:T(8,128)}) %all-reduce.2.cloned.1.call-update) | async-done | bytes 1966096 | tf_op jit(solution)/shard_map/psum | solution.py:114
  162.8 1.8 divide_convert_fusion
  165.9 1.6 fusion.48
  167.6 184.3 %while.13 = (s32[]{:T(128)}, bf16[32,320,128]{2,1,0:T(8,128)(2,1)}, bf16[32,320,128]{2,1,0:T(8,128)(2,1)S(1)}, bf16[32,320,128]{2,1,0:T(8,128)(2,1)}, f32[32,128...) while((s32[]{:T(128)}, bf16[32,320,128]{2,1,0:T(8,128)(2,1)}, ...), condition=%wide.region_13.14_spmd.clone, body=%wide.region_8.13_spmd.clone.sunk | while | flops 170354240 | bytes 5716877 | solution.py:153
  175.8 1.3 fusion.127
  187.3 1.3 fusion.127
  198.8 1.3 fusion.127
  204.6 1.3 fusion.127
  210.3 1.3 fusion.127
  216.1 1.3 fusion.127
  221.8 1.3 fusion.127
  227.6 1.3 fusion.127
  244.8 1.3 fusion.127
  250.6 1.3 fusion.127
  256.4 1.3 fusion.127
  273.7 1.3 fusion.127
  279.4 1.3 fusion.127
  285.2 1.3 fusion.127
  291.0 1.3 fusion.127
  296.7 1.3 fusion.127
  351.9 3.4 copy.46
  355.4 3.8 copy.47
  359.2 212.1 %all-gather.2.cloned.1.call-done = bf16[256,320,128]{1,0,2:T(8,128)(2,1)} async-done(((bf16[32,320,128]{1,0,2:T(8,128)(2,1)}), bf16[256,320,128]{1,0,2:T(8,128)(2,1)}) %all-gather.2.cloned.1.call-update) | async-done | bytes 20971536 | tf_op jit(solution)/shard_map/all_gather | solution.py:157
  571.4 13.8 %convolution_bitcast_fusion = f32[32,256,128]{1,0,2:T(8,128)} fusion(bf16[256,320,128]{1,0,2:T(8,128)(2,1)} %all-gather.2.cloned.1.call-done, bf16[32,320,128]{1,0,2:T(8,128)(2,1)S(1)} %copy.47), kind=kOutput, calls=%fused_computation.54 | convolution fusion | flops 671088640 | bytes 27787264 | tf_op jit(solution)/shard_map/ikc,jkc->ijc/dot_general | solution.py:154
  585.2 6.0 copy.48
  591.8 53.3 %reduce-scatter.2.cloned.1.call-done = f32[32,64,128]{2,0,1:T(8,128)} async-done(((f32[32,256,128]{2,0,1:T(8,128)}), f32[32,64,128]{2,0,1:T(8,128)}) %reduce-scatter.2.cloned.1.call-update) | async-done | bytes 1048592 | tf_op jit(solution)/shard_map/reduce_scatter | solution.py:160
  645.1 1.7 reduce_sum.94
  646.8 1.9 multiply_reduce_fusion.1
  (474 shorter events, 176.1 us)
Async XLA Ops:
  7.2 2.0 copy-start
  7.2 16.5 %copy-start.6 = (f32[4,160,128]{2,1,0:T(8,128)S(1)}, f32[4,160,128]{2,1,0:T(8,128)}, u32[]{:S(2)}) copy-start(f32[4,160,128]{2,1,0:T(8,128)} %param.18) | copy-start | bytes 983044
  7.2 155.7 %all-reduce.2.cloned.1.call-start = ((), (), s32[]{:S(2)}) async-start(), calls=%async_computation.1 | async-start | bytes 3932160 | tf_op jit(solution)/shard_map/psum | solution.py:114
  10.2 13.1 %collective-permute-start = (bf16[48,256]{1,0:T(8,128)(2,1)S(1)}, bf16[48,256]{1,0:T(8,128)(2,1)S(1)}, u32[]{:S(2)}, u32[]{:S(2)}) collective-permute-start(bf16[48,256]{1,0:T(8,128)(2,1)S(1)} %get-tuple-element.126), channel_id=1, source_target_pairs={{0,1},{1,2},{2,3},{3,4},{4,5},{5,6},{6,7},{7,8},{8,9},{9,10},{10,1... | collective-permute-start | bytes 73736 | tf_op jit(solution)/shard_map/ppermute | solution.py:21
  13.6 9.7 %collective-permute-start.1 = (bf16[48,256]{1,0:T(8,128)(2,1)S(1)}, bf16[48,256]{1,0:T(8,128)(2,1)S(1)}, u32[]{:S(2)}, u32[]{:S(2)}) collective-permute-start(bf16[48,256]{1,0:T(8,128)(2,1)S(1)} %get-tuple-element.125), channel_id=1, source_target_pairs={{1,0},{2,1},{3,2},{4,3},{5,4},{6,5},{7,6},{8,7},{9,8},{10,9},{11,1... | collective-permute-start | bytes 73736 | tf_op jit(solution)/shard_map/ppermute | solution.py:22
  23.4 2.5 copy-start.5
  23.4 2.5 copy-start.7
  23.4 2.5 copy-start.8
  29.8 137.7 %copy-start.2 = (bf16[128,1024]{1,0:T(8,128)(2,1)S(1)}, bf16[128,1024]{1,0:T(8,128)(2,1)}, u32[]{:S(2)}) copy-start(bf16[128,1024]{1,0:T(8,128)(2,1)} %param.28) | copy-start | bytes 786436
  29.8 137.7 %copy-start.3 = (bf16[128,512]{1,0:T(8,128)(2,1)S(1)}, bf16[128,512]{1,0:T(8,128)(2,1)}, u32[]{:S(2)}) copy-start(bf16[128,512]{1,0:T(8,128)(2,1)} %param.30) | copy-start | bytes 393220
  29.9 541.5 %all-gather.2.cloned.1.call-start = ((), (), s32[]{:S(2)}) async-start(), calls=%async_computation.2 | async-start | bytes 28311552 | tf_op jit(solution)/shard_map/all_gather | solution.py:157
  164.7 2.9 copy-start.4
  355.3 289.8 %reduce-scatter.2.cloned.1.call-start = ((), (), s32[]{:S(2)}) async-start(), calls=%async_computation.3 | async-start | bytes 5242880 | tf_op jit(solution)/shard_map/reduce_scatter | solution.py:160
  591.1 58.2 %copy-start.9 = (bf16[128,128]{1,0:T(8,128)(2,1)S(1)}, bf16[128,128]{1,0:T(8,128)(2,1)}, u32[]{:S(2)}) copy-start(bf16[128,128]{1,0:T(8,128)(2,1)} %param.31) | copy-start | bytes 98308
  645.1 3.6 copy-start.1
Sparse Core Ops, SparseCore 0:
  30.0 132.8 all-reduce.1
  355.5 215.8 all-gather.1
  591.3 53.8 reduce-scatter.1
where the time goes:
time: 662 us; the launch traced here: 657 us
  waiting for transfers between devices  398 us (60%)
  other arithmetic  106 us (16%)
  matrix products  85.3 us (13%)
  local copies, waits for them, and re-layouts  43.3 us (7%)
  between operations  16.1 us (2%)
  starting transfers between devices  7.48 us (1%)
    all_gather x1, waiting for transfers between devices, body(): lax.all_gather(right_ops, 'row', axis=0, tiled=True)  212 us
    psum x1, waiting for transfers between devices, body(): totals = lax.psum(table_sums, ('row', 'col'))  133 us
    reduce_scatter x1, waiting for transfers between devices, body(): lax.psum_scatter(partial_value, 'col', scatter_dimension=1, tiled=True)  53.3 us
    dot_general x32, matrix products, pair_row(): jnp.dot(inner, trans_out, preferred_element_type=jnp.float32)  42.2 us
    reduce_sum x34, other arithmetic, normalize(): average = jnp.mean(values, axis=-1, keepdims=True)  35.6 us
    mul x33, local copies, waits for them, and re-layouts, normalize(): return centered * lax.rsqrt(variance + EPS) * gain_row  25.1 us
    dynamic_update_slice x32, other arithmetic, body(): left_ops, right_ops = lax.map(pair_row, (pair_in, row_terms))  24.9 us
    convert_element_type x32, other arithmetic, body(): col_mask = (col_place * tok_col + jnp.arange(tok_col, dtype=jnp.int32) <...  21.4 us
  transfers between devices with their start and end apart: 5, of which 3 were waited for; matrix products, arithmetic and copies ran while one was open for 1% of the time, Pallas kernels for 0%

commit v1 on v0

v1 whole, which is shorter than its diff:
```python
import functools

import jax
import jax.numpy as jnp
from jax import lax
from jax.experimental import pallas as pl
from jax.experimental.pallas import tpu as pltpu
from jax.sharding import PartitionSpec as P

QBLOCK = 32
KEYS = 128
RIM = 48
EPS = 1e-05
BF = jnp.bfloat16
F32 = jnp.float32

VMEM = pl.BlockSpec(memory_space=pltpu.VMEM)
SMEM = pl.BlockSpec(memory_space=pltpu.SMEM)
NT = (((1,), (1,)), ((), ()))
TN = (((0,), (0,)), ((), ()))


def params(limit=48):
    return pltpu.CompilerParams(vmem_limit_bytes=limit << 20)


def cost(flops, nbytes):
    return pl.CostEstimate(flops=int(flops), bytes_accessed=int(nbytes), transcendentals=0)


def dot(a, b, dims=(((1,), (0,)), ((), ()))):
    return lax.dot_general(a, b, dims, preferred_element_type=F32)


def normalize(values, gain, axis):
    average = jnp.mean(values, axis=axis, keepdims=True)
    centered = values - average
    variance = jnp.mean(centered * centered, axis=axis, keepdims=True)
    return centered * lax.rsqrt(variance + EPS) * gain


def atom_kernel(heads, info, before, own, after, gain, proj, bias, out_proj, out, feats):
    rows, width = own.shape
    first, total = info[0], info[1]
    feats[0:RIM, :] = before[...]
    feats[RIM : RIM + rows, :] = own[...]
    feats[RIM + rows :, :] = after[...]
    normed = normalize(feats[...].astype(F32), gain[...], -1).astype(BF)
    projected = dot(normed, proj[...])
    queries = projected[RIM : RIM + rows, :width].astype(BF)
    keys = projected[:, width : 2 * width].astype(BF)
    values = projected[:, 2 * width : 3 * width].astype(BF)
    gating = 0.5 + 0.5 * jnp.tanh(0.5 * projected[RIM : RIM + rows, 3 * width :])
    size = width // heads
    head_of = lax.broadcasted_iota(jnp.int32, (QBLOCK, width), 1) // size
    for b in range(rows // QBLOCK):
        lo = QBLOCK * b
        query = queries[lo : lo + QBLOCK].astype(F32)
        stacked = jnp.concatenate(
            [jnp.where(head_of == h, query, 0.0) for h in range(heads)], axis=0
        ).astype(BF)
        scores = dot(stacked, keys[lo : lo + KEYS], NT) * size ** (-0.5)
        scores = scores + jnp.concatenate([bias[h, lo : lo + QBLOCK, :] for h in range(heads)], axis=0)
        slot = lax.broadcasted_iota(jnp.int32, scores.shape, 1) + (first - RIM + lo)
        scores = jnp.where((slot >= 0) & (slot < total), scores, -1e30)
        exponent = jnp.exp(scores - jnp.max(scores, axis=-1, keepdims=True))
        weights = (exponent / jnp.sum(exponent, axis=-1, keepdims=True)).astype(BF)
        mixed = dot(weights, values[lo : lo + KEYS])
        blended = jnp.zeros((QBLOCK, width), F32)
        for h in range(heads):
            blended = jnp.where(head_of == h, mixed[QBLOCK * h : QBLOCK * (h + 1)], blended)
        gated = (blended * gating[lo : lo + QBLOCK]).astype(BF)
        own_rows = own[lo : lo + QBLOCK, :].astype(F32)
        out[lo : lo + QBLOCK, :] = (own_rows + dot(gated, out_proj[...])).astype(BF)


CHUNK = 256


def pool_kernel(
    groups, cols, slab, kz, info, starts, *refs
):
    parts, refs = refs[:groups], refs[groups:]
    other, table_row, table_col, pool, to_pair, single, row_terms, col_terms, atoms, sums = refs
    z, core, col = info[0], info[1], info[2]
    rows = parts[0].shape[0] // cols
    total = rows * cols * 2 * groups
    for d in range(groups):
        zz = lax.rem(z - d + groups, groups)
        for c in range(cols):
            for s in range(2):
                place = (zz * 2 + (core if s == 0 else 1 - core)) * cols + jnp.bitwise_xor(col, c)
                source = (
                    parts[d][rows * c : rows * (c + 1), :]
                    if s == 0
                    else other[rows * (d * cols + c) : rows * (d * cols + c + 1), :]
                )
                atoms[pl.ds(pl.multiple_of(place * rows, 32), rows), :] = source
    atoms[total:, :] = jnp.zeros((atoms.shape[0] - total, atoms.shape[1]), BF)

    def block(table, lo, count, first_token):
        begin = starts[first_token]
        finish = starts[first_token + count]
        opens = table[lo : lo + count, 0:1]
        closes = table[lo : lo + count, 1:2]
        first = lax.div(begin, CHUNK)
        last = lax.div(finish + CHUNK - 1, CHUNK)

        sums[0:count, :] = jnp.zeros((count, sums.shape[1]), F32)

        def step(i, carry):
            base = pl.multiple_of(i * CHUNK, CHUNK)
            hidden = jnp.maximum(dot(atoms[pl.ds(base, CHUNK), :], pool[...]), 0.0)
            high = hidden.astype(BF)
            low = (hidden - high.astype(F32)).astype(BF)
            place = lax.broadcasted_iota(jnp.int32, (count, CHUNK), 1) + base
            hot = jnp.where((place >= opens) & (place < closes), 1.0, 0.0).astype(BF)
            sums[0:count, :] += dot(hot, high) + dot(hot, low)
            return carry

        lax.fori_loop(first, last, step, 0)
        return (sums[0:count, :] / (closes - opens).astype(F32)).astype(BF)

    tokens = single.shape[0]
    half = tokens // 2
    for t in range(2):
        single[half * t : half * (t + 1), :] = block(table_col, half * t, half, col * tokens + half * t)
    width = row_terms.shape[1]
    count = 128
    for t in range(slab // count):
        term = dot(block(table_row, count * t, count, count * t), to_pair[:, :width])
        for u in range(count // 64):
            zz = t * (count // 64) + u
            row_terms[32 * zz : 32 * zz + 32, :] = jnp.where(
                core == 0, term[64 * u : 64 * u + 32], term[64 * u + 32 : 64 * u + 64]
            )
    all_terms = dot(single[...], to_pair[:, width:])
    sums[0:tokens, 0:width] = all_terms
    col_terms[...] = sums[pl.ds(pl.multiple_of(z * kz, 8), kz), 0:width]


def pair_kernel(groups, cols, chunk_at, info, *refs):
    xs, refs = refs[:groups], refs[groups:]
    row_terms, col_terms, gain_in, gain_out, w_in, w_out, w_tri, eye = refs[:8]
    lefts, rights = refs[8 : 8 + cols], refs[8 + cols : 8 + 2 * cols]
    rows_buf, left_buf, right_buf = refs[8 + 2 * cols :]
    z, k_first, valid = info[0], info[1], info[2]
    kb, per, channels = xs[0].shape
    lanes = per * groups
    for d in range(groups):
        zz = lax.rem(z - d + groups, groups)
        rows_buf[:, pl.ds(pl.multiple_of(zz * per, 32), per), :] = xs[d][...]
    at = k_first + chunk_at + pl.program_id(0) * kb
    tile = max(1, 256 // lanes)
    hidden = w_in.shape[0] // 2
    for t in range(0, kb, tile):
        added = [
            (
                rows_buf[t + u].astype(F32) + row_terms[...] + col_terms[t + u : t + u + 1, :]
            ).astype(BF)
            for u in range(tile)
        ]
        paired = dot(eye[...], jnp.concatenate(added, axis=0), NT)
        normed = normalize(paired, gain_in[...], 0).astype(BF)
        gate_up = dot(w_in[...], normed)
        gate = 0.5 * gate_up[:hidden]
        inner = ((gate + gate * jnp.tanh(gate)) * gate_up[hidden:]).astype(BF)
        following = (paired + dot(w_out[...], inner)).astype(BF).astype(F32)
        normed = normalize(following, gain_out[...], 0).astype(BF)
        ops = dot(w_tri[...], normed)
        gate_l = jnp.tanh(0.5 * ops[:channels])
        gate_r = jnp.tanh(0.5 * ops[2 * channels : 3 * channels])
        val_l = ops[channels : 2 * channels]
        val_r = ops[3 * channels :]
        for u in range(tile):
            scale = jnp.where(at + t + u < valid, 0.5, 0.0).astype(F32)
            span = slice(lanes * u, lanes * (u + 1))
            left = val_l[:, span] * scale
            right = val_r[:, span] * scale
            left = left + left * gate_l[:, span]
            right = right + right * gate_r[:, span]
            for w in range(lanes // 128):
                part = slice(128 * w, 128 * (w + 1))
                left_buf[w, pl.ds(t + u, channels, stride=kb), :] = left[:, part]
                right_buf[w, pl.ds(t + u, channels, stride=kb), :] = right[:, part]
    each = channels // cols
    for d in range(cols):
        for w in range(lanes // 128):
            part = slice(128 * w, 128 * (w + 1))
            span = slice(each * kb * d, each * kb * (d + 1))
            lefts[d][:, :, part] = left_buf[w, span, :].reshape(each, kb, 128).astype(BF)
            rights[d][:, :, part] = right_buf[w, span, :].reshape(each, kb, 128).astype(BF)


CGROUP = 16


def triangle_kernel(groups, count, info, *refs):
    lefts, own, other = refs[:count], refs[count : 2 * count], refs[2 * count : 3 * count]
    outs, buf = refs[3 * count : 3 * count + groups], refs[-1]
    z = info[0]
    lanes = lefts[0].shape[2]
    for c in range(CGROUP):
        left = jnp.concatenate([ref[c] for ref in lefts], axis=0)
        for s, side in enumerate((own, other)):
            right = jnp.concatenate([ref[c] for ref in side], axis=0)
            total = dot(left, right, TN)
            for w in range(lanes // 128):
                buf[s * (lanes // 128) + w, pl.ds(c, lanes, stride=CGROUP), :] = total[
                    :, 128 * w : 128 * (w + 1)
                ]
    for d in range(groups):
        zz = lax.rem(z + d, groups)
        for w in range(2 * lanes // 128):
            piece = buf[w, pl.ds(pl.multiple_of(zz * 32 * CGROUP, 32), 32 * CGROUP), :]
            outs[d][:, :, 128 * w : 128 * (w + 1)] = piece.reshape(32, CGROUP, 128).astype(BF)


def gather_kernel(groups, cols, *refs):
    parts, out = refs[:groups], refs[groups]
    total = parts[0][...].astype(F32)
    for d in range(1, groups):
        total = total + parts[d][...].astype(F32)
    half = total.shape[2] // 2
    split = total.shape[0] // 2
    for col in range(cols):
        pieces = [
            total[split * r : split * (r + 1), :, half * s + 32 * col : half * s + 32 * (col + 1)]
            for r in range(2)
            for s in range(2)
        ]
        out[col] = jnp.concatenate(pieces, axis=-1).astype(BF)


def finish_kernel(cols, info, summed, gain, w_out, update):
    core = info[1]
    split = summed.shape[1]
    for r in range(split):
        values = jnp.concatenate([summed[c, r] for c in range(cols)], axis=0).astype(F32)
        normed = normalize(values, gain[...], 0).astype(BF)
        rows = dot(normed, w_out[...], TN).astype(BF)
        for p in range(2):
            for s in range(2):
                at = pl.multiple_of((core if s == 0 else 1 - core) * 32, 32)
                update[split * p + r, pl.ds(at, 32), :] = rows[64 * p + 32 * s : 64 * p + 32 * s + 32]


def body(
    atom_feats,
    atom_bias,
    atom_counts,
    valid_tokens,
    pair_in,
    atom_gain,
    atom_proj,
    atom_out,
    atom_pool,
    single_to_pair,
    pair_gains,
    trans_in,
    trans_out,
    tri_in,
    tri_out,
):
    atom_rows, atom_width = atom_feats.shape
    rows_n, cols = lax.axis_size("row"), lax.axis_size("col")
    groups = rows_n // 2
    row, col = lax.axis_index("row"), lax.axis_index("col")
    z, core = row // 2, row % 2
    position = row * cols + col
    total_atoms = atom_rows * rows_n * cols
    tokens = atom_counts.shape[0]
    row_dev, tok_col, channels = pair_in.shape
    slab = row_dev * rows_n
    kz = tok_col // groups
    lanes = row_dev * groups
    each = channels // cols
    i32 = jnp.int32

    size = rows_n * cols
    up = [(i, i + 1) for i in range(size - 1)]
    down = [(j, i) for i, j in up]
    before = lax.ppermute(atom_feats[atom_rows - RIM :], ("row", "col"), up)
    after = lax.ppermute(atom_feats[:RIM], ("row", "col"), down)

    def shift_z(value, d):
        pairs = [(i, (i + 2 * d) % rows_n) for i in range(rows_n)]
        return lax.ppermute(value, "row", pairs)

    def cross_col(value, d):
        return lax.ppermute(value, "col", [(i, i ^ d) for i in range(cols)])

    def swap_core(value):
        return lax.ppermute(value, "row", [(i, i ^ 1) for i in range(rows_n)])

    turned = pair_in.transpose(1, 0, 2)
    pair_parts = []
    for d in range(groups):
        share = lax.dynamic_slice_in_dim(turned, ((z + d) % groups) * kz, kz, 0)
        pair_parts.append(shift_z(share, d) if d else share)

    heads = atom_bias.shape[0]
    updated = pl.pallas_call(
        functools.partial(atom_kernel, heads),
        out_shape=jax.ShapeDtypeStruct((atom_rows, atom_width), BF),
        in_specs=[SMEM] + [VMEM] * 7,
        out_specs=VMEM,
        scratch_shapes=[pltpu.VMEM((atom_rows + 2 * RIM, atom_width), BF)],
        compiler_params=params(),
        cost_estimate=cost(1e8, 1e6),
        name="atoms",
    )(
        jnp.stack([position * atom_rows, jnp.asarray(total_atoms, i32)]).astype(i32),
        before,
        atom_feats,
        after,
        atom_gain[None, :],
        atom_proj,
        atom_bias,
        atom_out,
    )

    plane = jnp.concatenate([updated] + [cross_col(updated, d) for d in range(1, cols)], axis=0)
    planes = [plane] + [shift_z(plane, d) for d in range(1, groups)]
    other = swap_core(jnp.concatenate(planes, axis=0))

    ends = jnp.cumsum(atom_counts)
    starts = ends - atom_counts
    table = jnp.stack([starts, ends], axis=1)
    starts_all = jnp.concatenate([jnp.zeros((1,), i32), ends]).astype(i32)
    info = jnp.stack([z, core, col]).astype(i32)
    width = atom_pool.shape[1]
    padded_atoms = -(-total_atoms // CHUNK) * CHUNK + 32
    single, row_terms, col_terms = pl.pallas_call(
        functools.partial(pool_kernel, groups, cols, slab, kz),
        out_shape=(
            jax.ShapeDtypeStruct((tok_col, width), BF),
            jax.ShapeDtypeStruct((lanes, channels), F32),
            jax.ShapeDtypeStruct((kz, channels), F32),
        ),
        in_specs=[SMEM, SMEM] + [VMEM] * (groups + 5),
        out_specs=(VMEM, VMEM, VMEM),
        scratch_shapes=[
            pltpu.VMEM((padded_atoms, atom_width), BF),
            pltpu.VMEM((tok_col, width), F32),
        ],
        compiler_params=params(),
        cost_estimate=cost(1e9, 4e6),
        name="pool",
    )(
        info,
        starts_all,
        *planes,
        other,
        table[:slab],
        lax.dynamic_slice_in_dim(table, col * tok_col, tok_col),
        atom_pool,
        single_to_pair,
    )

    order = jnp.bitwise_xor(col, jnp.arange(cols, dtype=i32))
    w_tri = tri_in.T.reshape(4, cols, each, channels)
    w_tri = jnp.take(w_tri, order, axis=1).reshape(4 * channels, channels)
    unit = kz // 5
    tile_lanes = max(256, lanes)
    gain_in = jnp.broadcast_to(pair_gains[0][:, None], (channels, tile_lanes))
    gain_out = jnp.broadcast_to(pair_gains[1][:, None], (channels, tile_lanes))
    pair_info = jnp.stack([z, col * tok_col + z * kz, valid_tokens[0]]).astype(i32)
    eye = jnp.eye(channels, dtype=BF)
    lefts, rights = [], []
    at = 0
    for steps in (1, 2, 2):
        first = at
        whole = lambda *shape: pl.BlockSpec(shape, lambda g: (0,) * len(shape))
        outs = pl.pallas_call(
            functools.partial(pair_kernel, groups, cols, first * unit),
            grid=(steps,),
            out_shape=[jax.ShapeDtypeStruct((each, steps * unit, lanes), BF)] * (2 * cols),
            in_specs=[SMEM]
            + [pl.BlockSpec((unit, row_dev, channels), lambda g, first=first: (first + g, 0, 0))]
            * groups
            + [
                whole(lanes, channels),
                pl.BlockSpec((unit, channels), lambda g, first=first: (first + g, 0)),
                whole(channels, tile_lanes),
                whole(channels, tile_lanes),
                whole(*trans_in.shape[::-1]),
                whole(*trans_out.shape[::-1]),
                whole(4 * channels, channels),
                whole(channels, channels),
            ],
            out_specs=[pl.BlockSpec((each, unit, lanes), lambda g: (0, g, 0))] * (2 * cols),
            scratch_shapes=[
                pltpu.VMEM((unit, lanes, channels), BF),
                pltpu.VMEM((lanes // 128, channels * unit, 128), F32),
                pltpu.VMEM((lanes // 128, channels * unit, 128), F32),
            ],
            compiler_params=params(),
            cost_estimate=cost(steps * unit * lanes * 524288, steps * unit * lanes * channels * 6),
            name="pair",
        )(
            pair_info,
            *pair_parts,
            row_terms,
            col_terms,
            gain_in,
            gain_out,
            trans_in.T,
            trans_out.T,
            w_tri,
            eye,
        )
        at += steps
        for d in range(cols):
            left, right = outs[d], outs[cols + d]
            lefts.append(cross_col(left, d) if d else left)
            rights.append(cross_col(right, d) if d else right)
    others = [swap_core(right) for right in rights]

    count = len(lefts)
    specs = [pl.BlockSpec((CGROUP,) + v.shape[1:], lambda g: (g, 0, 0)) for v in lefts]
    sent = pl.pallas_call(
        functools.partial(triangle_kernel, groups, count),
        grid=(each // CGROUP,),
        out_shape=[jax.ShapeDtypeStruct((row_dev, each, 2 * lanes), BF)] * groups,
        in_specs=[SMEM] + specs * 3,
        out_specs=[pl.BlockSpec((row_dev, CGROUP, 2 * lanes), lambda g: (0, g, 0))] * groups,
        scratch_shapes=[pltpu.VMEM((2 * lanes // 128, lanes * CGROUP, 128), F32)],
        compiler_params=params(),
        cost_estimate=cost(2 * each * lanes * 2 * lanes * tok_col, 2e7),
        name="triangle",
    )(info, *lefts, *rights, *others)
    parts = [shift_z(part, d) if d else part for d, part in enumerate(sent)]
    gathered = pl.pallas_call(
        functools.partial(gather_kernel, groups, cols),
        out_shape=jax.ShapeDtypeStruct((cols, row_dev // 2, each, 128), BF),
        in_specs=[VMEM] * groups,
        out_specs=VMEM,
        compiler_params=params(),
        cost_estimate=cost(1e6, 3e6),
        name="gather",
    )(*parts)
    summed = lax.all_to_all(gathered, "col", split_axis=0, concat_axis=0, tiled=True)
    update = pl.pallas_call(
        functools.partial(finish_kernel, cols),
        out_shape=jax.ShapeDtypeStruct((row_dev, slab // cols, channels), BF),
        in_specs=[SMEM] + [VMEM] * 3,
        out_specs=VMEM,
        compiler_params=params(),
        cost_estimate=cost(1e8, 1e6),
        name="finish",
    )(info, summed, jnp.broadcast_to(pair_gains[2][:, None], (channels, 128)), tri_out)
    return (single, update)


def solution(mesh):
    in_specs = (
        P(("row", "col"), None),
        P(None, ("row", "col"), None),
        P(),
        P(),
        P("row", "col", None),
        P(),
        P(),
        P(),
        P(),
        P(),
        P(),
        P(),
        P(),
        P(),
        P(),
    )
    out_specs = (P("col", None), P("row", "col", None))
    return jax.shard_map(body, mesh=mesh, in_specs=in_specs, out_specs=out_specs, check_vma=False)
```

time: 662 us -> 270 us (0.41)
  waiting for transfers between devices: 398 us -> 123 us
  other arithmetic: 106 us -> 3.12 us
  matrix products: 85.3 us -> 0 us
  Pallas kernels: 0 us -> 59.4 us
  starting transfers between devices: 7.48 us -> 46.6 us
  local copies, waits for them, and re-layouts: 43.3 us -> 23.3 us
  between operations: 16.1 us -> 1.74 us
  blocking collectives: 0 us -> 11.8 us
    all_gather x1 -> x0, waiting for transfers between devices: 212 us -> none  [body(): lax.all_gather(right_ops, 'row', axis=0, tiled=True)]
    psum x1 -> x0, waiting for transfers between devices: 133 us -> none  [body(): totals = lax.psum(table_sums, ('row', 'col'))]
    ppermute x2 -> x45, waiting for transfers between devices: 0.01 us -> 123 us  [the longest x9 85.9 us: shift_z(): return lax.ppermute(value, 'row', pairs)]
    dot_general x105 -> x0, matrix products: 85.3 us -> none  [the longest x32 42.2 us: pair_row(): jnp.dot(inner, trans_out, preferred_element_type=jnp.float32)]
    pallas_call x0 -> x8, Pallas kernels: none -> 59.4 us  [the longest x3 42.1 us: body(): pl.pallas_call(functools.partial(pair_kernel, groups, cols, first * unit)...]
    reduce_scatter x1 -> x0, waiting for transfers between devices: 53.3 us -> none  [body(): lax.psum_scatter(partial_value, 'col', scatter_dimension=1, tiled=True)]
    reduce_sum x101 -> x0, other arithmetic: 53 us -> none  [the longest x34 35.6 us: normalize(): average = jnp.mean(values, axis=-1, keepdims=True)]
    ppermute x2 -> x45, starting transfers between devices: 7.36 us -> 46.6 us  [the longest x21 24.4 us: cross_col(): return lax.ppermute(value, 'col', [(i, i ^ d) for i in range(cols)])]
  transfers between devices with their start and end apart: 5 -> 45, of which waited for: 3 -> 21; matrix products, arithmetic and copies ran while one was open for 1% -> 9% of each run, Pallas kernels for 0% -> 16%
where the time goes in v1:
time: 270 us; the launch traced here: 269 us
  waiting for transfers between devices  123 us (46%)
  Pallas kernels  59.4 us (22%)
  starting transfers between devices  46.6 us (17%)
  local copies, waits for them, and re-layouts  23.3 us (9%)
  blocking collectives  11.8 us (4%)
  other arithmetic  3.12 us (1%)
    ppermute x9, waiting for transfers between devices, shift_z(): return lax.ppermute(value, 'row', pairs)  85.9 us
    pallas_call x3, Pallas kernels, body(): pl.pallas_call(functools.partial(pair_kernel, groups, cols, first * unit)...  42.1 us
    ppermute x21, waiting for transfers between devices, cross_col(): return lax.ppermute(value, 'col', [(i, i ^ d) for i in range(cols)])  35.8 us
    ppermute x21, starting transfers between devices, cross_col(): return lax.ppermute(value, 'col', [(i, i ^ d) for i in range(cols)])  24.4 us
    ppermute x9, starting transfers between devices, shift_z(): return lax.ppermute(value, 'row', pairs)  12 us
    all_to_all x1, blocking collectives, body(): lax.all_to_all(gathered, 'col', split_axis=0, concat_axis=0, tiled=True)  11.8 us
    unnamed x50, local copies, waits for them, and re-layouts  11.3 us
    pallas_call x1, Pallas kernels, body(): pl.pallas_call(functools.partial(pool_kernel, groups, cols, slab, kz), ou...  6.84 us
  transfers between devices with their start and end apart: 45, of which 21 were waited for; matrix products, arithmetic and copies ran while one was open for 9% of the time, Pallas kernels for 16%

profile of v1, /device:TPU:8, one launch (start us, length us, event | category | flops | bytes accessed | tf_op | source)
XLA Modules:
  0.0 269.3 jit_solution(13559341320708696706)
XLA Ops:
  2.0 3.4 %collective-permute-start = (bf16[48,128]{1,0:T(8,128)(2,1)}, bf16[48,128]{1,0:T(8,128)(2,1)S(1)}, u32[]{:S(2)}, u32[]{:S(2)}) collective-permute-start(bf16[48,128]{1,0:T(8,128)(2,1)} %get-tuple-element.71), channel_id=1, source_target_pairs={{0,1},{1,2},{2,3},{3,4},{4,5},{5,6},{6,7},{7,8},{8,9},{9,10},{10,1... | collective-permute-start | bytes 36872 | tf_op jit(solution)/shard_map/ppermute | solution.py:283
  5.4 4.0 %collective-permute-start.1 = (bf16[48,128]{1,0:T(8,128)(2,1)}, bf16[48,128]{1,0:T(8,128)(2,1)S(1)}, u32[]{:S(2)}, u32[]{:S(2)}) collective-permute-start(bf16[48,128]{1,0:T(8,128)(2,1)} %get-tuple-element.70), channel_id=1, source_target_pairs={{1,0},{2,1},{3,2},{4,3},{5,4},{6,5},{7,6},{8,7},{9,8},{10,9},{11,1... | collective-permute-start | bytes 36872 | tf_op jit(solution)/shard_map/ppermute | solution.py:284
  9.4 2.9 %constant_dynamic-slice_fusion = (bf16[32,80,128]{2,1,0:T(8,128)(2,1)}, bf16[32,80,128]{2,1,0:T(8,128)(2,1)S(1)}, bf16[32,80,128]{2,1,0:T(8,128)(2,1)S(1)}, bf16[32,80,128]{2,1,0:T(8,128)(2,1)}) fusion(bf16[32,320,128]{2,1,0:T(8,128)(2,1)} %param.19, s32[]{:T(128)S(6)} %select_n.73, s32[]{:T(128)S(6)} %select_n.71, s32[]{:T(128)S(6)} %select_n.69, ...), kind=kLoop, calls=%fused_computation.31 | loop fusion | bytes 5242896 | tf_op jit(solution)/shard_map/dynamic-slice.3
  21.5 2.1 copy.55
  27.4 2.2 gather_fusion
  33.9 2.2 atoms.1
  37.8 1.8 collective-permute-start.2
  41.1 2.1 collective-permute-start.11
  43.2 3.7 %collective-permute-start.6 = (bf16[640,128]{1,0:T(8,128)(2,1)S(1)}, bf16[640,128]{1,0:T(8,128)(2,1)S(1)}, u32[]{:S(2)}, u32[]{:S(2)}) collective-permute-start(bf16[640,128]{1,0:T(8,128)(2,1)S(1)} %pad_maximum_fusion.refs_0_), channel_id=1, source_target_pairs={{0,16},{4,20},{8,24},{12,28},{16,0},{20,4},{24,8},{28,12},{1,17},{... | collective-permute-start | bytes 491528 | tf_op jit(solution)/shard_map/ppermute | solution.py:288
  46.9 35.9 %collective-permute-done.5.refs_1_ = bf16[640,128]{1,0:T(8,128)(2,1)S(1)} collective-permute-done((bf16[640,128]{1,0:T(8,128)(2,1)S(1)}, bf16[640,128]{1,0:T(8,128)(2,1)S(1)}, u32[]{:S(2)}, u32[]{:S(2)}) %collective-permute-start.5) | collective-permute-done | bytes 163872 | tf_op jit(solution)/shard_map/ppermute | solution.py:288
  84.6 4.0 %collective-permute-done.7.refs_3_ = bf16[640,128]{1,0:T(8,128)(2,1)S(1)} collective-permute-done((bf16[640,128]{1,0:T(8,128)(2,1)S(1)}, bf16[640,128]{1,0:T(8,128)(2,1)S(1)}, u32[]{:S(2)}, u32[]{:S(2)}) %collective-permute-start.7) | collective-permute-done | bytes 163872 | tf_op jit(solution)/shard_map/ppermute | solution.py:288
  90.8 6.8 %pool.1 = (bf16[320,384]{1,0:T(8,128)(2,1)}, f32[128,128]{1,0:T(8,128)S(1)}, f32[80,128]{1,0:T(8,128)S(1)}) custom-call(s32[3]{0:T(128)S(1)} %pad_add_fusion.1.info, s32[1281]{0:T(1024)S(1)} %pad_add_fusion.starts, bf16[640,128]{1,0:T(8,128)(2,1)S(1)} %pad_maximum_fusion.refs_0_, bf16[640,128]{1,0:T(8,128)(2,1)S(1)} %collective-permute-done.5.refs_1_, ...), custom_call_target="tpu_custom_call" | custom-call | flops 1000000000 | bytes 4000000 | tf_op jit(solution)/shard_map/pool/pallas_call | solution.py:334
  97.8 8.5 %pair.3 = (bf16[32,16,128]{2,1,0:T(8,128)(2,1)S(1)}, bf16[32,16,128]{2,1,0:T(8,128)(2,1)S(1)}, bf16[32,16,128]{2,1,0:T(8,128)(2,1)S(1)}, bf16[32,16,128]{2,1,0:T...) custom-call(s32[3]{0:T(128)S(1)} %pad_add_fusion.3.info, ...), custom_call_target="tpu_custom_call" | custom-call | flops 1073741824 | bytes 1572864 | tf_op jit(solution)/shard_map/pair/pallas_call | solution.py:375
  108.1 1.9 collective-permute-start.21
  111.6 16.7 %pair.4 = (bf16[32,32,128]{2,1,0:T(8,128)(2,1)S(1)}, bf16[32,32,128]{2,1,0:T(8,128)(2,1)S(1)}, bf16[32,32,128]{2,1,0:T(8,128)(2,1)S(1)}, bf16[32,32,128]{2,1,0:T...) custom-call(s32[3]{0:T(128)S(1)} %pad_add_fusion.3.info, ...), custom_call_target="tpu_custom_call" | custom-call | flops 2147483648 | bytes 3145728 | tf_op jit(solution)/shard_map/pair/pallas_call | solution.py:375
  128.3 1.8 collective-permute-start.14
  131.2 16.9 %pair.5 = (bf16[32,32,128]{2,1,0:T(8,128)(2,1)S(1)}, bf16[32,32,128]{2,1,0:T(8,128)(2,1)S(1)}, bf16[32,32,128]{2,1,0:T(8,128)(2,1)S(1)}, bf16[32,32,128]{2,1,0:T...) custom-call(s32[3]{0:T(128)S(1)} %pad_add_fusion.3.info, ...), custom_call_target="tpu_custom_call" | custom-call | flops 2147483648 | bytes 3145728 | tf_op jit(solution)/shard_map/pair/pallas_call | solution.py:375
  149.9 1.7 collective-permute-start.17
  153.4 3.9 %collective-permute-done.15.refs_5_ = bf16[32,32,128]{2,1,0:T(8,128)(2,1)S(1)} collective-permute-done((bf16[32,32,128]{2,1,0:T(8,128)(2,1)S(1)}, bf16[32,32,128]{2,1,0:T(8,128)(2,1)S(1)}, u32[]{:S(2)}, u32[]{:S(2)}) %collective-permute-start.15) | collective-permute-done | bytes 262176 | tf_op jit(solution)/shard_map/ppermute | solution.py:291
  158.5 5.6 %collective-permute-done.16.refs_6_ = bf16[32,32,128]{2,1,0:T(8,128)(2,1)S(1)} collective-permute-done((bf16[32,32,128]{2,1,0:T(8,128)(2,1)S(1)}, bf16[32,32,128]{2,1,0:T(8,128)(2,1)S(1)}, u32[]{:S(2)}, u32[]{:S(2)}) %collective-permute-start.16) | collective-permute-done | bytes 262176 | tf_op jit(solution)/shard_map/ppermute | solution.py:291
  166.6 2.0 collective-permute-done.18.refs_9_
  169.8 5.5 %collective-permute-done.19.refs_10_ = bf16[32,32,128]{2,1,0:T(8,128)(2,1)S(1)} collective-permute-done((bf16[32,32,128]{2,1,0:T(8,128)(2,1)S(1)}, bf16[32,32,128]{2,1,0:T(8,128)(2,1)S(1)}, u32[]{:S(2)}, u32[]{:S(2)}) %collective-permute-start.19) | collective-permute-done | bytes 262176 | tf_op jit(solution)/shard_map/ppermute | solution.py:291
  177.8 2.1 collective-permute-done.24.refs_17_
  181.1 5.5 %collective-permute-done.25.refs_18_ = bf16[32,32,128]{2,1,0:T(8,128)(2,1)S(1)} collective-permute-done((bf16[32,32,128]{2,1,0:T(8,128)(2,1)S(1)}, bf16[32,32,128]{2,1,0:T(8,128)(2,1)S(1)}, u32[]{:S(2)}, u32[]{:S(2)}) %collective-permute-start.25) | collective-permute-done | bytes 262176 | tf_op jit(solution)/shard_map/ppermute | solution.py:291
  187.1 4.1 %collective-permute-done.27.refs_21_ = bf16[32,32,128]{2,1,0:T(8,128)(2,1)S(1)} collective-permute-done((bf16[32,32,128]{2,1,0:T(8,128)(2,1)S(1)}, bf16[32,32,128]{2,1,0:T(8,128)(2,1)S(1)}, u32[]{:S(2)}, u32[]{:S(2)}) %collective-permute-start.27) | collective-permute-done | bytes 262176 | tf_op jit(solution)/shard_map/ppermute | solution.py:291
  191.7 5.2 %collective-permute-done.29.refs_23_ = bf16[32,32,128]{2,1,0:T(8,128)(2,1)S(1)} collective-permute-done((bf16[32,32,128]{2,1,0:T(8,128)(2,1)S(1)}, bf16[32,32,128]{2,1,0:T(8,128)(2,1)S(1)}, u32[]{:S(2)}, u32[]{:S(2)}) %collective-permute-start.29) | collective-permute-done | bytes 262176 | tf_op jit(solution)/shard_map/ppermute | solution.py:291
  200.3 5.7 %triangle.1 = (bf16[32,32,256]{2,1,0:T(8,128)(2,1)}, bf16[32,32,256]{2,1,0:T(8,128)(2,1)}, bf16[32,32,256]{2,1,0:T(8,128)(2,1)}, bf16[32,32,256]{2,1,0:T(8,128)(2,1)}) custom-call(s32[3]{0:T(128)S(1)} %pad_add_fusion.1.info, bf16[32,16,128]{2,1,0:T(8,128)(2,1)S(1)} %get-tuple-element.36.refs_0_, bf16[32,16,128]{2,1,0:T(8,128)(2,1)S(1)} %collective-permute-done.12.refs_1_, ...), custom_call_target="tpu_custom_call" | custom-call | flops 671088640 | bytes 20000000 | tf_op jit(solution)/shard_map/triangle/pallas_call | solution.py:422
  206.0 2.0 collective-permute-start.42
  209.5 33.5 %collective-permute-done.42.refs_1_ = bf16[32,32,256]{2,1,0:T(8,128)(2,1)S(1)} collective-permute-done((bf16[32,32,256]{2,1,0:T(8,128)(2,1)}, bf16[32,32,256]{2,1,0:T(8,128)(2,1)S(1)}, u32[]{:S(2)}, u32[]{:S(2)}) %collective-permute-start.42) | collective-permute-done | bytes 524320 | tf_op jit(solution)/shard_map/ppermute | solution.py:288
  243.1 10.4 %collective-permute-done.43.refs_2_ = bf16[32,32,256]{2,1,0:T(8,128)(2,1)S(1)} collective-permute-done((bf16[32,32,256]{2,1,0:T(8,128)(2,1)}, bf16[32,32,256]{2,1,0:T(8,128)(2,1)S(1)}, u32[]{:S(2)}, u32[]{:S(2)}) %collective-permute-start.43) | collective-permute-done | bytes 524320 | tf_op jit(solution)/shard_map/ppermute | solution.py:288
  255.5 11.8 %all_to_all.5.summed = bf16[4,16,32,128]{3,2,1,0:T(8,128)(2,1)S(1)} all-to-all(bf16[4,16,32,128]{3,2,1,0:T(8,128)(2,1)S(1)} %gather.11), channel_id=1, replica_groups=mesh['row'=8,'col'=4] {'col'}, dimensions={0} | all-to-all | bytes 1048576 | tf_op jit(solution)/shard_map/all_to_all | solution.py:443
  267.4 1.9 finish.1
  (147 shorter events, 49.6 us)
Async XLA Ops:
  2.0 31.9 %collective-permute-start = (bf16[48,128]{1,0:T(8,128)(2,1)}, bf16[48,128]{1,0:T(8,128)(2,1)S(1)}, u32[]{:S(2)}, u32[]{:S(2)}) collective-permute-start(bf16[48,128]{1,0:T(8,128)(2,1)} %get-tuple-element.71), channel_id=1, source_target_pairs={{0,1},{1,2},{2,3},{3,4},{4,5},{5,6},{6,7},{7,8},{8,9},{9,10},{10,1... | collective-permute-start | bytes 36872 | tf_op jit(solution)/shard_map/ppermute | solution.py:283
  5.4 28.5 %collective-permute-start.1 = (bf16[48,128]{1,0:T(8,128)(2,1)}, bf16[48,128]{1,0:T(8,128)(2,1)S(1)}, u32[]{:S(2)}, u32[]{:S(2)}) collective-permute-start(bf16[48,128]{1,0:T(8,128)(2,1)} %get-tuple-element.70), channel_id=1, source_target_pairs={{1,0},{2,1},{3,2},{4,3},{5,4},{6,5},{7,6},{8,7},{9,8},{10,9},{11,1... | collective-permute-start | bytes 36872 | tf_op jit(solution)/shard_map/ppermute | solution.py:284
  13.4 84.3 %collective-permute-start.9 = (bf16[80,32,128]{2,1,0:T(8,128)(2,1)}, bf16[80,32,128]{2,1,0:T(8,128)(2,1)S(1)}, u32[]{:S(2)}, u32[]{:S(2)}) collective-permute-start(bf16[80,32,128]{2,1,0:T(8,128)(2,1)} %bitcast.42), channel_id=1, source_target_pairs={{0,8},{4,12},{8,16},{12,20},{16,24},{20,28},{24,0},{28,4},{1,9},{5... | collective-permute-start | bytes 1966088 | tf_op jit(solution)/shard_map/ppermute | solution.py:288
  16.0 81.6 %collective-permute-start.10 = (bf16[80,32,128]{2,1,0:T(8,128)(2,1)}, bf16[80,32,128]{2,1,0:T(8,128)(2,1)S(1)}, u32[]{:S(2)}, u32[]{:S(2)}) collective-permute-start(bf16[80,32,128]{2,1,0:T(8,128)(2,1)} %bitcast.41), channel_id=1, source_target_pairs={{0,16},{4,20},{8,24},{12,28},{16,0},{20,4},{24,8},{28,12},{1,17},{... | collective-permute-start | bytes 1966088 | tf_op jit(solution)/shard_map/ppermute | solution.py:288
  41.1 56.6 %collective-permute-start.11 = (bf16[80,32,128]{2,1,0:T(8,128)(2,1)}, bf16[80,32,128]{2,1,0:T(8,128)(2,1)S(1)}, u32[]{:S(2)}, u32[]{:S(2)}) collective-permute-start(bf16[80,32,128]{2,1,0:T(8,128)(2,1)} %bitcast.55), channel_id=1, source_target_pairs={{0,24},{4,28},{8,0},{12,4},{16,8},{20,12},{24,16},{28,20},{1,25},{... | collective-permute-start | bytes 1966088 | tf_op jit(solution)/shard_map/ppermute | solution.py:288
  43.1 39.7 %collective-permute-start.5 = (bf16[640,128]{1,0:T(8,128)(2,1)S(1)}, bf16[640,128]{1,0:T(8,128)(2,1)S(1)}, u32[]{:S(2)}, u32[]{:S(2)}) collective-permute-start(bf16[640,128]{1,0:T(8,128)(2,1)S(1)} %pad_maximum_fusion.refs_0_), channel_id=1, source_target_pairs={{0,8},{4,12},{8,16},{12,20},{16,24},{20,28},{24,0},{28,4},{1,9},{5... | collective-permute-start | bytes 491528 | tf_op jit(solution)/shard_map/ppermute | solution.py:288
  43.2 41.4 %collective-permute-start.6 = (bf16[640,128]{1,0:T(8,128)(2,1)S(1)}, bf16[640,128]{1,0:T(8,128)(2,1)S(1)}, u32[]{:S(2)}, u32[]{:S(2)}) collective-permute-start(bf16[640,128]{1,0:T(8,128)(2,1)S(1)} %pad_maximum_fusion.refs_0_), channel_id=1, source_target_pairs={{0,16},{4,20},{8,24},{12,28},{16,0},{20,4},{24,8},{28,12},{1,17},{... | collective-permute-start | bytes 491528 | tf_op jit(solution)/shard_map/ppermute | solution.py:288
  106.3 22.0 %collective-permute-start.12 = (bf16[32,16,128]{2,1,0:T(8,128)(2,1)S(1)}, bf16[32,16,128]{2,1,0:T(8,128)(2,1)S(1)}, u32[]{:S(2)}, u32[]{:S(2)}) collective-permute-start(bf16[32,16,128]{2,1,0:T(8,128)(2,1)S(1)} %get-tuple-element.37), channel_id=1, source_target_pairs={{0,1},{1,0},{2,3},{3,2},{4,5},{5,4},{6,7},{7,6},{8,9},{9,8},{10,11... | collective-permute-start | bytes 393224 | tf_op jit(solution)/shard_map/ppermute | solution.py:291
  107.5 22.7 %collective-permute-start.13 = (bf16[32,16,128]{2,1,0:T(8,128)(2,1)S(1)}, bf16[32,16,128]{2,1,0:T(8,128)(2,1)S(1)}, u32[]{:S(2)}, u32[]{:S(2)}) collective-permute-start(bf16[32,16,128]{2,1,0:T(8,128)(2,1)S(1)} %get-tuple-element.38), channel_id=1, source_target_pairs={{0,2},{1,3},{2,0},{3,1},{4,6},{5,7},{6,4},{7,5},{8,10},{9,11},{10,... | collective-permute-start | bytes 393224 | tf_op jit(solution)/shard_map/ppermute | solution.py:291
  108.1 22.0 %collective-permute-start.21 = (bf16[32,16,128]{2,1,0:T(8,128)(2,1)S(1)}, bf16[32,16,128]{2,1,0:T(8,128)(2,1)S(1)}, u32[]{:S(2)}, u32[]{:S(2)}) collective-permute-start(bf16[32,16,128]{2,1,0:T(8,128)(2,1)S(1)} %get-tuple-element.49), channel_id=1, source_target_pairs={{0,1},{1,0},{2,3},{3,2},{4,5},{5,4},{6,7},{7,6},{8,9},{9,8},{10,11... | collective-permute-start | bytes 393224 | tf_op jit(solution)/shard_map/ppermute | solution.py:291
  110.0 20.7 %collective-permute-start.22 = (bf16[32,16,128]{2,1,0:T(8,128)(2,1)S(1)}, bf16[32,16,128]{2,1,0:T(8,128)(2,1)S(1)}, u32[]{:S(2)}, u32[]{:S(2)}) collective-permute-start(bf16[32,16,128]{2,1,0:T(8,128)(2,1)S(1)} %get-tuple-element.50), channel_id=1, source_target_pairs={{0,2},{1,3},{2,0},{3,1},{4,6},{5,7},{6,4},{7,5},{8,10},{9,11},{10,... | collective-permute-start | bytes 393224 | tf_op jit(solution)/shard_map/ppermute | solution.py:291
  110.4 20.3 %collective-permute-start.23 = (bf16[32,16,128]{2,1,0:T(8,128)(2,1)S(1)}, bf16[32,16,128]{2,1,0:T(8,128)(2,1)S(1)}, u32[]{:S(2)}, u32[]{:S(2)}) collective-permute-start(bf16[32,16,128]{2,1,0:T(8,128)(2,1)S(1)} %get-tuple-element.51), channel_id=1, source_target_pairs={{0,3},{1,2},{2,1},{3,0},{4,7},{5,6},{6,5},{7,4},{8,11},{9,10},{10,... | collective-permute-start | bytes 393224 | tf_op jit(solution)/shard_map/ppermute | solution.py:291
  128.3 19.8 %collective-permute-start.14 = (bf16[32,16,128]{2,1,0:T(8,128)(2,1)S(1)}, bf16[32,16,128]{2,1,0:T(8,128)(2,1)S(1)}, u32[]{:S(2)}, u32[]{:S(2)}) collective-permute-start(bf16[32,16,128]{2,1,0:T(8,128)(2,1)S(1)} %get-tuple-element.39), channel_id=1, source_target_pairs={{0,3},{1,2},{2,1},{3,0},{4,7},{5,6},{6,5},{7,4},{8,11},{9,10},{10,... | collective-permute-start | bytes 393224 | tf_op jit(solution)/shard_map/ppermute | solution.py:291
  130.1 19.1 %collective-permute-start.30 = (bf16[32,16,128]{2,1,0:T(8,128)(2,1)S(1)}, bf16[32,16,128]{2,1,0:T(8,128)(2,1)S(1)}, u32[]{:S(2)}, u32[]{:S(2)}) collective-permute-start(bf16[32,16,128]{2,1,0:T(8,128)(2,1)S(1)} %get-tuple-element.48.refs_12_), channel_id=1, source_target_pairs={{0,4},{4,0},{8,12},{12,8},{16,20},{20,16},{24,28},{28,24},{1,5},{5... | collective-permute-start | bytes 393224 | tf_op jit(solution)/shard_map/ppermute | solution.py:294
  130.2 19.8 %collective-permute-start.31 = (bf16[32,16,128]{2,1,0:T(8,128)(2,1)S(1)}, bf16[32,16,128]{2,1,0:T(8,128)(2,1)S(1)}, u32[]{:S(2)}, u32[]{:S(2)}) collective-permute-start(bf16[32,16,128]{2,1,0:T(8,128)(2,1)S(1)} %collective-permute-done.21.refs_13_), channel_id=1, source_target_pairs={{0,4},{4,0},{8,12},{12,8},{16,20},{20,16},{24,28},{28,24},{1,5},{5... | collective-permute-start | bytes 393224 | tf_op jit(solution)/shard_map/ppermute | solution.py:294
  130.7 21.0 %collective-permute-start.32 = (bf16[32,16,128]{2,1,0:T(8,128)(2,1)S(1)}, bf16[32,16,128]{2,1,0:T(8,128)(2,1)S(1)}, u32[]{:S(2)}, u32[]{:S(2)}) collective-permute-start(bf16[32,16,128]{2,1,0:T(8,128)(2,1)S(1)} %collective-permute-done.22.refs_14_), channel_id=1, source_target_pairs={{0,4},{4,0},{8,12},{12,8},{16,20},{20,16},{24,28},{28,24},{1,5},{5... | collective-permute-start | bytes 393224 | tf_op jit(solution)/shard_map/ppermute | solution.py:294
  130.7 22.0 %collective-permute-start.33 = (bf16[32,16,128]{2,1,0:T(8,128)(2,1)S(1)}, bf16[32,16,128]{2,1,0:T(8,128)(2,1)S(1)}, u32[]{:S(2)}, u32[]{:S(2)}) collective-permute-start(bf16[32,16,128]{2,1,0:T(8,128)(2,1)S(1)} %collective-permute-done.23.refs_15_), channel_id=1, source_target_pairs={{0,4},{4,0},{8,12},{12,8},{16,20},{20,16},{24,28},{28,24},{1,5},{5... | collective-permute-start | bytes 393224 | tf_op jit(solution)/shard_map/ppermute | solution.py:294
  149.3 14.8 %collective-permute-start.16 = (bf16[32,32,128]{2,1,0:T(8,128)(2,1)S(1)}, bf16[32,32,128]{2,1,0:T(8,128)(2,1)S(1)}, u32[]{:S(2)}, u32[]{:S(2)}) collective-permute-start(bf16[32,32,128]{2,1,0:T(8,128)(2,1)S(1)} %get-tuple-element.42), channel_id=1, source_target_pairs={{0,2},{1,3},{2,0},{3,1},{4,6},{5,7},{6,4},{7,5},{8,10},{9,11},{10,... | collective-permute-start | bytes 786440 | tf_op jit(solution)/shard_map/ppermute | solution.py:291
  149.9 15.1 %collective-permute-start.17 = (bf16[32,32,128]{2,1,0:T(8,128)(2,1)S(1)}, bf16[32,32,128]{2,1,0:T(8,128)(2,1)S(1)}, u32[]{:S(2)}, u32[]{:S(2)}) collective-permute-start(bf16[32,32,128]{2,1,0:T(8,128)(2,1)S(1)} %get-tuple-element.43), channel_id=1, source_target_pairs={{0,3},{1,2},{2,1},{3,0},{4,7},{5,6},{6,5},{7,4},{8,11},{9,10},{10,... | collective-permute-start | bytes 786440 | tf_op jit(solution)/shard_map/ppermute | solution.py:291
  151.7 16.9 %collective-permute-start.18 = (bf16[32,32,128]{2,1,0:T(8,128)(2,1)S(1)}, bf16[32,32,128]{2,1,0:T(8,128)(2,1)S(1)}, u32[]{:S(2)}, u32[]{:S(2)}) collective-permute-start(bf16[32,32,128]{2,1,0:T(8,128)(2,1)S(1)} %get-tuple-element.45), channel_id=1, source_target_pairs={{0,1},{1,0},{2,3},{3,2},{4,5},{5,4},{6,7},{7,6},{8,9},{9,8},{10,11... | collective-permute-start | bytes 786440 | tf_op jit(solution)/shard_map/ppermute | solution.py:291
  152.8 22.6 %collective-permute-start.19 = (bf16[32,32,128]{2,1,0:T(8,128)(2,1)S(1)}, bf16[32,32,128]{2,1,0:T(8,128)(2,1)S(1)}, u32[]{:S(2)}, u32[]{:S(2)}) collective-permute-start(bf16[32,32,128]{2,1,0:T(8,128)(2,1)S(1)} %get-tuple-element.46), channel_id=1, source_target_pairs={{0,2},{1,3},{2,0},{3,1},{4,6},{5,7},{6,4},{7,5},{8,10},{9,11},{10,... | collective-permute-start | bytes 786440 | tf_op jit(solution)/shard_map/ppermute | solution.py:291
  157.3 18.9 %collective-permute-start.20 = (bf16[32,32,128]{2,1,0:T(8,128)(2,1)S(1)}, bf16[32,32,128]{2,1,0:T(8,128)(2,1)S(1)}, u32[]{:S(2)}, u32[]{:S(2)}) collective-permute-start(bf16[32,32,128]{2,1,0:T(8,128)(2,1)S(1)} %get-tuple-element.47), channel_id=1, source_target_pairs={{0,3},{1,2},{2,1},{3,0},{4,7},{5,6},{6,5},{7,4},{8,11},{9,10},{10,... | collective-permute-start | bytes 786440 | tf_op jit(solution)/shard_map/ppermute | solution.py:291
  164.1 15.8 %collective-permute-start.24 = (bf16[32,32,128]{2,1,0:T(8,128)(2,1)S(1)}, bf16[32,32,128]{2,1,0:T(8,128)(2,1)S(1)}, u32[]{:S(2)}, u32[]{:S(2)}) collective-permute-start(bf16[32,32,128]{2,1,0:T(8,128)(2,1)S(1)} %get-tuple-element.53), channel_id=1, source_target_pairs={{0,1},{1,0},{2,3},{3,2},{4,5},{5,4},{6,7},{7,6},{8,9},{9,8},{10,11... | collective-permute-start | bytes 786440 | tf_op jit(solution)/shard_map/ppermute | solution.py:291
  165.0 21.5 %collective-permute-start.25 = (bf16[32,32,128]{2,1,0:T(8,128)(2,1)S(1)}, bf16[32,32,128]{2,1,0:T(8,128)(2,1)S(1)}, u32[]{:S(2)}, u32[]{:S(2)}) collective-permute-start(bf16[32,32,128]{2,1,0:T(8,128)(2,1)S(1)} %get-tuple-element.54), channel_id=1, source_target_pairs={{0,2},{1,3},{2,0},{3,1},{4,6},{5,7},{6,4},{7,5},{8,10},{9,11},{10,... | collective-permute-start | bytes 786440 | tf_op jit(solution)/shard_map/ppermute | solution.py:291
  168.6 18.0 %collective-permute-start.26 = (bf16[32,32,128]{2,1,0:T(8,128)(2,1)S(1)}, bf16[32,32,128]{2,1,0:T(8,128)(2,1)S(1)}, u32[]{:S(2)}, u32[]{:S(2)}) collective-permute-start(bf16[32,32,128]{2,1,0:T(8,128)(2,1)S(1)} %get-tuple-element.55), channel_id=1, source_target_pairs={{0,3},{1,2},{2,1},{3,0},{4,7},{5,6},{6,5},{7,4},{8,11},{9,10},{10,... | collective-permute-start | bytes 786440 | tf_op jit(solution)/shard_map/ppermute | solution.py:291
  175.3 15.8 %collective-permute-start.27 = (bf16[32,32,128]{2,1,0:T(8,128)(2,1)S(1)}, bf16[32,32,128]{2,1,0:T(8,128)(2,1)S(1)}, u32[]{:S(2)}, u32[]{:S(2)}) collective-permute-start(bf16[32,32,128]{2,1,0:T(8,128)(2,1)S(1)} %get-tuple-element.57), channel_id=1, source_target_pairs={{0,1},{1,0},{2,3},{3,2},{4,5},{5,4},{6,7},{7,6},{8,9},{9,8},{10,11... | collective-permute-start | bytes 786440 | tf_op jit(solution)/shard_map/ppermute | solution.py:291
  176.3 15.3 %collective-permute-start.28 = (bf16[32,32,128]{2,1,0:T(8,128)(2,1)S(1)}, bf16[32,32,128]{2,1,0:T(8,128)(2,1)S(1)}, u32[]{:S(2)}, u32[]{:S(2)}) collective-permute-start(bf16[32,32,128]{2,1,0:T(8,128)(2,1)S(1)} %get-tuple-element.58), channel_id=1, source_target_pairs={{0,2},{1,3},{2,0},{3,1},{4,6},{5,7},{6,4},{7,5},{8,10},{9,11},{10,... | collective-permute-start | bytes 786440 | tf_op jit(solution)/shard_map/ppermute | solution.py:291
  179.9 17.0 %collective-permute-start.29 = (bf16[32,32,128]{2,1,0:T(8,128)(2,1)S(1)}, bf16[32,32,128]{2,1,0:T(8,128)(2,1)S(1)}, u32[]{:S(2)}, u32[]{:S(2)}) collective-permute-start(bf16[32,32,128]{2,1,0:T(8,128)(2,1)S(1)} %get-tuple-element.59), channel_id=1, source_target_pairs={{0,3},{1,2},{2,1},{3,0},{4,7},{5,6},{6,5},{7,4},{8,11},{9,10},{10,... | collective-permute-start | bytes 786440 | tf_op jit(solution)/shard_map/ppermute | solution.py:291
  186.6 10.9 %collective-permute-start.38 = (bf16[32,32,128]{2,1,0:T(8,128)(2,1)S(1)}, bf16[32,32,128]{2,1,0:T(8,128)(2,1)S(1)}, u32[]{:S(2)}, u32[]{:S(2)}) collective-permute-start(bf16[32,32,128]{2,1,0:T(8,128)(2,1)S(1)} %get-tuple-element.56.refs_20_), channel_id=1, source_target_pairs={{0,4},{4,0},{8,12},{12,8},{16,20},{20,16},{24,28},{28,24},{1,5},{5... | collective-permute-start | bytes 786440 | tf_op jit(solution)/shard_map/ppermute | solution.py:294
  206.0 37.1 %collective-permute-start.42 = (bf16[32,32,256]{2,1,0:T(8,128)(2,1)}, bf16[32,32,256]{2,1,0:T(8,128)(2,1)S(1)}, u32[]{:S(2)}, u32[]{:S(2)}) collective-permute-start(bf16[32,32,256]{2,1,0:T(8,128)(2,1)} %get-tuple-element.61), channel_id=1, source_target_pairs={{0,8},{4,12},{8,16},{12,20},{16,24},{20,28},{24,0},{28,4},{1,9},{5... | collective-permute-start | bytes 1572872 | tf_op jit(solution)/shard_map/ppermute | solution.py:288
  208.0 45.5 %collective-permute-start.43 = (bf16[32,32,256]{2,1,0:T(8,128)(2,1)}, bf16[32,32,256]{2,1,0:T(8,128)(2,1)S(1)}, u32[]{:S(2)}, u32[]{:S(2)}) collective-permute-start(bf16[32,32,256]{2,1,0:T(8,128)(2,1)} %get-tuple-element.62), channel_id=1, source_target_pairs={{0,16},{4,20},{8,24},{12,28},{16,0},{20,4},{24,8},{28,12},{1,17},{... | collective-permute-start | bytes 1572872 | tf_op jit(solution)/shard_map/ppermute | solution.py:288
  208.0 45.8 %collective-permute-start.44 = (bf16[32,32,256]{2,1,0:T(8,128)(2,1)}, bf16[32,32,256]{2,1,0:T(8,128)(2,1)S(1)}, u32[]{:S(2)}, u32[]{:S(2)}) collective-permute-start(bf16[32,32,256]{2,1,0:T(8,128)(2,1)} %get-tuple-element.63), channel_id=1, source_target_pairs={{0,24},{4,28},{8,0},{12,4},{16,8},{20,12},{24,16},{28,20},{1,25},{... | collective-permute-start | bytes 1572872 | tf_op jit(solution)/shard_map/ppermute | solution.py:288
  (30 other events, 374.2 us)

commit v2 on v1

--- a/solution.py
+++ b/solution.py
@@ -139,12 +139,11 @@
     col_terms[...] = sums[pl.ds(pl.multiple_of(z * kz, 8), kz), 0:width]
 
 
-def pair_kernel(groups, cols, chunk_at, info, *refs):
+def pair_kernel(groups, cols, halves, chunk_at, info, *refs):
     xs, refs = refs[:groups], refs[groups:]
     row_terms, col_terms, gain_in, gain_out, w_in, w_out, w_tri, eye = refs[:8]
-    lefts, rights = refs[8 : 8 + cols], refs[8 + cols : 8 + 2 * cols]
-    rows_buf, left_buf, right_buf = refs[8 + 2 * cols :]
-    z, k_first, valid = info[0], info[1], info[2]
+    outs, (left_buf, right_buf, rows_buf) = refs[8:-3], refs[-3:]
+    k_first, valid, z, col = info[0], info[1], info[2], info[3]
     kb, per, channels = xs[0].shape
     lanes = per * groups
     for d in range(groups):
@@ -153,7 +152,8 @@
     at = k_first + chunk_at + pl.program_id(0) * kb
     tile = max(1, 256 // lanes)
     hidden = w_in.shape[0] // 2
-    for t in range(0, kb, tile):
+
+    def opening(t):
         added = [
             (
                 rows_buf[t + u].astype(F32) + row_terms[...] + col_terms[t + u : t + u + 1, :]
@@ -162,7 +162,9 @@
         ]
         paired = dot(eye[...], jnp.concatenate(added, axis=0), NT)
         normed = normalize(paired, gain_in[...], 0).astype(BF)
-        gate_up = dot(w_in[...], normed)
+        return paired, dot(w_in[...], normed)
+
+    def closing(t, paired, gate_up):
         gate = 0.5 * gate_up[:hidden]
         inner = ((gate + gate * jnp.tanh(gate)) * gate_up[hidden:]).astype(BF)
         following = (paired + dot(w_out[...], inner)).astype(BF).astype(F32)
@@ -183,37 +185,50 @@
                 part = slice(128 * w, 128 * (w + 1))
                 left_buf[w, pl.ds(t + u, channels, stride=kb), :] = left[:, part]
                 right_buf[w, pl.ds(t + u, channels, stride=kb), :] = right[:, part]
+
+    ahead = opening(0)
+    for t in range(0, kb, tile):
+        held = ahead
+        if t + tile < kb:
+            ahead = opening(t + tile)
+        closing(t, *held)
     each = channels // cols
+    hc = each // 2
     for d in range(cols):
-        for w in range(lanes // 128):
-            part = slice(128 * w, 128 * (w + 1))
-            span = slice(each * kb * d, each * kb * (d + 1))
-            lefts[d][:, :, part] = left_buf[w, span, :].reshape(each, kb, 128).astype(BF)
-            rights[d][:, :, part] = right_buf[w, span, :].reshape(each, kb, 128).astype(BF)
-
-
-CGROUP = 16
+        for h in range(2):
+            if halves == 2 and h == 1:
+                out, at = outs[1 + d], (0, 0)
+                first = (jnp.bitwise_xor(col, d) * each + hc) * kb
+            else:
+                out, at = outs[0], (d, h)
+                first = (d * each + h * hc) * kb
+            span = pl.ds(pl.multiple_of(first, 8), hc * kb)
+            for w in range(lanes // 128):
+                part = slice(128 * w, 128 * (w + 1))
+                for side, buf in enumerate((left_buf, right_buf)):
+                    piece = buf[w, span, :].reshape(hc, kb, 128)
+                    out[at[0], at[1], side, :, :, part] = piece.astype(BF)
 
 
 def triangle_kernel(groups, count, info, *refs):
-    lefts, own, other = refs[:count], refs[count : 2 * count], refs[2 * count : 3 * count]
-    outs, buf = refs[3 * count : 3 * count + groups], refs[-1]
+    own, other = refs[:count], refs[count : -groups - 1]
+    outs, buf = refs[-groups - 1 : -1], refs[-1]
     z = info[0]
-    lanes = lefts[0].shape[2]
-    for c in range(CGROUP):
-        left = jnp.concatenate([ref[c] for ref in lefts], axis=0)
+    hc, lanes = own[0].shape[3], own[0].shape[5]
+    for c in range(hc):
+        left = jnp.concatenate([ref[d, 0, 0, c] for ref in own for d in range(ref.shape[0])], axis=0)
         for s, side in enumerate((own, other)):
-            right = jnp.concatenate([ref[c] for ref in side], axis=0)
+            right = jnp.concatenate([ref[d, 0, 1, c] for ref in side for d in range(ref.shape[0])], axis=0)
             total = dot(left, right, TN)
             for w in range(lanes // 128):
-                buf[s * (lanes // 128) + w, pl.ds(c, lanes, stride=CGROUP), :] = total[
+                buf[s * (lanes // 128) + w, pl.ds(c, lanes, stride=hc), :] = total[
                     :, 128 * w : 128 * (w + 1)
                 ]
     for d in range(groups):
         zz = lax.rem(z + d, groups)
         for w in range(2 * lanes // 128):
-            piece = buf[w, pl.ds(pl.multiple_of(zz * 32 * CGROUP, 32), 32 * CGROUP), :]
-            outs[d][:, :, 128 * w : 128 * (w + 1)] = piece.reshape(32, CGROUP, 128).astype(BF)
+            piece = buf[w, pl.ds(pl.multiple_of(zz * 32 * hc, 32), 32 * hc), :]
+            outs[d][:, :, 128 * w : 128 * (w + 1)] = piece.reshape(32, hc, 128).astype(BF)
 
 
 def gather_kernel(groups, cols, *refs):
@@ -232,11 +247,13 @@
         out[col] = jnp.concatenate(pieces, axis=-1).astype(BF)
 
 
-def finish_kernel(cols, info, summed, gain, w_out, update):
+def finish_kernel(cols, info, first, second, gain, w_out, update):
     core = info[1]
-    split = summed.shape[1]
+    split = first.shape[1]
     for r in range(split):
-        values = jnp.concatenate([summed[c, r] for c in range(cols)], axis=0).astype(F32)
+        values = jnp.concatenate(
+            [half[c, r].astype(F32) for c in range(cols) for half in (first, second)], axis=0
+        )
         normed = normalize(values, gain[...], 0).astype(BF)
         rows = dot(normed, w_out[...], TN).astype(BF)
         for p in range(2):
@@ -293,11 +310,24 @@
     def swap_core(value):
         return lax.ppermute(value, "row", [(i, i ^ 1) for i in range(rows_n)])
 
-    turned = pair_in.transpose(1, 0, 2)
-    pair_parts = []
-    for d in range(groups):
-        share = lax.dynamic_slice_in_dim(turned, ((z + d) % groups) * kz, kz, 0)
-        pair_parts.append(shift_z(share, d) if d else share)
+    unit = kz // 5
+    chunks = ((0, 2), (2, 3))
+
+    def spread_z(pieces):
+        return [shift_z(piece, d) if d else piece for d, piece in enumerate(pieces)]
+
+    def spread_col(value):
+        return lax.all_to_all(value, "col", split_axis=0, concat_axis=0, tiled=True)
+
+    def shares(z, first, steps):
+        pieces = []
+        for d in range(groups):
+            start = ((z + d) % groups) * kz + first * unit
+            piece = lax.dynamic_slice_in_dim(pair_in, start, steps * unit, 1)
+            pieces.append(piece.transpose(1, 0, 2))
+        return pieces
+
+    pair_parts = [spread_z(shares(z, *chunks[0]))]
 
     heads = atom_bias.shape[0]
     updated = pl.pallas_call(
@@ -320,9 +350,25 @@
         atom_out,
     )
 
+    updated, z_later, trans_in, trans_out, tri_in, gains = lax.optimization_barrier(
+        (updated, z, trans_in, trans_out, tri_in, pair_gains)
+    )
     plane = jnp.concatenate([updated] + [cross_col(updated, d) for d in range(1, cols)], axis=0)
+    plane, pair_parts[0] = lax.optimization_barrier((plane, pair_parts[0]))
     planes = [plane] + [shift_z(plane, d) for d in range(1, groups)]
+    later = [shares(z_later, *chunk) for chunk in chunks[1:]]
+    tile_lanes = max(256, lanes)
+    weights = [
+        jnp.broadcast_to(gains[0][:, None], (channels, tile_lanes)),
+        jnp.broadcast_to(gains[1][:, None], (channels, tile_lanes)),
+        trans_in.T,
+        trans_out.T,
+        tri_in.T,
+        jnp.eye(channels, dtype=BF),
+    ]
+    planes, later, weights = lax.optimization_barrier((planes, later, weights))
     other = swap_core(jnp.concatenate(planes, axis=0))
+    pair_parts += [spread_z(pieces) for pieces in later]
 
     ends = jnp.cumsum(atom_counts)
     starts = ends - atom_counts
@@ -345,7 +391,7 @@
             pltpu.VMEM((tok_col, width), F32),
         ],
         compiler_params=params(),
-        cost_estimate=cost(1e9, 4e6),
+        cost_estimate=cost(1e3, 1e3),
         name="pool",
     )(
         info,
@@ -358,27 +404,38 @@
         single_to_pair,
     )
 
-    order = jnp.bitwise_xor(col, jnp.arange(cols, dtype=i32))
-    w_tri = tri_in.T.reshape(4, cols, each, channels)
-    w_tri = jnp.take(w_tri, order, axis=1).reshape(4 * channels, channels)
-    unit = kz // 5
-    tile_lanes = max(256, lanes)
-    gain_in = jnp.broadcast_to(pair_gains[0][:, None], (channels, tile_lanes))
-    gain_out = jnp.broadcast_to(pair_gains[1][:, None], (channels, tile_lanes))
-    pair_info = jnp.stack([z, col * tok_col + z * kz, valid_tokens[0]]).astype(i32)
-    eye = jnp.eye(channels, dtype=BF)
-    lefts, rights = [], []
-    at = 0
-    for steps in (1, 2, 2):
-        first = at
+    pair_info = jnp.stack([col * tok_col + z * kz, valid_tokens[0], z, col]).astype(i32)
+    hc = each // 2
+    operands = []
+
+    def swap_joined(values):
+        return swap_core(jnp.concatenate(values, axis=0) if len(values) > 1 else values[0])
+
+
+    def exchange(values):
+        operands.append([spread_col(values[0])])
+        if len(values) > 1:
+            got = [cross_col(value, d) if d else value for d, value in enumerate(values[1:])]
+            operands.append(got)
+
+    for call, (first, steps) in enumerate(chunks):
+        halves = 2 if call == len(chunks) - 1 else 1
+        inner = 2 // halves
+        counts = [cols] + [1] * cols * (halves - 1)
+        parts = pair_parts[call]
+        if call:
+            exchange(outs)
+            _, parts = lax.optimization_barrier((outs, parts))
         whole = lambda *shape: pl.BlockSpec(shape, lambda g: (0,) * len(shape))
         outs = pl.pallas_call(
-            functools.partial(pair_kernel, groups, cols, first * unit),
+            functools.partial(pair_kernel, groups, cols, halves, first * unit),
             grid=(steps,),
-            out_shape=[jax.ShapeDtypeStruct((each, steps * unit, lanes), BF)] * (2 * cols),
+            out_shape=[
+                jax.ShapeDtypeStruct((blocks, inner, 2, hc, steps * unit, lanes), BF)
+                for blocks in counts
+            ],
             in_specs=[SMEM]
-            + [pl.BlockSpec((unit, row_dev, channels), lambda g, first=first: (first + g, 0, 0))]
-            * groups
+            + [pl.BlockSpec((unit, row_dev, channels), lambda g: (g, 0, 0))] * groups
             + [
                 whole(lanes, channels),
                 pl.BlockSpec((unit, channels), lambda g, first=first: (first + g, 0)),
@@ -389,67 +446,81 @@
                 whole(4 * channels, channels),
                 whole(channels, channels),
             ],
-            out_specs=[pl.BlockSpec((each, unit, lanes), lambda g: (0, g, 0))] * (2 * cols),
+            out_specs=[
+                pl.BlockSpec((blocks, inner, 2, hc, unit, lanes), lambda g: (0, 0, 0, 0, g, 0))
+                for blocks in counts
+            ],
             scratch_shapes=[
-                pltpu.VMEM((unit, lanes, channels), BF),
                 pltpu.VMEM((lanes // 128, channels * unit, 128), F32),
                 pltpu.VMEM((lanes // 128, channels * unit, 128), F32),
+                pltpu.VMEM((unit, lanes, channels), BF),
             ],
             compiler_params=params(),
-            cost_estimate=cost(steps * unit * lanes * 524288, steps * unit * lanes * channels * 6),
+            cost_estimate=cost(*((1e3, 1e3) if call == 0 else (3e10, 1e6))),
             name="pair",
         )(
             pair_info,
-            *pair_parts,
+            *parts,
             row_terms,
             col_terms,
-            gain_in,
-            gain_out,
-            trans_in.T,
-            trans_out.T,
-            w_tri,
-            eye,
+            *weights,
         )
-        at += steps
-        for d in range(cols):
-            left, right = outs[d], outs[cols + d]
-            lefts.append(cross_col(left, d) if d else left)
-            rights.append(cross_col(right, d) if d else right)
-    others = [swap_core(right) for right in rights]
-
-    count = len(lefts)
-    specs = [pl.BlockSpec((CGROUP,) + v.shape[1:], lambda g: (g, 0, 0)) for v in lefts]
-    sent = pl.pallas_call(
-        functools.partial(triangle_kernel, groups, count),
-        grid=(each // CGROUP,),
-        out_shape=[jax.ShapeDtypeStruct((row_dev, each, 2 * lanes), BF)] * groups,
-        in_specs=[SMEM] + specs * 3,
-        out_specs=[pl.BlockSpec((row_dev, CGROUP, 2 * lanes), lambda g: (0, g, 0))] * groups,
-        scratch_shapes=[pltpu.VMEM((2 * lanes // 128, lanes * CGROUP, 128), F32)],
-        compiler_params=params(),
-        cost_estimate=cost(2 * each * lanes * 2 * lanes * tok_col, 2e7),
-        name="triangle",
-    )(info, *lefts, *rights, *others)
-    parts = [shift_z(part, d) if d else part for d, part in enumerate(sent)]
-    gathered = pl.pallas_call(
-        functools.partial(gather_kernel, groups, cols),
-        out_shape=jax.ShapeDtypeStruct((cols, row_dev // 2, each, 128), BF),
-        in_specs=[VMEM] * groups,
-        out_specs=VMEM,
-        compiler_params=params(),
-        cost_estimate=cost(1e6, 3e6),
-        name="gather",
-    )(*parts)
-    summed = lax.all_to_all(gathered, "col", split_axis=0, concat_axis=0, tiled=True)
+    for at in range(len(operands)):
+        operands[at], outs = lax.optimization_barrier((operands[at], outs))
+        operands[at] = (operands[at], [swap_joined(operands[at])])
+    exchange(outs)
+    sent = None
+
+    def finish_sum(parts):
+        gathered = pl.pallas_call(
+            functools.partial(gather_kernel, groups, cols),
+            out_shape=jax.ShapeDtypeStruct((cols, row_dev // 2, hc, 128), BF),
+            in_specs=[VMEM] * groups,
+            out_specs=VMEM,
+            compiler_params=params(),
+            cost_estimate=cost(1e6, 3e6),
+            name="gather",
+        )(*parts)
+        return spread_col(gathered)
+
+    summed = []
+    last = len(chunks) - 1
+    for h in range(2):
+        late = operands[last + h]
+        if h:
+            parts = spread_z(sent)
+            late, parts[groups // 2] = lax.optimization_barrier((late, parts[groups // 2]))
+            summed.append(finish_sum(parts))
+        pairs = operands[:last] + [(late, [swap_joined(late)])]
+        own, others = sum([p[0] for p in pairs], []), sum([p[1] for p in pairs], [])
+        specs = [
+            pl.BlockSpec(
+                v.shape[:1] + (1,) + v.shape[2:],
+                lambda g, at=h * (v.shape[1] - 1): (0, at, 0, 0, 0, 0),
+            )
+            for v in own + others
+        ]
+        sent = pl.pallas_call(
+            functools.partial(triangle_kernel, groups, len(own)),
+            grid=(1,),
+            out_shape=[jax.ShapeDtypeStruct((row_dev, hc, 2 * lanes), BF)] * groups,
+            in_specs=[SMEM] + specs,
+            out_specs=[pl.BlockSpec((row_dev, hc, 2 * lanes), lambda g: (0, 0, 0))] * groups,
+            scratch_shapes=[pltpu.VMEM((2 * lanes // 128, lanes * hc, 128), F32)],
+            compiler_params=params(),
+            cost_estimate=cost(4 * hc * lanes * lanes * tok_col, 1e7),
+            name="triangle",
+        )(info, *own, *others)
+    summed.append(finish_sum(spread_z(sent)))
     update = pl.pallas_call(
         functools.partial(finish_kernel, cols),
         out_shape=jax.ShapeDtypeStruct((row_dev, slab // cols, channels), BF),
-        in_specs=[SMEM] + [VMEM] * 3,
+        in_specs=[SMEM] + [VMEM] * 4,
         out_specs=VMEM,
         compiler_params=params(),
         cost_estimate=cost(1e8, 1e6),
         name="finish",
-    )(info, summed, jnp.broadcast_to(pair_gains[2][:, None], (channels, 128)), tri_out)
+    )(info, *summed, jnp.broadcast_to(gains[2][:, None], (channels, 128)), tri_out)
     return (single, update)
 
 

time: 270 us -> 203 us (0.75)
  waiting for transfers between devices: 123 us -> 82.1 us
  Pallas kernels: 59.4 us -> 46.4 us
  local copies, waits for them, and re-layouts: 23.3 us -> 16.6 us
  blocking collectives: 11.8 us -> 8.6 us
    ppermute x9 -> x15, waiting for transfers between devices: 85.9 us -> 46 us  [shift_z(): return lax.ppermute(value, 'row', pairs)]
    ppermute x21 -> x6, waiting for transfers between devices: 35.8 us -> 15.2 us  [cross_col(): return lax.ppermute(value, 'col', [(i, i ^ d) for i in range(cols)])]
    all_to_all x0 -> x3, waiting for transfers between devices: none -> 19.6 us  [spread_col(): return lax.all_to_all(value, 'col', split_axis=0, concat_axis=0, tiled=True)]
    ppermute x21 -> x6, starting transfers between devices: 24.4 us -> 5.92 us  [cross_col(): return lax.ppermute(value, 'col', [(i, i ^ d) for i in range(cols)])]
    pallas_call x5 -> x6, Pallas kernels: 48.5 us -> 35.4 us  [the longest x2 27.6 us: body(): pl.pallas_call(functools.partial(pair_kernel, groups, cols, halves, first...]
    all_to_all x0 -> x3, starting transfers between devices: none -> 11.7 us  [spread_col(): return lax.all_to_all(value, 'col', split_axis=0, concat_axis=0, tiled=True)]
    ppermute x9 -> x15, starting transfers between devices: 12 us -> 18.9 us  [shift_z(): return lax.ppermute(value, 'row', pairs)]
    gather x2 -> x0, local copies, waits for them, and re-layouts: 3.81 us -> none  [body(): w_tri = jnp.take(w_tri, order, axis=1).reshape(4 * channels, channels)]
  transfers between devices with their start and end apart: 45 -> 30, of which waited for: 21 -> 18; matrix products, arithmetic and copies ran while one was open for 9% -> 5% of each run, Pallas kernels for 16% -> 22%
where the time goes in v2:
time: 203 us; the launch traced here: 202 us
  waiting for transfers between devices  82.1 us (40%)
  Pallas kernels  46.4 us (23%)
  starting transfers between devices  44.1 us (22%)
  local copies, waits for them, and re-layouts  16.6 us (8%)
  blocking collectives  8.6 us (4%)
  other arithmetic  2.57 us (1%)
    ppermute x15, waiting for transfers between devices, shift_z(): return lax.ppermute(value, 'row', pairs)  46 us
    pallas_call x2, Pallas kernels, body(): pl.pallas_call(functools.partial(pair_kernel, groups, cols, halves, first...  27.6 us
    all_to_all x3, waiting for transfers between devices, spread_col(): return lax.all_to_all(value, 'col', split_axis=0, concat_axis=0, tiled=True)  19.6 us
    ppermute x15, starting transfers between devices, shift_z(): return lax.ppermute(value, 'row', pairs)  18.9 us
    ppermute x6, waiting for transfers between devices, cross_col(): return lax.ppermute(value, 'col', [(i, i ^ d) for i in range(cols)])  15.2 us
    all_to_all x3, starting transfers between devices, spread_col(): return lax.all_to_all(value, 'col', split_axis=0, concat_axis=0, tiled=True)  11.7 us
    unnamed x63, local copies, waits for them, and re-layouts  8.88 us
    all_to_all x1, blocking collectives, spread_col(): return lax.all_to_all(value, 'col', split_axis=0, concat_axis=0, tiled=True)  8.6 us
  transfers between devices with their start and end apart: 30, of which 18 were waited for; matrix products, arithmetic and copies ran while one was open for 5% of the time, Pallas kernels for 22%

profile of v2, /device:TPU:8, one launch (start us, length us, event | category | flops | bytes accessed | tf_op | source)
XLA Modules:
  0.0 202.2 jit_solution(16483067578926810162)
XLA Ops:
  1.4 3.4 %collective-permute-start = (bf16[48,128]{1,0:T(8,128)(2,1)S(1)}, bf16[48,128]{1,0:T(8,128)(2,1)S(1)}, u32[]{:S(2)}, u32[]{:S(2)}) collective-permute-start(bf16[48,128]{1,0:T(8,128)(2,1)S(1)} %get-tuple-element.125), channel_id=1, source_target_pairs={{0,1},{1,2},{2,3},{3,4},{4,5},{5,6},{6,7},{7,8},{8,9},{9,10},{10,1... | collective-permute-start | bytes 36872 | tf_op jit(solution)/shard_map/ppermute | solution.py:300
  4.8 4.0 %collective-permute-start.1 = (bf16[48,128]{1,0:T(8,128)(2,1)S(1)}, bf16[48,128]{1,0:T(8,128)(2,1)S(1)}, u32[]{:S(2)}, u32[]{:S(2)}) collective-permute-start(bf16[48,128]{1,0:T(8,128)(2,1)S(1)} %get-tuple-element.124), channel_id=1, source_target_pairs={{1,0},{2,1},{3,2},{4,3},{5,4},{6,5},{7,6},{8,7},{9,8},{10,9},{11,1... | collective-permute-start | bytes 36872 | tf_op jit(solution)/shard_map/ppermute | solution.py:301
  11.0 1.6 collective-permute-start.5
  15.2 2.0 %collective-permute-start.7 = (bf16[32,32,128]{2,1,0:T(8,128)(2,1)}, bf16[32,32,128]{2,1,0:T(8,128)(2,1)S(1)}, u32[]{:S(2)}, u32[]{:S(2)}) collective-permute-start(bf16[32,32,128]{2,1,0:T(8,128)(2,1)} %bitcast.41), channel_id=1, source_target_pairs={{0,24},{4,28},{8,0},{12,4},{16,8},{20,12},{24,16},{28,20},{1,25},{... | collective-permute-start | bytes 786440 | tf_op jit(solution)/shard_map/ppermute | solution.py:305
  18.7 2.2 %atoms.1 = bf16[160,128]{1,0:T(8,128)(2,1)S(1)} custom-call(s32[2]{0:T(128)S(1)} %pad_add_fusion.2.info, bf16[48,128]{1,0:T(8,128)(2,1)S(1)} %collective-permute-done.before, bf16[160,128]{1,0:T(8,128)(2,1)S(1)} %copy-done.7, bf16[48,128]{1,0:T(8,128)(2,1)S(1)} %collective-permute-done.1.after, f32[1,128]{1,0:T(1,128)S(1)} %bitcast.53, ...), custom_call_target="tpu_custom_call" | custom-call | flops 100000000 | bytes 1000000 | tf_op jit(solution)/shard_map/atoms/pallas_call | solution.py:333
  30.9 3.6 %collective-permute-done.6.refs_2_ = bf16[32,32,128]{2,1,0:T(8,128)(2,1)S(1)} collective-permute-done((bf16[32,32,128]{2,1,0:T(8,128)(2,1)}, bf16[32,32,128]{2,1,0:T(8,128)(2,1)S(1)}, u32[]{:S(2)}, u32[]{:S(2)}) %collective-permute-start.6) | collective-permute-done | bytes 262176 | tf_op jit(solution)/shard_map/ppermute | solution.py:305
  36.2 2.4 %collective-permute-start.9 = (bf16[640,128]{1,0:T(8,128)(2,1)S(1)}, bf16[640,128]{1,0:T(8,128)(2,1)S(1)}, u32[]{:S(2)}, u32[]{:S(2)}) collective-permute-start(bf16[640,128]{1,0:T(8,128)(2,1)S(1)} %pad_maximum_fusion.2.refs_0_), channel_id=1, source_target_pairs={{0,16},{4,20},{8,24},{12,28},{16,0},{20,4},{24,8},{28,12},{1,17},{... | collective-permute-start | bytes 491528 | tf_op jit(solution)/shard_map/ppermute | solution.py:305
  38.6 2.0 collective-permute-start.10
  41.0 2.2 %collective-permute-done.8.refs_1_ = bf16[640,128]{1,0:T(8,128)(2,1)S(1)} collective-permute-done((bf16[640,128]{1,0:T(8,128)(2,1)S(1)}, bf16[640,128]{1,0:T(8,128)(2,1)S(1)}, u32[]{:S(2)}, u32[]{:S(2)}) %collective-permute-start.8) | collective-permute-done | bytes 163872 | tf_op jit(solution)/shard_map/ppermute | solution.py:305
  43.2 7.4 %collective-permute-done.9.refs_2_ = bf16[640,128]{1,0:T(8,128)(2,1)S(1)} collective-permute-done((bf16[640,128]{1,0:T(8,128)(2,1)S(1)}, bf16[640,128]{1,0:T(8,128)(2,1)S(1)}, u32[]{:S(2)}, u32[]{:S(2)}) %collective-permute-start.9) | collective-permute-done | bytes 163872 | tf_op jit(solution)/shard_map/ppermute | solution.py:305
  53.3 2.1 %collective-permute-start.13 = (bf16[48,32,128]{2,1,0:T(8,128)(2,1)}, bf16[48,32,128]{2,1,0:T(8,128)(2,1)}, u32[]{:S(2)}, u32[]{:S(2)}) collective-permute-start(bf16[48,32,128]{2,1,0:T(8,128)(2,1)} %get-tuple-element.84), channel_id=1, source_target_pairs={{0,16},{4,20},{8,24},{12,28},{16,0},{20,4},{24,8},{28,12},{1,17},{... | collective-permute-start | bytes 1179656 | tf_op jit(solution)/shard_map/ppermute | solution.py:305
  55.3 2.0 collective-permute-start.14
  59.4 6.8 %pool.1 = (bf16[320,384]{1,0:T(8,128)(2,1)}, f32[128,128]{1,0:T(8,128)S(1)}, f32[80,128]{1,0:T(8,128)S(1)}) custom-call(s32[3]{0:T(128)S(1)} %pad_add_fusion.1.info, s32[1281]{0:T(1024)S(1)} %pad_add_fusion.starts, bf16[640,128]{1,0:T(8,128)(2,1)S(1)} %pad_maximum_fusion.2.refs_0_, bf16[640,128]{1,0:T(8,128)(2,1)S(1)} %collective-permute-done.8.refs_1_, ...), custom_call_target="tpu_custom_call" | custom-call | flops 1000 | bytes 1000 | tf_op jit(solution)/shard_map/pool/pallas_call | solution.py:380
  66.3 11.1 %pair.2 = bf16[4,2,2,16,32,128]{5,4,3,2,1,0:T(8,128)(2,1)} custom-call(s32[4]{0:T(128)S(1)} %pad_add_fusion.3.info, bf16[32,32,128]{2,1,0:T(8,128)(2,1)S(1)} %bitcast.46, bf16[32,32,128]{2,1,0:T(8,128)(2,1)S(1)} %collective-permute-done.5.refs_1_, bf16[32,32,128]{2,1,0:T(8,128)(2,1)S(1)} %copy-done.2, bf16[32,32,128]{2,1,0:T(8,128)(2,1)S(1)} %copy-done.4, ...), custom_call_target="tpu_custom_call" | custom-call | flops 1000 | bytes 1000 | tf_op jit(solution)/shard_map/pair/pallas_call | solution.py:430
  78.6 4.6 %all-to-all-start = ((bf16[4,2,2,16,32,128]{5,4,3,2,1,0:T(8,128)(2,1)}), bf16[4,2,2,16,32,128]{5,4,3,2,1,0:T(8,128)(2,1)}, u32[]{:S(2)}, u32[]{:S(2)}) async-start(bf16[4,2,2,16,32,128]{5,4,3,2,1,0:T(8,128)(2,1)} %pair.2), calls=%async_computation | async-start | bytes 4194304 | tf_op jit(solution)/shard_map/all_to_all | solution.py:320
  83.3 4.8 %collective-permute-done.13.refs_2_ = bf16[48,32,128]{2,1,0:T(8,128)(2,1)} collective-permute-done((bf16[48,32,128]{2,1,0:T(8,128)(2,1)}, bf16[48,32,128]{2,1,0:T(8,128)(2,1)}, u32[]{:S(2)}, u32[]{:S(2)}) %collective-permute-start.13) | collective-permute-done | bytes 393248 | tf_op jit(solution)/shard_map/ppermute | solution.py:305
  88.2 2.5 %collective-permute-done.14.refs_3_ = bf16[48,32,128]{2,1,0:T(8,128)(2,1)} collective-permute-done((bf16[48,32,128]{2,1,0:T(8,128)(2,1)}, bf16[48,32,128]{2,1,0:T(8,128)(2,1)}, u32[]{:S(2)}, u32[]{:S(2)}) %collective-permute-start.14) | collective-permute-done | bytes 393248 | tf_op jit(solution)/shard_map/ppermute | solution.py:305
  92.3 16.5 %pair.3 = (bf16[4,1,2,16,48,128]{5,4,3,2,1,0:T(8,128)(2,1)}, bf16[1,1,2,16,48,128]{5,4,3,2,1,0:T(8,128)(2,1)S(1)}, bf16[1,1,2,16,48,128]{5,4,3,2,1,0:T(8,128)(2,...) custom-call(s32[4]{0:T(128)S(1)} %pad_add_fusion.3.info, ...), custom_call_target="tpu_custom_call" | custom-call | flops 30000001024 | bytes 1000000 | tf_op jit(solution)/shard_map/pair/pallas_call | solution.py:430
  110.3 3.7 %all-to-all-start.1 = ((bf16[4,1,2,16,48,128]{5,4,3,2,1,0:T(8,128)(2,1)}), bf16[4,1,2,16,48,128]{5,4,3,2,1,0:T(8,128)(2,1)S(1)}, u32[]{:S(2)}, u32[]{:S(2)}) async-start(bf16[4,1,2,16,48,128]{5,4,3,2,1,0:T(8,128)(2,1)} %get-tuple-element.96), calls=%async_computation.1 | async-start | bytes 3145728 | tf_op jit(solution)/shard_map/all_to_all | solution.py:320
  114.1 19.6 %all-to-all-done.1.refs_1_ = bf16[4,1,2,16,48,128]{5,4,3,2,1,0:T(8,128)(2,1)S(1)} async-done(((bf16[4,1,2,16,48,128]{5,4,3,2,1,0:T(8,128)(2,1)}), bf16[4,1,2,16,48,128]{5,4,3,2,1,0:T(8,128)(2,1)S(1)}, u32[]{:S(2)}, u32[]{:S(2)}) %all-to-all-start.1) | async-done | bytes 1572896 | tf_op jit(solution)/shard_map/all_to_all | solution.py:320
  137.2 3.2 %triangle.2 = (bf16[32,16,256]{2,1,0:T(8,128)(2,1)S(1)}, bf16[32,16,256]{2,1,0:T(8,128)(2,1)S(1)}, bf16[32,16,256]{2,1,0:T(8,128)(2,1)S(1)}, bf16[32,16,256]{2,1,0:T(8,128)(2,1)S(1)}) custom-call(s32[3]{0:T(128)S(1)} %pad_add_fusion.1.info, bf16[4,2,2,16,32,128]{5,4,3,2,1,0:T(8,128)(2,1)} %all-to-all-done.refs_0_, ...), custom_call_target="tpu_custom_call" | custom-call | flops 335544320 | bytes 10000000 | tf_op jit(solution)/shard_map/triangle/pallas_call | solution.py:503
  141.2 4.4 %collective-permute-done.18.refs_2_ = bf16[1,1,2,16,48,128]{5,4,3,2,1,0:T(8,128)(2,1)S(1)} collective-permute-done((bf16[1,1,2,16,48,128]{5,4,3,2,1,0:T(8,128)(2,1)S(1)}, bf16[1,1,2,16,48,128]{5,4,3,2,1,0:T(8,128)(2,1)S(1)}, u32[]{:S(2)}, u32[]{:S(2)}) %collective-permute-start.18) | collective-permute-done | bytes 393248 | tf_op jit(solution)/shard_map/ppermute | solution.py:308
  145.6 9.2 %collective-permute-done.19.refs_3_ = bf16[1,1,2,16,48,128]{5,4,3,2,1,0:T(8,128)(2,1)S(1)} collective-permute-done((bf16[1,1,2,16,48,128]{5,4,3,2,1,0:T(8,128)(2,1)S(1)}, bf16[1,1,2,16,48,128]{5,4,3,2,1,0:T(8,128)(2,1)S(1)}, u32[]{:S(2)}, u32[]{:S(2)}) %collective-permute-start.19) | collective-permute-done | bytes 393248 | tf_op jit(solution)/shard_map/ppermute | solution.py:308
  155.1 2.0 collective-permute-start.22
  158.5 3.2 %triangle.3 = (bf16[32,16,256]{2,1,0:T(8,128)(2,1)S(1)}, bf16[32,16,256]{2,1,0:T(8,128)(2,1)S(1)}, bf16[32,16,256]{2,1,0:T(8,128)(2,1)S(1)}, bf16[32,16,256]{2,1,0:T(8,128)(2,1)S(1)}) custom-call(s32[3]{0:T(128)S(1)} %pad_add_fusion.1.info, bf16[4,2,2,16,32,128]{5,4,3,2,1,0:T(8,128)(2,1)} %all-to-all-done.refs_0_, ...), custom_call_target="tpu_custom_call" | custom-call | flops 335544320 | bytes 10000000 | tf_op jit(solution)/shard_map/triangle/pallas_call | solution.py:503
  161.8 1.9 collective-permute-start.25
  164.7 4.6 %collective-permute-done.22.refs_3_ = bf16[32,16,256]{2,1,0:T(8,128)(2,1)S(1)} collective-permute-done((bf16[32,16,256]{2,1,0:T(8,128)(2,1)S(1)}, bf16[32,16,256]{2,1,0:T(8,128)(2,1)S(1)}, u32[]{:S(2)}, u32[]{:S(2)}) %collective-permute-start.22) | collective-permute-done | bytes 262176 | tf_op jit(solution)/shard_map/ppermute | solution.py:305
  170.3 3.4 %all-to-all-start.2 = ((bf16[4,16,16,128]{3,2,1,0:T(8,128)(2,1)}), bf16[4,16,16,128]{3,2,1,0:T(8,128)(2,1)S(1)}, u32[]{:S(2)}, u32[]{:S(2)}) async-start(bf16[4,16,16,128]{3,2,1,0:T(8,128)(2,1)} %gather.2), calls=%async_computation.2 | async-start | bytes 524288 | tf_op jit(solution)/shard_map/all_to_all | solution.py:320
  173.8 1.8 collective-permute-done.24.refs_1_
  175.5 14.9 %collective-permute-done.25.refs_2_ = bf16[32,16,256]{2,1,0:T(8,128)(2,1)S(1)} collective-permute-done((bf16[32,16,256]{2,1,0:T(8,128)(2,1)S(1)}, bf16[32,16,256]{2,1,0:T(8,128)(2,1)S(1)}, u32[]{:S(2)}, u32[]{:S(2)}) %collective-permute-start.25) | collective-permute-done | bytes 262176 | tf_op jit(solution)/shard_map/ppermute | solution.py:305
  191.6 8.6 %all_to_all.20.second = bf16[4,16,16,128]{3,2,1,0:T(8,128)(2,1)S(1)} all-to-all(bf16[4,16,16,128]{3,2,1,0:T(8,128)(2,1)S(1)} %gather.3), channel_id=1, replica_groups=mesh['row'=8,'col'=4] {'col'}, dimensions={0} | all-to-all | bytes 524288 | tf_op jit(solution)/shard_map/all_to_all | solution.py:320
  200.3 1.9 finish.1
  (130 shorter events, 36.8 us)
Async XLA Ops:
  1.4 17.3 %collective-permute-start = (bf16[48,128]{1,0:T(8,128)(2,1)S(1)}, bf16[48,128]{1,0:T(8,128)(2,1)S(1)}, u32[]{:S(2)}, u32[]{:S(2)}) collective-permute-start(bf16[48,128]{1,0:T(8,128)(2,1)S(1)} %get-tuple-element.125), channel_id=1, source_target_pairs={{0,1},{1,2},{2,3},{3,4},{4,5},{5,6},{6,7},{7,8},{8,9},{9,10},{10,1... | collective-permute-start | bytes 36872 | tf_op jit(solution)/shard_map/ppermute | solution.py:300
  4.8 13.9 %collective-permute-start.1 = (bf16[48,128]{1,0:T(8,128)(2,1)S(1)}, bf16[48,128]{1,0:T(8,128)(2,1)S(1)}, u32[]{:S(2)}, u32[]{:S(2)}) collective-permute-start(bf16[48,128]{1,0:T(8,128)(2,1)S(1)} %get-tuple-element.124), channel_id=1, source_target_pairs={{1,0},{2,1},{3,2},{4,3},{5,4},{6,5},{7,6},{8,7},{9,8},{10,9},{11,1... | collective-permute-start | bytes 36872 | tf_op jit(solution)/shard_map/ppermute | solution.py:301
  11.0 19.9 %collective-permute-start.5 = (bf16[32,32,128]{2,1,0:T(8,128)(2,1)}, bf16[32,32,128]{2,1,0:T(8,128)(2,1)S(1)}, u32[]{:S(2)}, u32[]{:S(2)}) collective-permute-start(bf16[32,32,128]{2,1,0:T(8,128)(2,1)} %bitcast.43), channel_id=1, source_target_pairs={{0,8},{4,12},{8,16},{12,20},{16,24},{20,28},{24,0},{28,4},{1,9},{5... | collective-permute-start | bytes 786440 | tf_op jit(solution)/shard_map/ppermute | solution.py:305
  13.4 21.1 %collective-permute-start.6 = (bf16[32,32,128]{2,1,0:T(8,128)(2,1)}, bf16[32,32,128]{2,1,0:T(8,128)(2,1)S(1)}, u32[]{:S(2)}, u32[]{:S(2)}) collective-permute-start(bf16[32,32,128]{2,1,0:T(8,128)(2,1)} %bitcast.42), channel_id=1, source_target_pairs={{0,16},{4,20},{8,24},{12,28},{16,0},{20,4},{24,8},{28,12},{1,17},{... | collective-permute-start | bytes 786440 | tf_op jit(solution)/shard_map/ppermute | solution.py:305
  15.2 20.9 %collective-permute-start.7 = (bf16[32,32,128]{2,1,0:T(8,128)(2,1)}, bf16[32,32,128]{2,1,0:T(8,128)(2,1)S(1)}, u32[]{:S(2)}, u32[]{:S(2)}) collective-permute-start(bf16[32,32,128]{2,1,0:T(8,128)(2,1)} %bitcast.41), channel_id=1, source_target_pairs={{0,24},{4,28},{8,0},{12,4},{16,8},{20,12},{24,16},{28,20},{1,25},{... | collective-permute-start | bytes 786440 | tf_op jit(solution)/shard_map/ppermute | solution.py:305
  20.9 5.0 %collective-permute-start.4 = (bf16[160,128]{1,0:T(8,128)(2,1)S(1)}, bf16[160,128]{1,0:T(8,128)(2,1)S(1)}, u32[]{:S(2)}, u32[]{:S(2)}) collective-permute-start(bf16[160,128]{1,0:T(8,128)(2,1)S(1)} %atoms.1), channel_id=1, source_target_pairs={{0,3},{1,2},{2,1},{3,0},{4,7},{5,6},{6,5},{7,4},{8,11},{9,10},{10,... | collective-permute-start | bytes 122888 | tf_op jit(solution)/shard_map/ppermute | solution.py:308
  21.9 7.5 %collective-permute-start.3 = (bf16[160,128]{1,0:T(8,128)(2,1)S(1)}, bf16[160,128]{1,0:T(8,128)(2,1)S(1)}, u32[]{:S(2)}, u32[]{:S(2)}) collective-permute-start(bf16[160,128]{1,0:T(8,128)(2,1)S(1)} %atoms.1), channel_id=1, source_target_pairs={{0,2},{1,3},{2,0},{3,1},{4,6},{5,7},{6,4},{7,5},{8,10},{9,11},{10,... | collective-permute-start | bytes 122888 | tf_op jit(solution)/shard_map/ppermute | solution.py:308
  25.9 4.0 %collective-permute-start.2 = (bf16[160,128]{1,0:T(8,128)(2,1)S(1)}, bf16[160,128]{1,0:T(8,128)(2,1)S(1)}, u32[]{:S(2)}, u32[]{:S(2)}) collective-permute-start(bf16[160,128]{1,0:T(8,128)(2,1)S(1)} %atoms.1), channel_id=1, source_target_pairs={{0,1},{1,0},{2,3},{3,2},{4,5},{5,4},{6,7},{7,6},{8,9},{9,8},{10,11... | collective-permute-start | bytes 122888 | tf_op jit(solution)/shard_map/ppermute | solution.py:308
  36.2 7.1 %collective-permute-start.8 = (bf16[640,128]{1,0:T(8,128)(2,1)S(1)}, bf16[640,128]{1,0:T(8,128)(2,1)S(1)}, u32[]{:S(2)}, u32[]{:S(2)}) collective-permute-start(bf16[640,128]{1,0:T(8,128)(2,1)S(1)} %pad_maximum_fusion.2.refs_0_), channel_id=1, source_target_pairs={{0,8},{4,12},{8,16},{12,20},{16,24},{20,28},{24,0},{28,4},{1,9},{5... | collective-permute-start | bytes 491528 | tf_op jit(solution)/shard_map/ppermute | solution.py:305
  36.2 14.5 %collective-permute-start.9 = (bf16[640,128]{1,0:T(8,128)(2,1)S(1)}, bf16[640,128]{1,0:T(8,128)(2,1)S(1)}, u32[]{:S(2)}, u32[]{:S(2)}) collective-permute-start(bf16[640,128]{1,0:T(8,128)(2,1)S(1)} %pad_maximum_fusion.2.refs_0_), channel_id=1, source_target_pairs={{0,16},{4,20},{8,24},{12,28},{16,0},{20,4},{24,8},{28,12},{1,17},{... | collective-permute-start | bytes 491528 | tf_op jit(solution)/shard_map/ppermute | solution.py:305
  38.6 13.4 %collective-permute-start.10 = (bf16[640,128]{1,0:T(8,128)(2,1)S(1)}, bf16[640,128]{1,0:T(8,128)(2,1)S(1)}, u32[]{:S(2)}, u32[]{:S(2)}) collective-permute-start(bf16[640,128]{1,0:T(8,128)(2,1)S(1)} %pad_maximum_fusion.2.refs_0_), channel_id=1, source_target_pairs={{0,24},{4,28},{8,0},{12,4},{16,8},{20,12},{24,16},{28,20},{1,25},{... | collective-permute-start | bytes 491528 | tf_op jit(solution)/shard_map/ppermute | solution.py:305
  53.0 5.5 %collective-permute-start.11 = (bf16[2560,128]{1,0:T(8,128)(2,1)}, bf16[2560,128]{1,0:T(8,128)(2,1)S(1)}, u32[]{:S(2)}, u32[]{:S(2)}) collective-permute-start(bf16[2560,128]{1,0:T(8,128)(2,1)} %pad_maximum_fusion.1), channel_id=1, source_target_pairs={{0,4},{4,0},{8,12},{12,8},{16,20},{20,16},{24,28},{28,24},{1,5},{5... | collective-permute-start | bytes 1966088 | tf_op jit(solution)/shard_map/ppermute | solution.py:311
  53.2 30.1 %collective-permute-start.12 = (bf16[48,32,128]{2,1,0:T(8,128)(2,1)}, bf16[48,32,128]{2,1,0:T(8,128)(2,1)}, u32[]{:S(2)}, u32[]{:S(2)}) collective-permute-start(bf16[48,32,128]{2,1,0:T(8,128)(2,1)} %get-tuple-element.83), channel_id=1, source_target_pairs={{0,8},{4,12},{8,16},{12,20},{16,24},{20,28},{24,0},{28,4},{1,9},{5... | collective-permute-start | bytes 1179656 | tf_op jit(solution)/shard_map/ppermute | solution.py:305
  53.3 34.9 %collective-permute-start.13 = (bf16[48,32,128]{2,1,0:T(8,128)(2,1)}, bf16[48,32,128]{2,1,0:T(8,128)(2,1)}, u32[]{:S(2)}, u32[]{:S(2)}) collective-permute-start(bf16[48,32,128]{2,1,0:T(8,128)(2,1)} %get-tuple-element.84), channel_id=1, source_target_pairs={{0,16},{4,20},{8,24},{12,28},{16,0},{20,4},{24,8},{28,12},{1,17},{... | collective-permute-start | bytes 1179656 | tf_op jit(solution)/shard_map/ppermute | solution.py:305
  55.3 35.3 %collective-permute-start.14 = (bf16[48,32,128]{2,1,0:T(8,128)(2,1)}, bf16[48,32,128]{2,1,0:T(8,128)(2,1)}, u32[]{:S(2)}, u32[]{:S(2)}) collective-permute-start(bf16[48,32,128]{2,1,0:T(8,128)(2,1)} %get-tuple-element.85), channel_id=1, source_target_pairs={{0,24},{4,28},{8,0},{12,4},{16,8},{20,12},{24,16},{28,20},{1,25},{... | collective-permute-start | bytes 1179656 | tf_op jit(solution)/shard_map/ppermute | solution.py:305
  78.6 31.6 %all-to-all-start = ((bf16[4,2,2,16,32,128]{5,4,3,2,1,0:T(8,128)(2,1)}), bf16[4,2,2,16,32,128]{5,4,3,2,1,0:T(8,128)(2,1)}, u32[]{:S(2)}, u32[]{:S(2)}) async-start(bf16[4,2,2,16,32,128]{5,4,3,2,1,0:T(8,128)(2,1)} %pair.2), calls=%async_computation | async-start | bytes 4194304 | tf_op jit(solution)/shard_map/all_to_all | solution.py:320
  110.3 23.4 %all-to-all-start.1 = ((bf16[4,1,2,16,48,128]{5,4,3,2,1,0:T(8,128)(2,1)}), bf16[4,1,2,16,48,128]{5,4,3,2,1,0:T(8,128)(2,1)S(1)}, u32[]{:S(2)}, u32[]{:S(2)}) async-start(bf16[4,1,2,16,48,128]{5,4,3,2,1,0:T(8,128)(2,1)} %get-tuple-element.96), calls=%async_computation.1 | async-start | bytes 3145728 | tf_op jit(solution)/shard_map/all_to_all | solution.py:320
  114.0 23.2 %collective-permute-start.15 = (bf16[4,2,2,16,32,128]{5,4,3,2,1,0:T(8,128)(2,1)}, bf16[4,2,2,16,32,128]{5,4,3,2,1,0:T(8,128)(2,1)}, u32[]{:S(2)}, u32[]{:S(2)}) collective-permute-start(bf16[4,2,2,16,32,128]{5,4,3,2,1,0:T(8,128)(2,1)} %all-to-all-done.refs_0_), channel_id=1, source_target_pairs={{0,4},{4,0},{8,12},{12,8},{16,20},{20,16},{24,28},{28,24},{1,5},{5... | collective-permute-start | bytes 6291464 | tf_op jit(solution)/shard_map/ppermute | solution.py:311
  133.7 3.5 %collective-permute-start.16 = (bf16[4,1,2,16,48,128]{5,4,3,2,1,0:T(8,128)(2,1)S(1)}, bf16[4,1,2,16,48,128]{5,4,3,2,1,0:T(8,128)(2,1)S(1)}, u32[]{:S(2)}, u32[]{:S(2)}) collective-permute-start(bf16[4,1,2,16,48,128]{5,4,3,2,1,0:T(8,128)(2,1)S(1)} %all-to-all-done.1.refs_1_), channel_id=1, source_target_pairs={{0,4},{4,0},{8,12},{12,8},{16,20},{20,16},{24,28},{28,24},{1,5},{5... | collective-permute-start | bytes 4718600 | tf_op jit(solution)/shard_map/ppermute | solution.py:311
  133.7 11.9 %collective-permute-start.18 = (bf16[1,1,2,16,48,128]{5,4,3,2,1,0:T(8,128)(2,1)S(1)}, bf16[1,1,2,16,48,128]{5,4,3,2,1,0:T(8,128)(2,1)S(1)}, u32[]{:S(2)}, u32[]{:S(2)}) collective-permute-start(bf16[1,1,2,16,48,128]{5,4,3,2,1,0:T(8,128)(2,1)S(1)} %copy-done.19), channel_id=1, source_target_pairs={{0,1},{1,0},{2,3},{3,2},{4,5},{5,4},{6,7},{7,6},{8,9},{9,8},{10,11... | collective-permute-start | bytes 1179656 | tf_op jit(solution)/shard_map/ppermute | solution.py:308
  135.1 19.7 %collective-permute-start.19 = (bf16[1,1,2,16,48,128]{5,4,3,2,1,0:T(8,128)(2,1)S(1)}, bf16[1,1,2,16,48,128]{5,4,3,2,1,0:T(8,128)(2,1)S(1)}, u32[]{:S(2)}, u32[]{:S(2)}) collective-permute-start(bf16[1,1,2,16,48,128]{5,4,3,2,1,0:T(8,128)(2,1)S(1)} %copy-done.17), channel_id=1, source_target_pairs={{0,2},{1,3},{2,0},{3,1},{4,6},{5,7},{6,4},{7,5},{8,10},{9,11},{10,... | collective-permute-start | bytes 1179656 | tf_op jit(solution)/shard_map/ppermute | solution.py:308
  135.7 19.1 %collective-permute-start.20 = (bf16[1,1,2,16,48,128]{5,4,3,2,1,0:T(8,128)(2,1)S(1)}, bf16[1,1,2,16,48,128]{5,4,3,2,1,0:T(8,128)(2,1)S(1)}, u32[]{:S(2)}, u32[]{:S(2)}) collective-permute-start(bf16[1,1,2,16,48,128]{5,4,3,2,1,0:T(8,128)(2,1)S(1)} %get-tuple-element.102), channel_id=1, source_target_pairs={{0,3},{1,2},{2,1},{3,0},{4,7},{5,6},{6,5},{7,4},{8,11},{9,10},{10,... | collective-permute-start | bytes 1179656 | tf_op jit(solution)/shard_map/ppermute | solution.py:308
  140.4 14.4 %collective-permute-start.21 = (bf16[32,16,256]{2,1,0:T(8,128)(2,1)S(1)}, bf16[32,16,256]{2,1,0:T(8,128)(2,1)S(1)}, u32[]{:S(2)}, u32[]{:S(2)}) collective-permute-start(bf16[32,16,256]{2,1,0:T(8,128)(2,1)S(1)} %get-tuple-element.103), channel_id=1, source_target_pairs={{0,16},{4,20},{8,24},{12,28},{16,0},{20,4},{24,8},{28,12},{1,17},{... | collective-permute-start | bytes 786440 | tf_op jit(solution)/shard_map/ppermute | solution.py:305
  155.0 3.5 %collective-permute-start.23 = (bf16[4,1,2,16,48,128]{5,4,3,2,1,0:T(8,128)(2,1)S(1)}, bf16[4,1,2,16,48,128]{5,4,3,2,1,0:T(8,128)(2,1)S(1)}, u32[]{:S(2)}, u32[]{:S(2)}) collective-permute-start(bf16[4,1,2,16,48,128]{5,4,3,2,1,0:T(8,128)(2,1)S(1)} %pad_maximum_fusion), channel_id=1, source_target_pairs={{0,4},{4,0},{8,12},{12,8},{16,20},{20,16},{24,28},{28,24},{1,5},{5... | collective-permute-start | bytes 4718600 | tf_op jit(solution)/shard_map/ppermute | solution.py:311
  155.1 9.6 %collective-permute-start.17 = (bf16[32,16,256]{2,1,0:T(8,128)(2,1)S(1)}, bf16[32,16,256]{2,1,0:T(8,128)(2,1)S(1)}, u32[]{:S(2)}, u32[]{:S(2)}) collective-permute-start(bf16[32,16,256]{2,1,0:T(8,128)(2,1)S(1)} %get-tuple-element.98), channel_id=1, source_target_pairs={{0,8},{4,12},{8,16},{12,20},{16,24},{20,28},{24,0},{28,4},{1,9},{5... | collective-permute-start | bytes 786440 | tf_op jit(solution)/shard_map/ppermute | solution.py:305
  155.1 14.1 %collective-permute-start.22 = (bf16[32,16,256]{2,1,0:T(8,128)(2,1)S(1)}, bf16[32,16,256]{2,1,0:T(8,128)(2,1)S(1)}, u32[]{:S(2)}, u32[]{:S(2)}) collective-permute-start(bf16[32,16,256]{2,1,0:T(8,128)(2,1)S(1)} %get-tuple-element.105), channel_id=1, source_target_pairs={{0,24},{4,28},{8,0},{12,4},{16,8},{20,12},{24,16},{28,20},{1,25},{... | collective-permute-start | bytes 786440 | tf_op jit(solution)/shard_map/ppermute | solution.py:305
  161.7 13.8 %collective-permute-start.24 = (bf16[32,16,256]{2,1,0:T(8,128)(2,1)S(1)}, bf16[32,16,256]{2,1,0:T(8,128)(2,1)S(1)}, u32[]{:S(2)}, u32[]{:S(2)}) collective-permute-start(bf16[32,16,256]{2,1,0:T(8,128)(2,1)S(1)} %get-tuple-element.111), channel_id=1, source_target_pairs={{0,8},{4,12},{8,16},{12,20},{16,24},{20,28},{24,0},{28,4},{1,9},{5... | collective-permute-start | bytes 786440 | tf_op jit(solution)/shard_map/ppermute | solution.py:305
  161.8 28.6 %collective-permute-start.25 = (bf16[32,16,256]{2,1,0:T(8,128)(2,1)S(1)}, bf16[32,16,256]{2,1,0:T(8,128)(2,1)S(1)}, u32[]{:S(2)}, u32[]{:S(2)}) collective-permute-start(bf16[32,16,256]{2,1,0:T(8,128)(2,1)S(1)} %get-tuple-element.112), channel_id=1, source_target_pairs={{0,16},{4,20},{8,24},{12,28},{16,0},{20,4},{24,8},{28,12},{1,17},{... | collective-permute-start | bytes 786440 | tf_op jit(solution)/shard_map/ppermute | solution.py:305
  163.6 27.6 %collective-permute-start.26 = (bf16[32,16,256]{2,1,0:T(8,128)(2,1)S(1)}, bf16[32,16,256]{2,1,0:T(8,128)(2,1)S(1)}, u32[]{:S(2)}, u32[]{:S(2)}) collective-permute-start(bf16[32,16,256]{2,1,0:T(8,128)(2,1)S(1)} %get-tuple-element.113), channel_id=1, source_target_pairs={{0,24},{4,28},{8,0},{12,4},{16,8},{20,12},{24,16},{28,20},{1,25},{... | collective-permute-start | bytes 786440 | tf_op jit(solution)/shard_map/ppermute | solution.py:305
  169.3 30.9 %copy-start.26 = (f32[128]{0:T(128)S(1)}, f32[128]{0:T(128)}, u32[]{:S(2)}) copy-start(f32[128]{0:T(128)} %get-tuple-element.126) | copy-start | bytes 1540
  169.3 31.0 %copy-start.14 = (bf16[128,128]{1,0:T(8,128)(2,1)S(1)}, bf16[128,128]{1,0:T(8,128)(2,1)}, u32[]{:S(2)}) copy-start(bf16[128,128]{1,0:T(8,128)(2,1)} %w_out.1) | copy-start | bytes 98308
  170.3 21.2 %all-to-all-start.2 = ((bf16[4,16,16,128]{3,2,1,0:T(8,128)(2,1)}), bf16[4,16,16,128]{3,2,1,0:T(8,128)(2,1)S(1)}, u32[]{:S(2)}, u32[]{:S(2)}) async-start(bf16[4,16,16,128]{3,2,1,0:T(8,128)(2,1)} %gather.2), calls=%async_computation.2 | async-start | bytes 524288 | tf_op jit(solution)/shard_map/all_to_all | solution.py:320
  (26 other events, 247.2 us)

commit v3 on v2

--- a/solution.py
+++ b/solution.py
@@ -141,8 +141,8 @@
 
 def pair_kernel(groups, cols, halves, chunk_at, info, *refs):
     xs, refs = refs[:groups], refs[groups:]
-    row_terms, col_terms, gain_in, gain_out, w_in, w_out, w_tri, eye = refs[:8]
-    outs, (left_buf, right_buf, rows_buf) = refs[8:-3], refs[-3:]
+    row_terms, col_terms, gain_in, gain_out, w_in, w_out, w_tri = refs[:7]
+    outs, (left_buf, right_buf, rows_buf) = refs[7:-3], refs[-3:]
     k_first, valid, z, col = info[0], info[1], info[2], info[3]
     kb, per, channels = xs[0].shape
     lanes = per * groups
@@ -150,7 +150,8 @@
         zz = lax.rem(z - d + groups, groups)
         rows_buf[:, pl.ds(pl.multiple_of(zz * per, 32), per), :] = xs[d][...]
     at = k_first + chunk_at + pl.program_id(0) * kb
-    tile = max(1, 256 // lanes)
+    tile = max(1, 1024 // lanes)
+    repeat = tile * lanes // 128
     hidden = w_in.shape[0] // 2
 
     def opening(t):
@@ -160,15 +161,15 @@
             ).astype(BF)
             for u in range(tile)
         ]
-        paired = dot(eye[...], jnp.concatenate(added, axis=0), NT)
-        normed = normalize(paired, gain_in[...], 0).astype(BF)
+        paired = jnp.concatenate([value.astype(F32).T for value in added], axis=1)
+        normed = normalize(paired, jnp.concatenate([gain_in[...]] * repeat, axis=1), 0).astype(BF)
         return paired, dot(w_in[...], normed)
 
     def closing(t, paired, gate_up):
         gate = 0.5 * gate_up[:hidden]
         inner = ((gate + gate * jnp.tanh(gate)) * gate_up[hidden:]).astype(BF)
         following = (paired + dot(w_out[...], inner)).astype(BF).astype(F32)
-        normed = normalize(following, gain_out[...], 0).astype(BF)
+        normed = normalize(following, jnp.concatenate([gain_out[...]] * repeat, axis=1), 0).astype(BF)
         ops = dot(w_tri[...], normed)
         gate_l = jnp.tanh(0.5 * ops[:channels])
         gate_r = jnp.tanh(0.5 * ops[2 * channels : 3 * channels])
@@ -357,16 +358,15 @@
     plane, pair_parts[0] = lax.optimization_barrier((plane, pair_parts[0]))
     planes = [plane] + [shift_z(plane, d) for d in range(1, groups)]
     later = [shares(z_later, *chunk) for chunk in chunks[1:]]
-    tile_lanes = max(256, lanes)
     weights = [
-        jnp.broadcast_to(gains[0][:, None], (channels, tile_lanes)),
-        jnp.broadcast_to(gains[1][:, None], (channels, tile_lanes)),
+        jnp.broadcast_to(gains[0][:, None], (channels, 128)),
+        jnp.broadcast_to(gains[1][:, None], (channels, 128)),
         trans_in.T,
         trans_out.T,
         tri_in.T,
-        jnp.eye(channels, dtype=BF),
     ]
-    planes, later, weights = lax.optimization_barrier((planes, later, weights))
+    planes[1], later = lax.optimization_barrier((planes[1], later))
+    planes, weights = lax.optimization_barrier((planes, weights))
     other = swap_core(jnp.concatenate(planes, axis=0))
     pair_parts += [spread_z(pieces) for pieces in later]
 
@@ -439,12 +439,11 @@
             + [
                 whole(lanes, channels),
                 pl.BlockSpec((unit, channels), lambda g, first=first: (first + g, 0)),
-                whole(channels, tile_lanes),
-                whole(channels, tile_lanes),
+                whole(channels, 128),
+                whole(channels, 128),
                 whole(*trans_in.shape[::-1]),
                 whole(*trans_out.shape[::-1]),
                 whole(4 * channels, channels),
-                whole(channels, channels),
             ],
             out_specs=[
                 pl.BlockSpec((blocks, inner, 2, hc, unit, lanes), lambda g: (0, 0, 0, 0, g, 0))

time: 203 us -> 200 us (0.985)
  Pallas kernels: 46.4 us -> 40.2 us
  waiting for transfers between devices: 82.1 us -> 87.4 us
    pallas_call x2, Pallas kernels: 27.6 us -> 21.5 us  [body(): pl.pallas_call(functools.partial(pair_kernel, groups, cols, halves, first...]
    ppermute x15, waiting for transfers between devices: 46 us -> 50.1 us  [shift_z(): return lax.ppermute(value, 'row', pairs)]
    unnamed x63 -> x61, local copies, waits for them, and re-layouts: 8.88 us -> 8.95 us
  transfers between devices with their start and end apart: 30 -> 30, of which waited for: 18 -> 17; matrix products, arithmetic and copies ran while one was open for 5% -> 5% of each run, Pallas kernels for 22% -> 19%
where the time goes in v3:
time: 200 us
  waiting for transfers between devices  87.4 us (44%)
  starting transfers between devices  43.4 us (22%)
  Pallas kernels  40.2 us (20%)
  local copies, waits for them, and re-layouts  15.9 us (8%)
  blocking collectives  8.3 us (4%)
  other arithmetic  2.56 us (1%)
    ppermute x15, waiting for transfers between devices, shift_z(): return lax.ppermute(value, 'row', pairs)  50.1 us
    pallas_call x2, Pallas kernels, body(): pl.pallas_call(functools.partial(pair_kernel, groups, cols, halves, first...  21.5 us
    all_to_all x3, waiting for transfers between devices, spread_col(): return lax.all_to_all(value, 'col', split_axis=0, concat_axis=0, tiled=True)  19.6 us
    ppermute x15, starting transfers between devices, shift_z(): return lax.ppermute(value, 'row', pairs)  18.1 us
    ppermute x6, waiting for transfers between devices, cross_col(): return lax.ppermute(value, 'col', [(i, i ^ d) for i in range(cols)])  16.4 us
    all_to_all x3, starting transfers between devices, spread_col(): return lax.all_to_all(value, 'col', split_axis=0, concat_axis=0, tiled=True)  11.8 us
    unnamed x61, local copies, waits for them, and re-layouts  8.95 us
    all_to_all x1, blocking collectives, spread_col(): return lax.all_to_all(value, 'col', split_axis=0, concat_axis=0, tiled=True)  8.3 us
  transfers between devices with their start and end apart: 30, of which 17 were waited for; matrix products, arithmetic and copies ran while one was open for 5% of the time, Pallas kernels for 19%

profile of v3, /device:TPU:8, one launch (start us, length us, event | category | flops | bytes accessed | tf_op | source)
XLA Modules:
  0.0 199.6 jit_solution(9212243174276316726)
XLA Ops:
  1.4 3.4 %collective-permute-start = (bf16[48,128]{1,0:T(8,128)(2,1)S(1)}, bf16[48,128]{1,0:T(8,128)(2,1)S(1)}, u32[]{:S(2)}, u32[]{:S(2)}) collective-permute-start(bf16[48,128]{1,0:T(8,128)(2,1)S(1)} %get-tuple-element.125), channel_id=1, source_target_pairs={{0,1},{1,2},{2,3},{3,4},{4,5},{5,6},{6,7},{7,8},{8,9},{9,10},{10,1... | collective-permute-start | bytes 36872 | tf_op jit(solution)/shard_map/ppermute | solution.py:301
  4.8 4.0 %collective-permute-start.1 = (bf16[48,128]{1,0:T(8,128)(2,1)S(1)}, bf16[48,128]{1,0:T(8,128)(2,1)S(1)}, u32[]{:S(2)}, u32[]{:S(2)}) collective-permute-start(bf16[48,128]{1,0:T(8,128)(2,1)S(1)} %get-tuple-element.124), channel_id=1, source_target_pairs={{1,0},{2,1},{3,2},{4,3},{5,4},{6,5},{7,6},{8,7},{9,8},{10,9},{11,1... | collective-permute-start | bytes 36872 | tf_op jit(solution)/shard_map/ppermute | solution.py:302
  11.0 1.6 collective-permute-start.5
  15.3 2.0 %collective-permute-start.7 = (bf16[32,32,128]{2,1,0:T(8,128)(2,1)}, bf16[32,32,128]{2,1,0:T(8,128)(2,1)S(1)}, u32[]{:S(2)}, u32[]{:S(2)}) collective-permute-start(bf16[32,32,128]{2,1,0:T(8,128)(2,1)} %bitcast.41), channel_id=1, source_target_pairs={{0,24},{4,28},{8,0},{12,4},{16,8},{20,12},{24,16},{28,20},{1,25},{... | collective-permute-start | bytes 786440 | tf_op jit(solution)/shard_map/ppermute | solution.py:306
  18.7 2.2 %atoms.1 = bf16[160,128]{1,0:T(8,128)(2,1)S(1)} custom-call(s32[2]{0:T(128)S(1)} %pad_add_fusion.2.info, bf16[48,128]{1,0:T(8,128)(2,1)S(1)} %collective-permute-done.before, bf16[160,128]{1,0:T(8,128)(2,1)S(1)} %copy-done.5, bf16[48,128]{1,0:T(8,128)(2,1)S(1)} %collective-permute-done.1.after, f32[1,128]{1,0:T(1,128)S(1)} %bitcast.53, ...), custom_call_target="tpu_custom_call" | custom-call | flops 100000000 | bytes 1000000 | tf_op jit(solution)/shard_map/atoms/pallas_call | solution.py:334
  30.9 3.6 %collective-permute-done.6.refs_2_ = bf16[32,32,128]{2,1,0:T(8,128)(2,1)S(1)} collective-permute-done((bf16[32,32,128]{2,1,0:T(8,128)(2,1)}, bf16[32,32,128]{2,1,0:T(8,128)(2,1)S(1)}, u32[]{:S(2)}, u32[]{:S(2)}) %collective-permute-start.6) | collective-permute-done | bytes 262176 | tf_op jit(solution)/shard_map/ppermute | solution.py:306
  34.5 1.6 collective-permute-done.7.refs_3_
  36.9 1.6 collective-permute-start.9
  38.5 2.0 %collective-permute-start.10 = (bf16[640,128]{1,0:T(8,128)(2,1)S(1)}, bf16[640,128]{1,0:T(8,128)(2,1)S(1)}, u32[]{:S(2)}, u32[]{:S(2)}) collective-permute-start(bf16[640,128]{1,0:T(8,128)(2,1)S(1)} %pad_maximum_fusion.2.refs_0_), channel_id=1, source_target_pairs={{0,24},{4,28},{8,0},{12,4},{16,8},{20,12},{24,16},{28,20},{1,25},{... | collective-permute-start | bytes 491528 | tf_op jit(solution)/shard_map/ppermute | solution.py:306
  41.1 2.8 %collective-permute-done.8.refs_1_ = bf16[640,128]{1,0:T(8,128)(2,1)S(1)} collective-permute-done((bf16[640,128]{1,0:T(8,128)(2,1)S(1)}, bf16[640,128]{1,0:T(8,128)(2,1)S(1)}, u32[]{:S(2)}, u32[]{:S(2)}) %collective-permute-start.8) | collective-permute-done | bytes 163872 | tf_op jit(solution)/shard_map/ppermute | solution.py:306
  44.0 7.4 %collective-permute-done.9.refs_2_ = bf16[640,128]{1,0:T(8,128)(2,1)S(1)} collective-permute-done((bf16[640,128]{1,0:T(8,128)(2,1)S(1)}, bf16[640,128]{1,0:T(8,128)(2,1)S(1)}, u32[]{:S(2)}, u32[]{:S(2)}) %collective-permute-start.9) | collective-permute-done | bytes 163872 | tf_op jit(solution)/shard_map/ppermute | solution.py:306
  53.6 2.4 %collective-permute-start.13 = (bf16[48,32,128]{2,1,0:T(8,128)(2,1)}, bf16[48,32,128]{2,1,0:T(8,128)(2,1)}, u32[]{:S(2)}, u32[]{:S(2)}) collective-permute-start(bf16[48,32,128]{2,1,0:T(8,128)(2,1)} %get-tuple-element.84), channel_id=1, source_target_pairs={{0,16},{4,20},{8,24},{12,28},{16,0},{20,4},{24,8},{28,12},{1,17},{... | collective-permute-start | bytes 1179656 | tf_op jit(solution)/shard_map/ppermute | solution.py:306
  56.1 2.0 collective-permute-start.14
  60.2 6.8 %pool.1 = (bf16[320,384]{1,0:T(8,128)(2,1)}, f32[128,128]{1,0:T(8,128)S(1)}, f32[80,128]{1,0:T(8,128)S(1)}) custom-call(s32[3]{0:T(128)S(1)} %pad_add_fusion.1.info, s32[1281]{0:T(1024)S(1)} %pad_add_fusion.starts, bf16[640,128]{1,0:T(8,128)(2,1)S(1)} %pad_maximum_fusion.2.refs_0_, bf16[640,128]{1,0:T(8,128)(2,1)S(1)} %collective-permute-done.8.refs_1_, ...), custom_call_target="tpu_custom_call" | custom-call | flops 1000 | bytes 1000 | tf_op jit(solution)/shard_map/pool/pallas_call | solution.py:380
  67.0 8.7 %pair.2 = bf16[4,2,2,16,32,128]{5,4,3,2,1,0:T(8,128)(2,1)} custom-call(s32[4]{0:T(128)S(1)} %pad_add_fusion.3.info, bf16[32,32,128]{2,1,0:T(8,128)(2,1)S(1)} %bitcast.46, bf16[32,32,128]{2,1,0:T(8,128)(2,1)S(1)} %collective-permute-done.5.refs_1_, bf16[32,32,128]{2,1,0:T(8,128)(2,1)S(1)} %collective-permute-done.6.refs_2_, ...), custom_call_target="tpu_custom_call" | custom-call | flops 1000 | bytes 1000 | tf_op jit(solution)/shard_map/pair/pallas_call | solution.py:430
  76.9 4.6 %all-to-all-start = ((bf16[4,2,2,16,32,128]{5,4,3,2,1,0:T(8,128)(2,1)}), bf16[4,2,2,16,32,128]{5,4,3,2,1,0:T(8,128)(2,1)}, u32[]{:S(2)}, u32[]{:S(2)}) async-start(bf16[4,2,2,16,32,128]{5,4,3,2,1,0:T(8,128)(2,1)} %pair.2), calls=%async_computation | async-start | bytes 4194304 | tf_op jit(solution)/shard_map/all_to_all | solution.py:321
  81.6 6.9 %collective-permute-done.13.refs_2_ = bf16[48,32,128]{2,1,0:T(8,128)(2,1)} collective-permute-done((bf16[48,32,128]{2,1,0:T(8,128)(2,1)}, bf16[48,32,128]{2,1,0:T(8,128)(2,1)}, u32[]{:S(2)}, u32[]{:S(2)}) %collective-permute-start.13) | collective-permute-done | bytes 393248 | tf_op jit(solution)/shard_map/ppermute | solution.py:306
  88.5 2.9 %collective-permute-done.14.refs_3_ = bf16[48,32,128]{2,1,0:T(8,128)(2,1)} collective-permute-done((bf16[48,32,128]{2,1,0:T(8,128)(2,1)}, bf16[48,32,128]{2,1,0:T(8,128)(2,1)}, u32[]{:S(2)}, u32[]{:S(2)}) %collective-permute-start.14) | collective-permute-done | bytes 393248 | tf_op jit(solution)/shard_map/ppermute | solution.py:306
  93.0 12.7 %pair.3 = (bf16[4,1,2,16,48,128]{5,4,3,2,1,0:T(8,128)(2,1)}, bf16[1,1,2,16,48,128]{5,4,3,2,1,0:T(8,128)(2,1)S(1)}, bf16[1,1,2,16,48,128]{5,4,3,2,1,0:T(8,128)(2,...) custom-call(s32[4]{0:T(128)S(1)} %pad_add_fusion.3.info, ...), custom_call_target="tpu_custom_call" | custom-call | flops 30000001024 | bytes 1000000 | tf_op jit(solution)/shard_map/pair/pallas_call | solution.py:430
  107.3 3.7 %all-to-all-start.1 = ((bf16[4,1,2,16,48,128]{5,4,3,2,1,0:T(8,128)(2,1)}), bf16[4,1,2,16,48,128]{5,4,3,2,1,0:T(8,128)(2,1)S(1)}, u32[]{:S(2)}, u32[]{:S(2)}) async-start(bf16[4,1,2,16,48,128]{5,4,3,2,1,0:T(8,128)(2,1)} %get-tuple-element.96), calls=%async_computation.1 | async-start | bytes 3145728 | tf_op jit(solution)/shard_map/all_to_all | solution.py:321
  111.1 19.6 %all-to-all-done.1.refs_1_ = bf16[4,1,2,16,48,128]{5,4,3,2,1,0:T(8,128)(2,1)S(1)} async-done(((bf16[4,1,2,16,48,128]{5,4,3,2,1,0:T(8,128)(2,1)}), bf16[4,1,2,16,48,128]{5,4,3,2,1,0:T(8,128)(2,1)S(1)}, u32[]{:S(2)}, u32[]{:S(2)}) %all-to-all-start.1) | async-done | bytes 1572896 | tf_op jit(solution)/shard_map/all_to_all | solution.py:321
  134.2 3.2 %triangle.2 = (bf16[32,16,256]{2,1,0:T(8,128)(2,1)S(1)}, bf16[32,16,256]{2,1,0:T(8,128)(2,1)S(1)}, bf16[32,16,256]{2,1,0:T(8,128)(2,1)S(1)}, bf16[32,16,256]{2,1,0:T(8,128)(2,1)S(1)}) custom-call(s32[3]{0:T(128)S(1)} %pad_add_fusion.1.info, bf16[4,2,2,16,32,128]{5,4,3,2,1,0:T(8,128)(2,1)} %all-to-all-done.refs_0_, ...), custom_call_target="tpu_custom_call" | custom-call | flops 335544320 | bytes 10000000 | tf_op jit(solution)/shard_map/triangle/pallas_call | solution.py:502
  137.9 4.7 %collective-permute-done.18.refs_2_ = bf16[1,1,2,16,48,128]{5,4,3,2,1,0:T(8,128)(2,1)S(1)} collective-permute-done((bf16[1,1,2,16,48,128]{5,4,3,2,1,0:T(8,128)(2,1)S(1)}, bf16[1,1,2,16,48,128]{5,4,3,2,1,0:T(8,128)(2,1)S(1)}, u32[]{:S(2)}, u32[]{:S(2)}) %collective-permute-start.18) | collective-permute-done | bytes 393248 | tf_op jit(solution)/shard_map/ppermute | solution.py:309
  142.6 9.2 %collective-permute-done.19.refs_3_ = bf16[1,1,2,16,48,128]{5,4,3,2,1,0:T(8,128)(2,1)S(1)} collective-permute-done((bf16[1,1,2,16,48,128]{5,4,3,2,1,0:T(8,128)(2,1)S(1)}, bf16[1,1,2,16,48,128]{5,4,3,2,1,0:T(8,128)(2,1)S(1)}, u32[]{:S(2)}, u32[]{:S(2)}) %collective-permute-start.19) | collective-permute-done | bytes 393248 | tf_op jit(solution)/shard_map/ppermute | solution.py:309
  152.1 2.0 %collective-permute-start.22 = (bf16[32,16,256]{2,1,0:T(8,128)(2,1)S(1)}, bf16[32,16,256]{2,1,0:T(8,128)(2,1)S(1)}, u32[]{:S(2)}, u32[]{:S(2)}) collective-permute-start(bf16[32,16,256]{2,1,0:T(8,128)(2,1)S(1)} %get-tuple-element.105), channel_id=1, source_target_pairs={{0,24},{4,28},{8,0},{12,4},{16,8},{20,12},{24,16},{28,20},{1,25},{... | collective-permute-start | bytes 786440 | tf_op jit(solution)/shard_map/ppermute | solution.py:306
  155.5 3.2 %triangle.3 = (bf16[32,16,256]{2,1,0:T(8,128)(2,1)S(1)}, bf16[32,16,256]{2,1,0:T(8,128)(2,1)S(1)}, bf16[32,16,256]{2,1,0:T(8,128)(2,1)S(1)}, bf16[32,16,256]{2,1,0:T(8,128)(2,1)S(1)}) custom-call(s32[3]{0:T(128)S(1)} %pad_add_fusion.1.info, bf16[4,2,2,16,32,128]{5,4,3,2,1,0:T(8,128)(2,1)} %all-to-all-done.refs_0_, ...), custom_call_target="tpu_custom_call" | custom-call | flops 335544320 | bytes 10000000 | tf_op jit(solution)/shard_map/triangle/pallas_call | solution.py:502
  158.8 2.8 %collective-permute-start.25 = (bf16[32,16,256]{2,1,0:T(8,128)(2,1)S(1)}, bf16[32,16,256]{2,1,0:T(8,128)(2,1)S(1)}, u32[]{:S(2)}, u32[]{:S(2)}) collective-permute-start(bf16[32,16,256]{2,1,0:T(8,128)(2,1)S(1)} %get-tuple-element.112), channel_id=1, source_target_pairs={{0,16},{4,20},{8,24},{12,28},{16,0},{20,4},{24,8},{28,12},{1,17},{... | collective-permute-start | bytes 786440 | tf_op jit(solution)/shard_map/ppermute | solution.py:306
  161.6 9.8 %collective-permute-done.22.refs_3_ = bf16[32,16,256]{2,1,0:T(8,128)(2,1)S(1)} collective-permute-done((bf16[32,16,256]{2,1,0:T(8,128)(2,1)S(1)}, bf16[32,16,256]{2,1,0:T(8,128)(2,1)S(1)}, u32[]{:S(2)}, u32[]{:S(2)}) %collective-permute-start.22) | collective-permute-done | bytes 262176 | tf_op jit(solution)/shard_map/ppermute | solution.py:306
  172.5 3.4 %all-to-all-start.2 = ((bf16[4,16,16,128]{3,2,1,0:T(8,128)(2,1)}), bf16[4,16,16,128]{3,2,1,0:T(8,128)(2,1)S(1)}, u32[]{:S(2)}, u32[]{:S(2)}) async-start(bf16[4,16,16,128]{3,2,1,0:T(8,128)(2,1)} %gather.2), calls=%async_computation.2 | async-start | bytes 524288 | tf_op jit(solution)/shard_map/all_to_all | solution.py:321
  175.9 11.4 %collective-permute-done.25.refs_2_ = bf16[32,16,256]{2,1,0:T(8,128)(2,1)S(1)} collective-permute-done((bf16[32,16,256]{2,1,0:T(8,128)(2,1)S(1)}, bf16[32,16,256]{2,1,0:T(8,128)(2,1)S(1)}, u32[]{:S(2)}, u32[]{:S(2)}) %collective-permute-start.25) | collective-permute-done | bytes 262176 | tf_op jit(solution)/shard_map/ppermute | solution.py:306
  189.3 8.3 %all_to_all.20.second = bf16[4,16,16,128]{3,2,1,0:T(8,128)(2,1)S(1)} all-to-all(bf16[4,16,16,128]{3,2,1,0:T(8,128)(2,1)S(1)} %gather.3), channel_id=1, replica_groups=mesh['row'=8,'col'=4] {'col'}, dimensions={0} | all-to-all | bytes 524288 | tf_op jit(solution)/shard_map/all_to_all | solution.py:321
  197.7 1.9 finish.1
  (127 shorter events, 35.0 us)
Async XLA Ops:
  1.4 17.3 %collective-permute-start = (bf16[48,128]{1,0:T(8,128)(2,1)S(1)}, bf16[48,128]{1,0:T(8,128)(2,1)S(1)}, u32[]{:S(2)}, u32[]{:S(2)}) collective-permute-start(bf16[48,128]{1,0:T(8,128)(2,1)S(1)} %get-tuple-element.125), channel_id=1, source_target_pairs={{0,1},{1,2},{2,3},{3,4},{4,5},{5,6},{6,7},{7,8},{8,9},{9,10},{10,1... | collective-permute-start | bytes 36872 | tf_op jit(solution)/shard_map/ppermute | solution.py:301
  4.8 13.9 %collective-permute-start.1 = (bf16[48,128]{1,0:T(8,128)(2,1)S(1)}, bf16[48,128]{1,0:T(8,128)(2,1)S(1)}, u32[]{:S(2)}, u32[]{:S(2)}) collective-permute-start(bf16[48,128]{1,0:T(8,128)(2,1)S(1)} %get-tuple-element.124), channel_id=1, source_target_pairs={{1,0},{2,1},{3,2},{4,3},{5,4},{6,5},{7,6},{8,7},{9,8},{10,9},{11,1... | collective-permute-start | bytes 36872 | tf_op jit(solution)/shard_map/ppermute | solution.py:302
  11.0 19.9 %collective-permute-start.5 = (bf16[32,32,128]{2,1,0:T(8,128)(2,1)}, bf16[32,32,128]{2,1,0:T(8,128)(2,1)S(1)}, u32[]{:S(2)}, u32[]{:S(2)}) collective-permute-start(bf16[32,32,128]{2,1,0:T(8,128)(2,1)} %bitcast.43), channel_id=1, source_target_pairs={{0,8},{4,12},{8,16},{12,20},{16,24},{20,28},{24,0},{28,4},{1,9},{5... | collective-permute-start | bytes 786440 | tf_op jit(solution)/shard_map/ppermute | solution.py:306
  13.4 21.1 %collective-permute-start.6 = (bf16[32,32,128]{2,1,0:T(8,128)(2,1)}, bf16[32,32,128]{2,1,0:T(8,128)(2,1)S(1)}, u32[]{:S(2)}, u32[]{:S(2)}) collective-permute-start(bf16[32,32,128]{2,1,0:T(8,128)(2,1)} %bitcast.42), channel_id=1, source_target_pairs={{0,16},{4,20},{8,24},{12,28},{16,0},{20,4},{24,8},{28,12},{1,17},{... | collective-permute-start | bytes 786440 | tf_op jit(solution)/shard_map/ppermute | solution.py:306
  15.3 20.9 %collective-permute-start.7 = (bf16[32,32,128]{2,1,0:T(8,128)(2,1)}, bf16[32,32,128]{2,1,0:T(8,128)(2,1)S(1)}, u32[]{:S(2)}, u32[]{:S(2)}) collective-permute-start(bf16[32,32,128]{2,1,0:T(8,128)(2,1)} %bitcast.41), channel_id=1, source_target_pairs={{0,24},{4,28},{8,0},{12,4},{16,8},{20,12},{24,16},{28,20},{1,25},{... | collective-permute-start | bytes 786440 | tf_op jit(solution)/shard_map/ppermute | solution.py:306
  20.9 5.0 %collective-permute-start.4 = (bf16[160,128]{1,0:T(8,128)(2,1)S(1)}, bf16[160,128]{1,0:T(8,128)(2,1)S(1)}, u32[]{:S(2)}, u32[]{:S(2)}) collective-permute-start(bf16[160,128]{1,0:T(8,128)(2,1)S(1)} %atoms.1), channel_id=1, source_target_pairs={{0,3},{1,2},{2,1},{3,0},{4,7},{5,6},{6,5},{7,4},{8,11},{9,10},{10,... | collective-permute-start | bytes 122888 | tf_op jit(solution)/shard_map/ppermute | solution.py:309
  21.9 6.6 %collective-permute-start.3 = (bf16[160,128]{1,0:T(8,128)(2,1)S(1)}, bf16[160,128]{1,0:T(8,128)(2,1)S(1)}, u32[]{:S(2)}, u32[]{:S(2)}) collective-permute-start(bf16[160,128]{1,0:T(8,128)(2,1)S(1)} %atoms.1), channel_id=1, source_target_pairs={{0,2},{1,3},{2,0},{3,1},{4,6},{5,7},{6,4},{7,5},{8,10},{9,11},{10,... | collective-permute-start | bytes 122888 | tf_op jit(solution)/shard_map/ppermute | solution.py:309
  25.9 4.0 %collective-permute-start.2 = (bf16[160,128]{1,0:T(8,128)(2,1)S(1)}, bf16[160,128]{1,0:T(8,128)(2,1)S(1)}, u32[]{:S(2)}, u32[]{:S(2)}) collective-permute-start(bf16[160,128]{1,0:T(8,128)(2,1)S(1)} %atoms.1), channel_id=1, source_target_pairs={{0,1},{1,0},{2,3},{3,2},{4,5},{5,4},{6,7},{7,6},{8,9},{9,8},{10,11... | collective-permute-start | bytes 122888 | tf_op jit(solution)/shard_map/ppermute | solution.py:309
  28.1 31.2 %copy-start.6 = (bf16[128,384]{1,0:T(8,128)(2,1)S(1)}, bf16[128,384]{1,0:T(8,128)(2,1)}, u32[]{:S(2)}) copy-start(bf16[128,384]{1,0:T(8,128)(2,1)} %refs_7_.1) | copy-start | bytes 294916
  36.9 7.1 %collective-permute-start.8 = (bf16[640,128]{1,0:T(8,128)(2,1)S(1)}, bf16[640,128]{1,0:T(8,128)(2,1)S(1)}, u32[]{:S(2)}, u32[]{:S(2)}) collective-permute-start(bf16[640,128]{1,0:T(8,128)(2,1)S(1)} %pad_maximum_fusion.2.refs_0_), channel_id=1, source_target_pairs={{0,8},{4,12},{8,16},{12,20},{16,24},{20,28},{24,0},{28,4},{1,9},{5... | collective-permute-start | bytes 491528 | tf_op jit(solution)/shard_map/ppermute | solution.py:306
  36.9 14.5 %collective-permute-start.9 = (bf16[640,128]{1,0:T(8,128)(2,1)S(1)}, bf16[640,128]{1,0:T(8,128)(2,1)S(1)}, u32[]{:S(2)}, u32[]{:S(2)}) collective-permute-start(bf16[640,128]{1,0:T(8,128)(2,1)S(1)} %pad_maximum_fusion.2.refs_0_), channel_id=1, source_target_pairs={{0,16},{4,20},{8,24},{12,28},{16,0},{20,4},{24,8},{28,12},{1,17},{... | collective-permute-start | bytes 491528 | tf_op jit(solution)/shard_map/ppermute | solution.py:306
  38.5 13.8 %collective-permute-start.10 = (bf16[640,128]{1,0:T(8,128)(2,1)S(1)}, bf16[640,128]{1,0:T(8,128)(2,1)S(1)}, u32[]{:S(2)}, u32[]{:S(2)}) collective-permute-start(bf16[640,128]{1,0:T(8,128)(2,1)S(1)} %pad_maximum_fusion.2.refs_0_), channel_id=1, source_target_pairs={{0,24},{4,28},{8,0},{12,4},{16,8},{20,12},{24,16},{28,20},{1,25},{... | collective-permute-start | bytes 491528 | tf_op jit(solution)/shard_map/ppermute | solution.py:306
  53.4 5.8 %collective-permute-start.11 = (bf16[2560,128]{1,0:T(8,128)(2,1)}, bf16[2560,128]{1,0:T(8,128)(2,1)S(1)}, u32[]{:S(2)}, u32[]{:S(2)}) collective-permute-start(bf16[2560,128]{1,0:T(8,128)(2,1)} %pad_maximum_fusion.1), channel_id=1, source_target_pairs={{0,4},{4,0},{8,12},{12,8},{16,20},{20,16},{24,28},{28,24},{1,5},{5... | collective-permute-start | bytes 1966088 | tf_op jit(solution)/shard_map/ppermute | solution.py:312
  53.6 28.0 %collective-permute-start.12 = (bf16[48,32,128]{2,1,0:T(8,128)(2,1)}, bf16[48,32,128]{2,1,0:T(8,128)(2,1)}, u32[]{:S(2)}, u32[]{:S(2)}) collective-permute-start(bf16[48,32,128]{2,1,0:T(8,128)(2,1)} %get-tuple-element.83), channel_id=1, source_target_pairs={{0,8},{4,12},{8,16},{12,20},{16,24},{20,28},{24,0},{28,4},{1,9},{5... | collective-permute-start | bytes 1179656 | tf_op jit(solution)/shard_map/ppermute | solution.py:306
  53.6 34.9 %collective-permute-start.13 = (bf16[48,32,128]{2,1,0:T(8,128)(2,1)}, bf16[48,32,128]{2,1,0:T(8,128)(2,1)}, u32[]{:S(2)}, u32[]{:S(2)}) collective-permute-start(bf16[48,32,128]{2,1,0:T(8,128)(2,1)} %get-tuple-element.84), channel_id=1, source_target_pairs={{0,16},{4,20},{8,24},{12,28},{16,0},{20,4},{24,8},{28,12},{1,17},{... | collective-permute-start | bytes 1179656 | tf_op jit(solution)/shard_map/ppermute | solution.py:306
  56.1 35.3 %collective-permute-start.14 = (bf16[48,32,128]{2,1,0:T(8,128)(2,1)}, bf16[48,32,128]{2,1,0:T(8,128)(2,1)}, u32[]{:S(2)}, u32[]{:S(2)}) collective-permute-start(bf16[48,32,128]{2,1,0:T(8,128)(2,1)} %get-tuple-element.85), channel_id=1, source_target_pairs={{0,24},{4,28},{8,0},{12,4},{16,8},{20,12},{24,16},{28,20},{1,25},{... | collective-permute-start | bytes 1179656 | tf_op jit(solution)/shard_map/ppermute | solution.py:306
  76.9 30.3 %all-to-all-start = ((bf16[4,2,2,16,32,128]{5,4,3,2,1,0:T(8,128)(2,1)}), bf16[4,2,2,16,32,128]{5,4,3,2,1,0:T(8,128)(2,1)}, u32[]{:S(2)}, u32[]{:S(2)}) async-start(bf16[4,2,2,16,32,128]{5,4,3,2,1,0:T(8,128)(2,1)} %pair.2), calls=%async_computation | async-start | bytes 4194304 | tf_op jit(solution)/shard_map/all_to_all | solution.py:321
  107.3 23.4 %all-to-all-start.1 = ((bf16[4,1,2,16,48,128]{5,4,3,2,1,0:T(8,128)(2,1)}), bf16[4,1,2,16,48,128]{5,4,3,2,1,0:T(8,128)(2,1)S(1)}, u32[]{:S(2)}, u32[]{:S(2)}) async-start(bf16[4,1,2,16,48,128]{5,4,3,2,1,0:T(8,128)(2,1)} %get-tuple-element.96), calls=%async_computation.1 | async-start | bytes 3145728 | tf_op jit(solution)/shard_map/all_to_all | solution.py:321
  111.0 23.2 %collective-permute-start.15 = (bf16[4,2,2,16,32,128]{5,4,3,2,1,0:T(8,128)(2,1)}, bf16[4,2,2,16,32,128]{5,4,3,2,1,0:T(8,128)(2,1)}, u32[]{:S(2)}, u32[]{:S(2)}) collective-permute-start(bf16[4,2,2,16,32,128]{5,4,3,2,1,0:T(8,128)(2,1)} %all-to-all-done.refs_0_), channel_id=1, source_target_pairs={{0,4},{4,0},{8,12},{12,8},{16,20},{20,16},{24,28},{28,24},{1,5},{5... | collective-permute-start | bytes 6291464 | tf_op jit(solution)/shard_map/ppermute | solution.py:312
  130.7 3.5 %collective-permute-start.16 = (bf16[4,1,2,16,48,128]{5,4,3,2,1,0:T(8,128)(2,1)S(1)}, bf16[4,1,2,16,48,128]{5,4,3,2,1,0:T(8,128)(2,1)S(1)}, u32[]{:S(2)}, u32[]{:S(2)}) collective-permute-start(bf16[4,1,2,16,48,128]{5,4,3,2,1,0:T(8,128)(2,1)S(1)} %all-to-all-done.1.refs_1_), channel_id=1, source_target_pairs={{0,4},{4,0},{8,12},{12,8},{16,20},{20,16},{24,28},{28,24},{1,5},{5... | collective-permute-start | bytes 4718600 | tf_op jit(solution)/shard_map/ppermute | solution.py:312
  130.7 11.9 %collective-permute-start.18 = (bf16[1,1,2,16,48,128]{5,4,3,2,1,0:T(8,128)(2,1)S(1)}, bf16[1,1,2,16,48,128]{5,4,3,2,1,0:T(8,128)(2,1)S(1)}, u32[]{:S(2)}, u32[]{:S(2)}) collective-permute-start(bf16[1,1,2,16,48,128]{5,4,3,2,1,0:T(8,128)(2,1)S(1)} %copy-done.17), channel_id=1, source_target_pairs={{0,1},{1,0},{2,3},{3,2},{4,5},{5,4},{6,7},{7,6},{8,9},{9,8},{10,11... | collective-permute-start | bytes 1179656 | tf_op jit(solution)/shard_map/ppermute | solution.py:309
  132.1 19.7 %collective-permute-start.19 = (bf16[1,1,2,16,48,128]{5,4,3,2,1,0:T(8,128)(2,1)S(1)}, bf16[1,1,2,16,48,128]{5,4,3,2,1,0:T(8,128)(2,1)S(1)}, u32[]{:S(2)}, u32[]{:S(2)}) collective-permute-start(bf16[1,1,2,16,48,128]{5,4,3,2,1,0:T(8,128)(2,1)S(1)} %copy-done.15), channel_id=1, source_target_pairs={{0,2},{1,3},{2,0},{3,1},{4,6},{5,7},{6,4},{7,5},{8,10},{9,11},{10,... | collective-permute-start | bytes 1179656 | tf_op jit(solution)/shard_map/ppermute | solution.py:309
  132.7 19.1 %collective-permute-start.20 = (bf16[1,1,2,16,48,128]{5,4,3,2,1,0:T(8,128)(2,1)S(1)}, bf16[1,1,2,16,48,128]{5,4,3,2,1,0:T(8,128)(2,1)S(1)}, u32[]{:S(2)}, u32[]{:S(2)}) collective-permute-start(bf16[1,1,2,16,48,128]{5,4,3,2,1,0:T(8,128)(2,1)S(1)} %get-tuple-element.102), channel_id=1, source_target_pairs={{0,3},{1,2},{2,1},{3,0},{4,7},{5,6},{6,5},{7,4},{8,11},{9,10},{10,... | collective-permute-start | bytes 1179656 | tf_op jit(solution)/shard_map/ppermute | solution.py:309
  137.4 14.4 %collective-permute-start.21 = (bf16[32,16,256]{2,1,0:T(8,128)(2,1)S(1)}, bf16[32,16,256]{2,1,0:T(8,128)(2,1)S(1)}, u32[]{:S(2)}, u32[]{:S(2)}) collective-permute-start(bf16[32,16,256]{2,1,0:T(8,128)(2,1)S(1)} %get-tuple-element.103), channel_id=1, source_target_pairs={{0,16},{4,20},{8,24},{12,28},{16,0},{20,4},{24,8},{28,12},{1,17},{... | collective-permute-start | bytes 786440 | tf_op jit(solution)/shard_map/ppermute | solution.py:306
  152.0 3.5 %collective-permute-start.23 = (bf16[4,1,2,16,48,128]{5,4,3,2,1,0:T(8,128)(2,1)S(1)}, bf16[4,1,2,16,48,128]{5,4,3,2,1,0:T(8,128)(2,1)S(1)}, u32[]{:S(2)}, u32[]{:S(2)}) collective-permute-start(bf16[4,1,2,16,48,128]{5,4,3,2,1,0:T(8,128)(2,1)S(1)} %pad_maximum_fusion), channel_id=1, source_target_pairs={{0,4},{4,0},{8,12},{12,8},{16,20},{20,16},{24,28},{28,24},{1,5},{5... | collective-permute-start | bytes 4718600 | tf_op jit(solution)/shard_map/ppermute | solution.py:312
  152.1 9.5 %collective-permute-start.17 = (bf16[32,16,256]{2,1,0:T(8,128)(2,1)S(1)}, bf16[32,16,256]{2,1,0:T(8,128)(2,1)S(1)}, u32[]{:S(2)}, u32[]{:S(2)}) collective-permute-start(bf16[32,16,256]{2,1,0:T(8,128)(2,1)S(1)} %get-tuple-element.98), channel_id=1, source_target_pairs={{0,8},{4,12},{8,16},{12,20},{16,24},{20,28},{24,0},{28,4},{1,9},{5... | collective-permute-start | bytes 786440 | tf_op jit(solution)/shard_map/ppermute | solution.py:306
  152.1 19.3 %collective-permute-start.22 = (bf16[32,16,256]{2,1,0:T(8,128)(2,1)S(1)}, bf16[32,16,256]{2,1,0:T(8,128)(2,1)S(1)}, u32[]{:S(2)}, u32[]{:S(2)}) collective-permute-start(bf16[32,16,256]{2,1,0:T(8,128)(2,1)S(1)} %get-tuple-element.105), channel_id=1, source_target_pairs={{0,24},{4,28},{8,0},{12,4},{16,8},{20,12},{24,16},{28,20},{1,25},{... | collective-permute-start | bytes 786440 | tf_op jit(solution)/shard_map/ppermute | solution.py:306
  158.7 17.2 %collective-permute-start.24 = (bf16[32,16,256]{2,1,0:T(8,128)(2,1)S(1)}, bf16[32,16,256]{2,1,0:T(8,128)(2,1)S(1)}, u32[]{:S(2)}, u32[]{:S(2)}) collective-permute-start(bf16[32,16,256]{2,1,0:T(8,128)(2,1)S(1)} %get-tuple-element.111), channel_id=1, source_target_pairs={{0,8},{4,12},{8,16},{12,20},{16,24},{20,28},{24,0},{28,4},{1,9},{5... | collective-permute-start | bytes 786440 | tf_op jit(solution)/shard_map/ppermute | solution.py:306
  158.8 28.6 %collective-permute-start.25 = (bf16[32,16,256]{2,1,0:T(8,128)(2,1)S(1)}, bf16[32,16,256]{2,1,0:T(8,128)(2,1)S(1)}, u32[]{:S(2)}, u32[]{:S(2)}) collective-permute-start(bf16[32,16,256]{2,1,0:T(8,128)(2,1)S(1)} %get-tuple-element.112), channel_id=1, source_target_pairs={{0,16},{4,20},{8,24},{12,28},{16,0},{20,4},{24,8},{28,12},{1,17},{... | collective-permute-start | bytes 786440 | tf_op jit(solution)/shard_map/ppermute | solution.py:306
  161.6 27.3 %collective-permute-start.26 = (bf16[32,16,256]{2,1,0:T(8,128)(2,1)S(1)}, bf16[32,16,256]{2,1,0:T(8,128)(2,1)S(1)}, u32[]{:S(2)}, u32[]{:S(2)}) collective-permute-start(bf16[32,16,256]{2,1,0:T(8,128)(2,1)S(1)} %get-tuple-element.113), channel_id=1, source_target_pairs={{0,24},{4,28},{8,0},{12,4},{16,8},{20,12},{24,16},{28,20},{1,25},{... | collective-permute-start | bytes 786440 | tf_op jit(solution)/shard_map/ppermute | solution.py:306
  171.4 26.2 %copy-start.12 = (bf16[128,128]{1,0:T(8,128)(2,1)S(1)}, bf16[128,128]{1,0:T(8,128)(2,1)}, u32[]{:S(2)}) copy-start(bf16[128,128]{1,0:T(8,128)(2,1)} %w_out.1) | copy-start | bytes 98308
  172.5 16.8 %all-to-all-start.2 = ((bf16[4,16,16,128]{3,2,1,0:T(8,128)(2,1)}), bf16[4,16,16,128]{3,2,1,0:T(8,128)(2,1)S(1)}, u32[]{:S(2)}, u32[]{:S(2)}) async-start(bf16[4,16,16,128]{3,2,1,0:T(8,128)(2,1)} %gather.2), calls=%async_computation.2 | async-start | bytes 524288 | tf_op jit(solution)/shard_map/all_to_all | solution.py:321
  (25 other events, 217.9 us)

commit v4 on v3

--- a/solution.py
+++ b/solution.py
@@ -74,7 +74,7 @@
         out[lo : lo + QBLOCK, :] = (own_rows + dot(gated, out_proj[...])).astype(BF)
 
 
-CHUNK = 256
+CHUNK = 512
 
 
 def pool_kernel(
@@ -115,7 +115,9 @@
             low = (hidden - high.astype(F32)).astype(BF)
             place = lax.broadcasted_iota(jnp.int32, (count, CHUNK), 1) + base
             hot = jnp.where((place >= opens) & (place < closes), 1.0, 0.0).astype(BF)
-            sums[0:count, :] += dot(hot, high) + dot(hot, low)
+            sums[0:count, :] += dot(
+                jnp.concatenate([hot, hot], axis=1), jnp.concatenate([high, low], axis=0)
+            )
             return carry
 
         lax.fori_loop(first, last, step, 0)
@@ -404,6 +406,8 @@
         single_to_pair,
     )
 
+    row_terms = pltpu.with_memory_space_constraint(row_terms, pltpu.HBM)
+    col_terms = pltpu.with_memory_space_constraint(col_terms, pltpu.HBM)
     pair_info = jnp.stack([col * tok_col + z * kz, valid_tokens[0], z, col]).astype(i32)
     hc = each // 2
     operands = []

time: 200 us -> 199 us (level)
    unnamed x61 -> x57, local copies, waits for them, and re-layouts: 8.95 us -> 7.28 us
  transfers between devices with their start and end apart: 30 -> 30, of which waited for: 17 -> 18; matrix products, arithmetic and copies ran while one was open for 5% -> 5% of each run, Pallas kernels for 19% -> 19%
where the time goes in v4:
time: 199 us; the launch traced here: 198 us
  waiting for transfers between devices  86.6 us (44%)
  starting transfers between devices  44.1 us (22%)
  Pallas kernels  40.5 us (20%)
  local copies, waits for them, and re-layouts  14.2 us (7%)
  blocking collectives  8.3 us (4%)
  other arithmetic  2.57 us (1%)
    ppermute x15, waiting for transfers between devices, shift_z(): return lax.ppermute(value, 'row', pairs)  49.3 us
    pallas_call x2, Pallas kernels, body(): pl.pallas_call(functools.partial(pair_kernel, groups, cols, halves, first...  21.9 us
    all_to_all x3, waiting for transfers between devices, spread_col(): return lax.all_to_all(value, 'col', split_axis=0, concat_axis=0, tiled=True)  19.6 us
    ppermute x15, starting transfers between devices, shift_z(): return lax.ppermute(value, 'row', pairs)  18.8 us
    ppermute x6, waiting for transfers between devices, cross_col(): return lax.ppermute(value, 'col', [(i, i ^ d) for i in range(cols)])  16.4 us
    all_to_all x3, starting transfers between devices, spread_col(): return lax.all_to_all(value, 'col', split_axis=0, concat_axis=0, tiled=True)  11.7 us
    all_to_all x1, blocking collectives, spread_col(): return lax.all_to_all(value, 'col', split_axis=0, concat_axis=0, tiled=True)  8.3 us
    unnamed x57, local copies, waits for them, and re-layouts  7.28 us
  transfers between devices with their start and end apart: 30, of which 18 were waited for; matrix products, arithmetic and copies ran while one was open for 5% of the time, Pallas kernels for 19%

profile of v4, /device:TPU:8, one launch (start us, length us, event | category | flops | bytes accessed | tf_op | source)
XLA Modules:
  0.0 198.1 jit_solution(12377663545924162646)
XLA Ops:
  1.4 3.4 %collective-permute-start = (bf16[48,128]{1,0:T(8,128)(2,1)S(1)}, bf16[48,128]{1,0:T(8,128)(2,1)S(1)}, u32[]{:S(2)}, u32[]{:S(2)}) collective-permute-start(bf16[48,128]{1,0:T(8,128)(2,1)S(1)} %get-tuple-element.125), channel_id=1, source_target_pairs={{0,1},{1,2},{2,3},{3,4},{4,5},{5,6},{6,7},{7,8},{8,9},{9,10},{10,1... | collective-permute-start | bytes 36872 | tf_op jit(solution)/shard_map/ppermute | solution.py:303
  4.8 4.0 %collective-permute-start.1 = (bf16[48,128]{1,0:T(8,128)(2,1)S(1)}, bf16[48,128]{1,0:T(8,128)(2,1)S(1)}, u32[]{:S(2)}, u32[]{:S(2)}) collective-permute-start(bf16[48,128]{1,0:T(8,128)(2,1)S(1)} %get-tuple-element.124), channel_id=1, source_target_pairs={{1,0},{2,1},{3,2},{4,3},{5,4},{6,5},{7,6},{8,7},{9,8},{10,9},{11,1... | collective-permute-start | bytes 36872 | tf_op jit(solution)/shard_map/ppermute | solution.py:304
  11.0 1.6 collective-permute-start.5
  15.2 2.0 %collective-permute-start.7 = (bf16[32,32,128]{2,1,0:T(8,128)(2,1)}, bf16[32,32,128]{2,1,0:T(8,128)(2,1)S(1)}, u32[]{:S(2)}, u32[]{:S(2)}) collective-permute-start(bf16[32,32,128]{2,1,0:T(8,128)(2,1)} %bitcast.41), channel_id=1, source_target_pairs={{0,24},{4,28},{8,0},{12,4},{16,8},{20,12},{24,16},{28,20},{1,25},{... | collective-permute-start | bytes 786440 | tf_op jit(solution)/shard_map/ppermute | solution.py:308
  18.7 2.2 %atoms.1 = bf16[160,128]{1,0:T(8,128)(2,1)S(1)} custom-call(s32[2]{0:T(128)S(1)} %pad_add_fusion.2.info, bf16[48,128]{1,0:T(8,128)(2,1)S(1)} %collective-permute-done.before, bf16[160,128]{1,0:T(8,128)(2,1)S(1)} %copy-done.5, bf16[48,128]{1,0:T(8,128)(2,1)S(1)} %collective-permute-done.1.after, f32[1,128]{1,0:T(1,128)S(1)} %bitcast.53, ...), custom_call_target="tpu_custom_call" | custom-call | flops 100000000 | bytes 1000000 | tf_op jit(solution)/shard_map/atoms/pallas_call | solution.py:336
  30.9 3.6 %collective-permute-done.6.refs_2_ = bf16[32,32,128]{2,1,0:T(8,128)(2,1)S(1)} collective-permute-done((bf16[32,32,128]{2,1,0:T(8,128)(2,1)}, bf16[32,32,128]{2,1,0:T(8,128)(2,1)S(1)}, u32[]{:S(2)}, u32[]{:S(2)}) %collective-permute-start.6) | collective-permute-done | bytes 262176 | tf_op jit(solution)/shard_map/ppermute | solution.py:308
  34.5 1.6 collective-permute-done.7.refs_3_
  36.9 1.6 collective-permute-start.9
  38.5 2.0 %collective-permute-start.10 = (bf16[640,128]{1,0:T(8,128)(2,1)S(1)}, bf16[640,128]{1,0:T(8,128)(2,1)S(1)}, u32[]{:S(2)}, u32[]{:S(2)}) collective-permute-start(bf16[640,128]{1,0:T(8,128)(2,1)S(1)} %pad_maximum_fusion.2.refs_0_), channel_id=1, source_target_pairs={{0,24},{4,28},{8,0},{12,4},{16,8},{20,12},{24,16},{28,20},{1,25},{... | collective-permute-start | bytes 491528 | tf_op jit(solution)/shard_map/ppermute | solution.py:308
  41.1 2.8 %collective-permute-done.8.refs_1_ = bf16[640,128]{1,0:T(8,128)(2,1)S(1)} collective-permute-done((bf16[640,128]{1,0:T(8,128)(2,1)S(1)}, bf16[640,128]{1,0:T(8,128)(2,1)S(1)}, u32[]{:S(2)}, u32[]{:S(2)}) %collective-permute-start.8) | collective-permute-done | bytes 163872 | tf_op jit(solution)/shard_map/ppermute | solution.py:308
  43.9 7.4 %collective-permute-done.9.refs_2_ = bf16[640,128]{1,0:T(8,128)(2,1)S(1)} collective-permute-done((bf16[640,128]{1,0:T(8,128)(2,1)S(1)}, bf16[640,128]{1,0:T(8,128)(2,1)S(1)}, u32[]{:S(2)}, u32[]{:S(2)}) %collective-permute-start.9) | collective-permute-done | bytes 163872 | tf_op jit(solution)/shard_map/ppermute | solution.py:308
  53.6 2.4 %collective-permute-start.13 = (bf16[48,32,128]{2,1,0:T(8,128)(2,1)}, bf16[48,32,128]{2,1,0:T(8,128)(2,1)}, u32[]{:S(2)}, u32[]{:S(2)}) collective-permute-start(bf16[48,32,128]{2,1,0:T(8,128)(2,1)} %get-tuple-element.84), channel_id=1, source_target_pairs={{0,16},{4,20},{8,24},{12,28},{16,0},{20,4},{24,8},{28,12},{1,17},{... | collective-permute-start | bytes 1179656 | tf_op jit(solution)/shard_map/ppermute | solution.py:308
  56.1 2.0 collective-permute-start.14
  60.2 6.6 %pool.1 = (bf16[320,384]{1,0:T(8,128)(2,1)}, f32[128,128]{1,0:T(8,128)S(1)}, f32[80,128]{1,0:T(8,128)S(1)}) custom-call(s32[3]{0:T(128)S(1)} %pad_add_fusion.1.info, s32[1281]{0:T(1024)S(1)} %pad_add_fusion.starts, bf16[640,128]{1,0:T(8,128)(2,1)S(1)} %pad_maximum_fusion.2.refs_0_, bf16[640,128]{1,0:T(8,128)(2,1)S(1)} %collective-permute-done.8.refs_1_, ...), custom_call_target="tpu_custom_call" | custom-call | flops 1000 | bytes 1000 | tf_op jit(solution)/shard_map/pool/pallas_call | solution.py:382
  68.0 9.0 %pair.2 = bf16[4,2,2,16,32,128]{5,4,3,2,1,0:T(8,128)(2,1)} custom-call(s32[4]{0:T(128)S(1)} %pad_add_fusion.3.info, bf16[32,32,128]{2,1,0:T(8,128)(2,1)S(1)} %bitcast.46, bf16[32,32,128]{2,1,0:T(8,128)(2,1)S(1)} %collective-permute-done.5.refs_1_, bf16[32,32,128]{2,1,0:T(8,128)(2,1)S(1)} %collective-permute-done.6.refs_2_, ...), custom_call_target="tpu_custom_call" | custom-call | flops 1000 | bytes 1000 | tf_op jit(solution)/shard_map/pair/pallas_call | solution.py:434
  77.1 4.6 %all-to-all-start = ((bf16[4,2,2,16,32,128]{5,4,3,2,1,0:T(8,128)(2,1)}), bf16[4,2,2,16,32,128]{5,4,3,2,1,0:T(8,128)(2,1)}, u32[]{:S(2)}, u32[]{:S(2)}) async-start(bf16[4,2,2,16,32,128]{5,4,3,2,1,0:T(8,128)(2,1)} %pair.2), calls=%async_computation | async-start | bytes 4194304 | tf_op jit(solution)/shard_map/all_to_all | solution.py:323
  81.7 6.8 %collective-permute-done.13.refs_2_ = bf16[48,32,128]{2,1,0:T(8,128)(2,1)} collective-permute-done((bf16[48,32,128]{2,1,0:T(8,128)(2,1)}, bf16[48,32,128]{2,1,0:T(8,128)(2,1)}, u32[]{:S(2)}, u32[]{:S(2)}) %collective-permute-start.13) | collective-permute-done | bytes 393248 | tf_op jit(solution)/shard_map/ppermute | solution.py:308
  88.5 2.9 %collective-permute-done.14.refs_3_ = bf16[48,32,128]{2,1,0:T(8,128)(2,1)} collective-permute-done((bf16[48,32,128]{2,1,0:T(8,128)(2,1)}, bf16[48,32,128]{2,1,0:T(8,128)(2,1)}, u32[]{:S(2)}, u32[]{:S(2)}) %collective-permute-start.14) | collective-permute-done | bytes 393248 | tf_op jit(solution)/shard_map/ppermute | solution.py:308
  91.4 12.9 %pair.3 = (bf16[4,1,2,16,48,128]{5,4,3,2,1,0:T(8,128)(2,1)}, bf16[1,1,2,16,48,128]{5,4,3,2,1,0:T(8,128)(2,1)S(1)}, bf16[1,1,2,16,48,128]{5,4,3,2,1,0:T(8,128)(2,...) custom-call(s32[4]{0:T(128)S(1)} %pad_add_fusion.3.info, ...), custom_call_target="tpu_custom_call" | custom-call | flops 30000001024 | bytes 1000000 | tf_op jit(solution)/shard_map/pair/pallas_call | solution.py:434
  106.6 3.7 %all-to-all-start.1 = ((bf16[4,1,2,16,48,128]{5,4,3,2,1,0:T(8,128)(2,1)}), bf16[4,1,2,16,48,128]{5,4,3,2,1,0:T(8,128)(2,1)S(1)}, u32[]{:S(2)}, u32[]{:S(2)}) async-start(bf16[4,1,2,16,48,128]{5,4,3,2,1,0:T(8,128)(2,1)} %get-tuple-element.96), calls=%async_computation.1 | async-start | bytes 3145728 | tf_op jit(solution)/shard_map/all_to_all | solution.py:323
  110.4 18.8 %all-to-all-done.1.refs_1_ = bf16[4,1,2,16,48,128]{5,4,3,2,1,0:T(8,128)(2,1)S(1)} async-done(((bf16[4,1,2,16,48,128]{5,4,3,2,1,0:T(8,128)(2,1)}), bf16[4,1,2,16,48,128]{5,4,3,2,1,0:T(8,128)(2,1)S(1)}, u32[]{:S(2)}, u32[]{:S(2)}) %all-to-all-start.1) | async-done | bytes 1572896 | tf_op jit(solution)/shard_map/all_to_all | solution.py:323
  132.7 3.2 %triangle.2 = (bf16[32,16,256]{2,1,0:T(8,128)(2,1)S(1)}, bf16[32,16,256]{2,1,0:T(8,128)(2,1)S(1)}, bf16[32,16,256]{2,1,0:T(8,128)(2,1)S(1)}, bf16[32,16,256]{2,1,0:T(8,128)(2,1)S(1)}) custom-call(s32[3]{0:T(128)S(1)} %pad_add_fusion.1.info, bf16[4,2,2,16,32,128]{5,4,3,2,1,0:T(8,128)(2,1)} %all-to-all-done.refs_0_, ...), custom_call_target="tpu_custom_call" | custom-call | flops 335544320 | bytes 10000000 | tf_op jit(solution)/shard_map/triangle/pallas_call | solution.py:506
  136.4 4.7 %collective-permute-done.18.refs_2_ = bf16[1,1,2,16,48,128]{5,4,3,2,1,0:T(8,128)(2,1)S(1)} collective-permute-done((bf16[1,1,2,16,48,128]{5,4,3,2,1,0:T(8,128)(2,1)S(1)}, bf16[1,1,2,16,48,128]{5,4,3,2,1,0:T(8,128)(2,1)S(1)}, u32[]{:S(2)}, u32[]{:S(2)}) %collective-permute-start.18) | collective-permute-done | bytes 393248 | tf_op jit(solution)/shard_map/ppermute | solution.py:311
  141.1 9.2 %collective-permute-done.19.refs_3_ = bf16[1,1,2,16,48,128]{5,4,3,2,1,0:T(8,128)(2,1)S(1)} collective-permute-done((bf16[1,1,2,16,48,128]{5,4,3,2,1,0:T(8,128)(2,1)S(1)}, bf16[1,1,2,16,48,128]{5,4,3,2,1,0:T(8,128)(2,1)S(1)}, u32[]{:S(2)}, u32[]{:S(2)}) %collective-permute-start.19) | collective-permute-done | bytes 393248 | tf_op jit(solution)/shard_map/ppermute | solution.py:311
  150.9 1.7 collective-permute-start.22
  154.0 3.2 %triangle.3 = (bf16[32,16,256]{2,1,0:T(8,128)(2,1)S(1)}, bf16[32,16,256]{2,1,0:T(8,128)(2,1)S(1)}, bf16[32,16,256]{2,1,0:T(8,128)(2,1)S(1)}, bf16[32,16,256]{2,1,0:T(8,128)(2,1)S(1)}) custom-call(s32[3]{0:T(128)S(1)} %pad_add_fusion.1.info, bf16[4,2,2,16,32,128]{5,4,3,2,1,0:T(8,128)(2,1)} %all-to-all-done.refs_0_, ...), custom_call_target="tpu_custom_call" | custom-call | flops 335544320 | bytes 10000000 | tf_op jit(solution)/shard_map/triangle/pallas_call | solution.py:506
  157.6 3.3 %collective-permute-start.25 = (bf16[32,16,256]{2,1,0:T(8,128)(2,1)S(1)}, bf16[32,16,256]{2,1,0:T(8,128)(2,1)S(1)}, u32[]{:S(2)}, u32[]{:S(2)}) collective-permute-start(bf16[32,16,256]{2,1,0:T(8,128)(2,1)S(1)} %get-tuple-element.112), channel_id=1, source_target_pairs={{0,16},{4,20},{8,24},{12,28},{16,0},{20,4},{24,8},{28,12},{1,17},{... | collective-permute-start | bytes 786440 | tf_op jit(solution)/shard_map/ppermute | solution.py:308
  160.9 10.8 %collective-permute-done.22.refs_3_ = bf16[32,16,256]{2,1,0:T(8,128)(2,1)S(1)} collective-permute-done((bf16[32,16,256]{2,1,0:T(8,128)(2,1)S(1)}, bf16[32,16,256]{2,1,0:T(8,128)(2,1)S(1)}, u32[]{:S(2)}, u32[]{:S(2)}) %collective-permute-start.22) | collective-permute-done | bytes 262176 | tf_op jit(solution)/shard_map/ppermute | solution.py:308
  172.7 3.4 %all-to-all-start.2 = ((bf16[4,16,16,128]{3,2,1,0:T(8,128)(2,1)}), bf16[4,16,16,128]{3,2,1,0:T(8,128)(2,1)S(1)}, u32[]{:S(2)}, u32[]{:S(2)}) async-start(bf16[4,16,16,128]{3,2,1,0:T(8,128)(2,1)} %gather.2), calls=%async_computation.2 | async-start | bytes 524288 | tf_op jit(solution)/shard_map/all_to_all | solution.py:323
  176.1 9.8 %collective-permute-done.25.refs_2_ = bf16[32,16,256]{2,1,0:T(8,128)(2,1)S(1)} collective-permute-done((bf16[32,16,256]{2,1,0:T(8,128)(2,1)S(1)}, bf16[32,16,256]{2,1,0:T(8,128)(2,1)S(1)}, u32[]{:S(2)}, u32[]{:S(2)}) %collective-permute-start.25) | collective-permute-done | bytes 262176 | tf_op jit(solution)/shard_map/ppermute | solution.py:308
  187.8 8.3 %all_to_all.20.second = bf16[4,16,16,128]{3,2,1,0:T(8,128)(2,1)S(1)} all-to-all(bf16[4,16,16,128]{3,2,1,0:T(8,128)(2,1)S(1)} %gather.3), channel_id=1, replica_groups=mesh['row'=8,'col'=4] {'col'}, dimensions={0} | all-to-all | bytes 524288 | tf_op jit(solution)/shard_map/all_to_all | solution.py:323
  196.2 1.9 finish.1
  (123 shorter events, 34.8 us)
Async XLA Ops:
  1.4 17.3 %collective-permute-start = (bf16[48,128]{1,0:T(8,128)(2,1)S(1)}, bf16[48,128]{1,0:T(8,128)(2,1)S(1)}, u32[]{:S(2)}, u32[]{:S(2)}) collective-permute-start(bf16[48,128]{1,0:T(8,128)(2,1)S(1)} %get-tuple-element.125), channel_id=1, source_target_pairs={{0,1},{1,2},{2,3},{3,4},{4,5},{5,6},{6,7},{7,8},{8,9},{9,10},{10,1... | collective-permute-start | bytes 36872 | tf_op jit(solution)/shard_map/ppermute | solution.py:303
  4.8 13.9 %collective-permute-start.1 = (bf16[48,128]{1,0:T(8,128)(2,1)S(1)}, bf16[48,128]{1,0:T(8,128)(2,1)S(1)}, u32[]{:S(2)}, u32[]{:S(2)}) collective-permute-start(bf16[48,128]{1,0:T(8,128)(2,1)S(1)} %get-tuple-element.124), channel_id=1, source_target_pairs={{1,0},{2,1},{3,2},{4,3},{5,4},{6,5},{7,6},{8,7},{9,8},{10,9},{11,1... | collective-permute-start | bytes 36872 | tf_op jit(solution)/shard_map/ppermute | solution.py:304
  11.0 19.9 %collective-permute-start.5 = (bf16[32,32,128]{2,1,0:T(8,128)(2,1)}, bf16[32,32,128]{2,1,0:T(8,128)(2,1)S(1)}, u32[]{:S(2)}, u32[]{:S(2)}) collective-permute-start(bf16[32,32,128]{2,1,0:T(8,128)(2,1)} %bitcast.43), channel_id=1, source_target_pairs={{0,8},{4,12},{8,16},{12,20},{16,24},{20,28},{24,0},{28,4},{1,9},{5... | collective-permute-start | bytes 786440 | tf_op jit(solution)/shard_map/ppermute | solution.py:308
  13.4 21.1 %collective-permute-start.6 = (bf16[32,32,128]{2,1,0:T(8,128)(2,1)}, bf16[32,32,128]{2,1,0:T(8,128)(2,1)S(1)}, u32[]{:S(2)}, u32[]{:S(2)}) collective-permute-start(bf16[32,32,128]{2,1,0:T(8,128)(2,1)} %bitcast.42), channel_id=1, source_target_pairs={{0,16},{4,20},{8,24},{12,28},{16,0},{20,4},{24,8},{28,12},{1,17},{... | collective-permute-start | bytes 786440 | tf_op jit(solution)/shard_map/ppermute | solution.py:308
  15.2 20.9 %collective-permute-start.7 = (bf16[32,32,128]{2,1,0:T(8,128)(2,1)}, bf16[32,32,128]{2,1,0:T(8,128)(2,1)S(1)}, u32[]{:S(2)}, u32[]{:S(2)}) collective-permute-start(bf16[32,32,128]{2,1,0:T(8,128)(2,1)} %bitcast.41), channel_id=1, source_target_pairs={{0,24},{4,28},{8,0},{12,4},{16,8},{20,12},{24,16},{28,20},{1,25},{... | collective-permute-start | bytes 786440 | tf_op jit(solution)/shard_map/ppermute | solution.py:308
  20.9 5.0 %collective-permute-start.4 = (bf16[160,128]{1,0:T(8,128)(2,1)S(1)}, bf16[160,128]{1,0:T(8,128)(2,1)S(1)}, u32[]{:S(2)}, u32[]{:S(2)}) collective-permute-start(bf16[160,128]{1,0:T(8,128)(2,1)S(1)} %atoms.1), channel_id=1, source_target_pairs={{0,3},{1,2},{2,1},{3,0},{4,7},{5,6},{6,5},{7,4},{8,11},{9,10},{10,... | collective-permute-start | bytes 122888 | tf_op jit(solution)/shard_map/ppermute | solution.py:311
  21.8 6.6 %collective-permute-start.3 = (bf16[160,128]{1,0:T(8,128)(2,1)S(1)}, bf16[160,128]{1,0:T(8,128)(2,1)S(1)}, u32[]{:S(2)}, u32[]{:S(2)}) collective-permute-start(bf16[160,128]{1,0:T(8,128)(2,1)S(1)} %atoms.1), channel_id=1, source_target_pairs={{0,2},{1,3},{2,0},{3,1},{4,6},{5,7},{6,4},{7,5},{8,10},{9,11},{10,... | collective-permute-start | bytes 122888 | tf_op jit(solution)/shard_map/ppermute | solution.py:311
  25.9 4.0 %collective-permute-start.2 = (bf16[160,128]{1,0:T(8,128)(2,1)S(1)}, bf16[160,128]{1,0:T(8,128)(2,1)S(1)}, u32[]{:S(2)}, u32[]{:S(2)}) collective-permute-start(bf16[160,128]{1,0:T(8,128)(2,1)S(1)} %atoms.1), channel_id=1, source_target_pairs={{0,1},{1,0},{2,3},{3,2},{4,5},{5,4},{6,7},{7,6},{8,9},{9,8},{10,11... | collective-permute-start | bytes 122888 | tf_op jit(solution)/shard_map/ppermute | solution.py:311
  28.0 25.5 %copy-start.20 = (s32[1280]{0:T(1024)S(1)}, s32[1280]{0:T(1024)}, u32[]{:S(2)}) copy-start(s32[1280]{0:T(1024)} %get-tuple-element.114) | copy-start | bytes 15364
  28.0 31.2 %copy-start.6 = (bf16[128,384]{1,0:T(8,128)(2,1)S(1)}, bf16[128,384]{1,0:T(8,128)(2,1)}, u32[]{:S(2)}) copy-start(bf16[128,384]{1,0:T(8,128)(2,1)} %refs_7_.1) | copy-start | bytes 294916
  36.9 7.1 %collective-permute-start.8 = (bf16[640,128]{1,0:T(8,128)(2,1)S(1)}, bf16[640,128]{1,0:T(8,128)(2,1)S(1)}, u32[]{:S(2)}, u32[]{:S(2)}) collective-permute-start(bf16[640,128]{1,0:T(8,128)(2,1)S(1)} %pad_maximum_fusion.2.refs_0_), channel_id=1, source_target_pairs={{0,8},{4,12},{8,16},{12,20},{16,24},{20,28},{24,0},{28,4},{1,9},{5... | collective-permute-start | bytes 491528 | tf_op jit(solution)/shard_map/ppermute | solution.py:308
  36.9 14.5 %collective-permute-start.9 = (bf16[640,128]{1,0:T(8,128)(2,1)S(1)}, bf16[640,128]{1,0:T(8,128)(2,1)S(1)}, u32[]{:S(2)}, u32[]{:S(2)}) collective-permute-start(bf16[640,128]{1,0:T(8,128)(2,1)S(1)} %pad_maximum_fusion.2.refs_0_), channel_id=1, source_target_pairs={{0,16},{4,20},{8,24},{12,28},{16,0},{20,4},{24,8},{28,12},{1,17},{... | collective-permute-start | bytes 491528 | tf_op jit(solution)/shard_map/ppermute | solution.py:308
  38.5 13.8 %collective-permute-start.10 = (bf16[640,128]{1,0:T(8,128)(2,1)S(1)}, bf16[640,128]{1,0:T(8,128)(2,1)S(1)}, u32[]{:S(2)}, u32[]{:S(2)}) collective-permute-start(bf16[640,128]{1,0:T(8,128)(2,1)S(1)} %pad_maximum_fusion.2.refs_0_), channel_id=1, source_target_pairs={{0,24},{4,28},{8,0},{12,4},{16,8},{20,12},{24,16},{28,20},{1,25},{... | collective-permute-start | bytes 491528 | tf_op jit(solution)/shard_map/ppermute | solution.py:308
  53.4 5.8 %collective-permute-start.11 = (bf16[2560,128]{1,0:T(8,128)(2,1)}, bf16[2560,128]{1,0:T(8,128)(2,1)S(1)}, u32[]{:S(2)}, u32[]{:S(2)}) collective-permute-start(bf16[2560,128]{1,0:T(8,128)(2,1)} %pad_maximum_fusion.1), channel_id=1, source_target_pairs={{0,4},{4,0},{8,12},{12,8},{16,20},{20,16},{24,28},{28,24},{1,5},{5... | collective-permute-start | bytes 1966088 | tf_op jit(solution)/shard_map/ppermute | solution.py:314
  53.6 28.1 %collective-permute-start.12 = (bf16[48,32,128]{2,1,0:T(8,128)(2,1)}, bf16[48,32,128]{2,1,0:T(8,128)(2,1)}, u32[]{:S(2)}, u32[]{:S(2)}) collective-permute-start(bf16[48,32,128]{2,1,0:T(8,128)(2,1)} %get-tuple-element.83), channel_id=1, source_target_pairs={{0,8},{4,12},{8,16},{12,20},{16,24},{20,28},{24,0},{28,4},{1,9},{5... | collective-permute-start | bytes 1179656 | tf_op jit(solution)/shard_map/ppermute | solution.py:308
  53.6 34.9 %collective-permute-start.13 = (bf16[48,32,128]{2,1,0:T(8,128)(2,1)}, bf16[48,32,128]{2,1,0:T(8,128)(2,1)}, u32[]{:S(2)}, u32[]{:S(2)}) collective-permute-start(bf16[48,32,128]{2,1,0:T(8,128)(2,1)} %get-tuple-element.84), channel_id=1, source_target_pairs={{0,16},{4,20},{8,24},{12,28},{16,0},{20,4},{24,8},{28,12},{1,17},{... | collective-permute-start | bytes 1179656 | tf_op jit(solution)/shard_map/ppermute | solution.py:308
  56.1 35.3 %collective-permute-start.14 = (bf16[48,32,128]{2,1,0:T(8,128)(2,1)}, bf16[48,32,128]{2,1,0:T(8,128)(2,1)}, u32[]{:S(2)}, u32[]{:S(2)}) collective-permute-start(bf16[48,32,128]{2,1,0:T(8,128)(2,1)} %get-tuple-element.85), channel_id=1, source_target_pairs={{0,24},{4,28},{8,0},{12,4},{16,8},{20,12},{24,16},{28,20},{1,25},{... | collective-permute-start | bytes 1179656 | tf_op jit(solution)/shard_map/ppermute | solution.py:308
  77.1 29.6 %all-to-all-start = ((bf16[4,2,2,16,32,128]{5,4,3,2,1,0:T(8,128)(2,1)}), bf16[4,2,2,16,32,128]{5,4,3,2,1,0:T(8,128)(2,1)}, u32[]{:S(2)}, u32[]{:S(2)}) async-start(bf16[4,2,2,16,32,128]{5,4,3,2,1,0:T(8,128)(2,1)} %pair.2), calls=%async_computation | async-start | bytes 4194304 | tf_op jit(solution)/shard_map/all_to_all | solution.py:323
  106.6 22.6 %all-to-all-start.1 = ((bf16[4,1,2,16,48,128]{5,4,3,2,1,0:T(8,128)(2,1)}), bf16[4,1,2,16,48,128]{5,4,3,2,1,0:T(8,128)(2,1)S(1)}, u32[]{:S(2)}, u32[]{:S(2)}) async-start(bf16[4,1,2,16,48,128]{5,4,3,2,1,0:T(8,128)(2,1)} %get-tuple-element.96), calls=%async_computation.1 | async-start | bytes 3145728 | tf_op jit(solution)/shard_map/all_to_all | solution.py:323
  110.3 22.4 %collective-permute-start.15 = (bf16[4,2,2,16,32,128]{5,4,3,2,1,0:T(8,128)(2,1)}, bf16[4,2,2,16,32,128]{5,4,3,2,1,0:T(8,128)(2,1)}, u32[]{:S(2)}, u32[]{:S(2)}) collective-permute-start(bf16[4,2,2,16,32,128]{5,4,3,2,1,0:T(8,128)(2,1)} %all-to-all-done.refs_0_), channel_id=1, source_target_pairs={{0,4},{4,0},{8,12},{12,8},{16,20},{20,16},{24,28},{28,24},{1,5},{5... | collective-permute-start | bytes 6291464 | tf_op jit(solution)/shard_map/ppermute | solution.py:314
  129.2 3.5 %collective-permute-start.16 = (bf16[4,1,2,16,48,128]{5,4,3,2,1,0:T(8,128)(2,1)S(1)}, bf16[4,1,2,16,48,128]{5,4,3,2,1,0:T(8,128)(2,1)S(1)}, u32[]{:S(2)}, u32[]{:S(2)}) collective-permute-start(bf16[4,1,2,16,48,128]{5,4,3,2,1,0:T(8,128)(2,1)S(1)} %all-to-all-done.1.refs_1_), channel_id=1, source_target_pairs={{0,4},{4,0},{8,12},{12,8},{16,20},{20,16},{24,28},{28,24},{1,5},{5... | collective-permute-start | bytes 4718600 | tf_op jit(solution)/shard_map/ppermute | solution.py:314
  129.2 11.9 %collective-permute-start.18 = (bf16[1,1,2,16,48,128]{5,4,3,2,1,0:T(8,128)(2,1)S(1)}, bf16[1,1,2,16,48,128]{5,4,3,2,1,0:T(8,128)(2,1)S(1)}, u32[]{:S(2)}, u32[]{:S(2)}) collective-permute-start(bf16[1,1,2,16,48,128]{5,4,3,2,1,0:T(8,128)(2,1)S(1)} %copy-done.15), channel_id=1, source_target_pairs={{0,1},{1,0},{2,3},{3,2},{4,5},{5,4},{6,7},{7,6},{8,9},{9,8},{10,11... | collective-permute-start | bytes 1179656 | tf_op jit(solution)/shard_map/ppermute | solution.py:311
  130.6 19.7 %collective-permute-start.19 = (bf16[1,1,2,16,48,128]{5,4,3,2,1,0:T(8,128)(2,1)S(1)}, bf16[1,1,2,16,48,128]{5,4,3,2,1,0:T(8,128)(2,1)S(1)}, u32[]{:S(2)}, u32[]{:S(2)}) collective-permute-start(bf16[1,1,2,16,48,128]{5,4,3,2,1,0:T(8,128)(2,1)S(1)} %copy-done.13), channel_id=1, source_target_pairs={{0,2},{1,3},{2,0},{3,1},{4,6},{5,7},{6,4},{7,5},{8,10},{9,11},{10,... | collective-permute-start | bytes 1179656 | tf_op jit(solution)/shard_map/ppermute | solution.py:311
  131.2 19.1 %collective-permute-start.20 = (bf16[1,1,2,16,48,128]{5,4,3,2,1,0:T(8,128)(2,1)S(1)}, bf16[1,1,2,16,48,128]{5,4,3,2,1,0:T(8,128)(2,1)S(1)}, u32[]{:S(2)}, u32[]{:S(2)}) collective-permute-start(bf16[1,1,2,16,48,128]{5,4,3,2,1,0:T(8,128)(2,1)S(1)} %get-tuple-element.102), channel_id=1, source_target_pairs={{0,3},{1,2},{2,1},{3,0},{4,7},{5,6},{6,5},{7,4},{8,11},{9,10},{10,... | collective-permute-start | bytes 1179656 | tf_op jit(solution)/shard_map/ppermute | solution.py:311
  135.9 14.4 %collective-permute-start.21 = (bf16[32,16,256]{2,1,0:T(8,128)(2,1)S(1)}, bf16[32,16,256]{2,1,0:T(8,128)(2,1)S(1)}, u32[]{:S(2)}, u32[]{:S(2)}) collective-permute-start(bf16[32,16,256]{2,1,0:T(8,128)(2,1)S(1)} %get-tuple-element.103), channel_id=1, source_target_pairs={{0,16},{4,20},{8,24},{12,28},{16,0},{20,4},{24,8},{28,12},{1,17},{... | collective-permute-start | bytes 786440 | tf_op jit(solution)/shard_map/ppermute | solution.py:308
  150.5 3.5 %collective-permute-start.23 = (bf16[4,1,2,16,48,128]{5,4,3,2,1,0:T(8,128)(2,1)S(1)}, bf16[4,1,2,16,48,128]{5,4,3,2,1,0:T(8,128)(2,1)S(1)}, u32[]{:S(2)}, u32[]{:S(2)}) collective-permute-start(bf16[4,1,2,16,48,128]{5,4,3,2,1,0:T(8,128)(2,1)S(1)} %pad_maximum_fusion), channel_id=1, source_target_pairs={{0,4},{4,0},{8,12},{12,8},{16,20},{20,16},{24,28},{28,24},{1,5},{5... | collective-permute-start | bytes 4718600 | tf_op jit(solution)/shard_map/ppermute | solution.py:314
  150.6 10.3 %collective-permute-start.17 = (bf16[32,16,256]{2,1,0:T(8,128)(2,1)S(1)}, bf16[32,16,256]{2,1,0:T(8,128)(2,1)S(1)}, u32[]{:S(2)}, u32[]{:S(2)}) collective-permute-start(bf16[32,16,256]{2,1,0:T(8,128)(2,1)S(1)} %get-tuple-element.98), channel_id=1, source_target_pairs={{0,8},{4,12},{8,16},{12,20},{16,24},{20,28},{24,0},{28,4},{1,9},{5... | collective-permute-start | bytes 786440 | tf_op jit(solution)/shard_map/ppermute | solution.py:308
  150.9 20.7 %collective-permute-start.22 = (bf16[32,16,256]{2,1,0:T(8,128)(2,1)S(1)}, bf16[32,16,256]{2,1,0:T(8,128)(2,1)S(1)}, u32[]{:S(2)}, u32[]{:S(2)}) collective-permute-start(bf16[32,16,256]{2,1,0:T(8,128)(2,1)S(1)} %get-tuple-element.105), channel_id=1, source_target_pairs={{0,24},{4,28},{8,0},{12,4},{16,8},{20,12},{24,16},{28,20},{1,25},{... | collective-permute-start | bytes 786440 | tf_op jit(solution)/shard_map/ppermute | solution.py:308
  157.2 18.9 %collective-permute-start.24 = (bf16[32,16,256]{2,1,0:T(8,128)(2,1)S(1)}, bf16[32,16,256]{2,1,0:T(8,128)(2,1)S(1)}, u32[]{:S(2)}, u32[]{:S(2)}) collective-permute-start(bf16[32,16,256]{2,1,0:T(8,128)(2,1)S(1)} %get-tuple-element.111), channel_id=1, source_target_pairs={{0,8},{4,12},{8,16},{12,20},{16,24},{20,28},{24,0},{28,4},{1,9},{5... | collective-permute-start | bytes 786440 | tf_op jit(solution)/shard_map/ppermute | solution.py:308
  157.6 28.3 %collective-permute-start.25 = (bf16[32,16,256]{2,1,0:T(8,128)(2,1)S(1)}, bf16[32,16,256]{2,1,0:T(8,128)(2,1)S(1)}, u32[]{:S(2)}, u32[]{:S(2)}) collective-permute-start(bf16[32,16,256]{2,1,0:T(8,128)(2,1)S(1)} %get-tuple-element.112), channel_id=1, source_target_pairs={{0,16},{4,20},{8,24},{12,28},{16,0},{20,4},{24,8},{28,12},{1,17},{... | collective-permute-start | bytes 786440 | tf_op jit(solution)/shard_map/ppermute | solution.py:308
  160.9 26.6 %collective-permute-start.26 = (bf16[32,16,256]{2,1,0:T(8,128)(2,1)S(1)}, bf16[32,16,256]{2,1,0:T(8,128)(2,1)S(1)}, u32[]{:S(2)}, u32[]{:S(2)}) collective-permute-start(bf16[32,16,256]{2,1,0:T(8,128)(2,1)S(1)} %get-tuple-element.113), channel_id=1, source_target_pairs={{0,24},{4,28},{8,0},{12,4},{16,8},{20,12},{24,16},{28,20},{1,25},{... | collective-permute-start | bytes 786440 | tf_op jit(solution)/shard_map/ppermute | solution.py:308
  172.7 15.1 %all-to-all-start.2 = ((bf16[4,16,16,128]{3,2,1,0:T(8,128)(2,1)}), bf16[4,16,16,128]{3,2,1,0:T(8,128)(2,1)S(1)}, u32[]{:S(2)}, u32[]{:S(2)}) async-start(bf16[4,16,16,128]{3,2,1,0:T(8,128)(2,1)} %gather.2), calls=%async_computation.2 | async-start | bytes 524288 | tf_op jit(solution)/shard_map/all_to_all | solution.py:323
  (23 other events, 212.9 us)

commit v5 on v4

--- a/solution.py
+++ b/solution.py
@@ -152,7 +152,7 @@
         zz = lax.rem(z - d + groups, groups)
         rows_buf[:, pl.ds(pl.multiple_of(zz * per, 32), per), :] = xs[d][...]
     at = k_first + chunk_at + pl.program_id(0) * kb
-    tile = max(1, 1024 // lanes)
+    tile = min(kb, max(1, 2048 // lanes))
     repeat = tile * lanes // 128
     hidden = w_in.shape[0] // 2
 

time: 199 us -> 198 us (level)
  no operation moved by 1% of the time
where the time goes in v5:
time: 198 us
  waiting for transfers between devices  87.6 us (44%)
  starting transfers between devices  44 us (22%)
  Pallas kernels  39.1 us (20%)
  local copies, waits for them, and re-layouts  14.2 us (7%)
  blocking collectives  8.26 us (4%)
  other arithmetic  2.57 us (1%)
    ppermute x15, waiting for transfers between devices, shift_z(): return lax.ppermute(value, 'row', pairs)  50.3 us
    pallas_call x2, Pallas kernels, body(): pl.pallas_call(functools.partial(pair_kernel, groups, cols, halves, first...  21 us
    all_to_all x3, waiting for transfers between devices, spread_col(): return lax.all_to_all(value, 'col', split_axis=0, concat_axis=0, tiled=True)  19.6 us
    ppermute x15, starting transfers between devices, shift_z(): return lax.ppermute(value, 'row', pairs)  18.8 us
    ppermute x6, waiting for transfers between devices, cross_col(): return lax.ppermute(value, 'col', [(i, i ^ d) for i in range(cols)])  16.3 us
    all_to_all x3, starting transfers between devices, spread_col(): return lax.all_to_all(value, 'col', split_axis=0, concat_axis=0, tiled=True)  11.7 us
    all_to_all x1, blocking collectives, spread_col(): return lax.all_to_all(value, 'col', split_axis=0, concat_axis=0, tiled=True)  8.26 us
    unnamed x57, local copies, waits for them, and re-layouts  7.28 us
  transfers between devices with their start and end apart: 30, of which 18 were waited for; matrix products, arithmetic and copies ran while one was open for 5% of the time, Pallas kernels for 19%

profile of v5, /device:TPU:8, one launch (start us, length us, event | category | flops | bytes accessed | tf_op | source)
XLA Modules:
  0.0 197.6 jit_solution(16395470450359471531)
XLA Ops:
  1.4 3.4 %collective-permute-start = (bf16[48,128]{1,0:T(8,128)(2,1)S(1)}, bf16[48,128]{1,0:T(8,128)(2,1)S(1)}, u32[]{:S(2)}, u32[]{:S(2)}) collective-permute-start(bf16[48,128]{1,0:T(8,128)(2,1)S(1)} %get-tuple-element.125), channel_id=1, source_target_pairs={{0,1},{1,2},{2,3},{3,4},{4,5},{5,6},{6,7},{7,8},{8,9},{9,10},{10,1... | collective-permute-start | bytes 36872 | tf_op jit(solution)/shard_map/ppermute | solution.py:303
  4.8 4.0 %collective-permute-start.1 = (bf16[48,128]{1,0:T(8,128)(2,1)S(1)}, bf16[48,128]{1,0:T(8,128)(2,1)S(1)}, u32[]{:S(2)}, u32[]{:S(2)}) collective-permute-start(bf16[48,128]{1,0:T(8,128)(2,1)S(1)} %get-tuple-element.124), channel_id=1, source_target_pairs={{1,0},{2,1},{3,2},{4,3},{5,4},{6,5},{7,6},{8,7},{9,8},{10,9},{11,1... | collective-permute-start | bytes 36872 | tf_op jit(solution)/shard_map/ppermute | solution.py:304
  15.2 2.0 %collective-permute-start.7 = (bf16[32,32,128]{2,1,0:T(8,128)(2,1)}, bf16[32,32,128]{2,1,0:T(8,128)(2,1)S(1)}, u32[]{:S(2)}, u32[]{:S(2)}) collective-permute-start(bf16[32,32,128]{2,1,0:T(8,128)(2,1)} %bitcast.41), channel_id=1, source_target_pairs={{0,24},{4,28},{8,0},{12,4},{16,8},{20,12},{24,16},{28,20},{1,25},{... | collective-permute-start | bytes 786440 | tf_op jit(solution)/shard_map/ppermute | solution.py:308
  18.7 2.2 %atoms.1 = bf16[160,128]{1,0:T(8,128)(2,1)S(1)} custom-call(s32[2]{0:T(128)S(1)} %pad_add_fusion.2.info, bf16[48,128]{1,0:T(8,128)(2,1)S(1)} %collective-permute-done.before, bf16[160,128]{1,0:T(8,128)(2,1)S(1)} %copy-done.5, bf16[48,128]{1,0:T(8,128)(2,1)S(1)} %collective-permute-done.1.after, f32[1,128]{1,0:T(1,128)S(1)} %bitcast.53, ...), custom_call_target="tpu_custom_call" | custom-call | flops 100000000 | bytes 1000000 | tf_op jit(solution)/shard_map/atoms/pallas_call | solution.py:336
  30.9 3.6 %collective-permute-done.6.refs_2_ = bf16[32,32,128]{2,1,0:T(8,128)(2,1)S(1)} collective-permute-done((bf16[32,32,128]{2,1,0:T(8,128)(2,1)}, bf16[32,32,128]{2,1,0:T(8,128)(2,1)S(1)}, u32[]{:S(2)}, u32[]{:S(2)}) %collective-permute-start.6) | collective-permute-done | bytes 262176 | tf_op jit(solution)/shard_map/ppermute | solution.py:308
  34.5 1.6 collective-permute-done.7.refs_3_
  36.9 1.6 collective-permute-start.9
  38.5 2.0 %collective-permute-start.10 = (bf16[640,128]{1,0:T(8,128)(2,1)S(1)}, bf16[640,128]{1,0:T(8,128)(2,1)S(1)}, u32[]{:S(2)}, u32[]{:S(2)}) collective-permute-start(bf16[640,128]{1,0:T(8,128)(2,1)S(1)} %pad_maximum_fusion.2.refs_0_), channel_id=1, source_target_pairs={{0,24},{4,28},{8,0},{12,4},{16,8},{20,12},{24,16},{28,20},{1,25},{... | collective-permute-start | bytes 491528 | tf_op jit(solution)/shard_map/ppermute | solution.py:308
  41.1 2.8 %collective-permute-done.8.refs_1_ = bf16[640,128]{1,0:T(8,128)(2,1)S(1)} collective-permute-done((bf16[640,128]{1,0:T(8,128)(2,1)S(1)}, bf16[640,128]{1,0:T(8,128)(2,1)S(1)}, u32[]{:S(2)}, u32[]{:S(2)}) %collective-permute-start.8) | collective-permute-done | bytes 163872 | tf_op jit(solution)/shard_map/ppermute | solution.py:308
  43.9 7.4 %collective-permute-done.9.refs_2_ = bf16[640,128]{1,0:T(8,128)(2,1)S(1)} collective-permute-done((bf16[640,128]{1,0:T(8,128)(2,1)S(1)}, bf16[640,128]{1,0:T(8,128)(2,1)S(1)}, u32[]{:S(2)}, u32[]{:S(2)}) %collective-permute-start.9) | collective-permute-done | bytes 163872 | tf_op jit(solution)/shard_map/ppermute | solution.py:308
  53.6 2.4 %collective-permute-start.13 = (bf16[48,32,128]{2,1,0:T(8,128)(2,1)}, bf16[48,32,128]{2,1,0:T(8,128)(2,1)}, u32[]{:S(2)}, u32[]{:S(2)}) collective-permute-start(bf16[48,32,128]{2,1,0:T(8,128)(2,1)} %get-tuple-element.84), channel_id=1, source_target_pairs={{0,16},{4,20},{8,24},{12,28},{16,0},{20,4},{24,8},{28,12},{1,17},{... | collective-permute-start | bytes 1179656 | tf_op jit(solution)/shard_map/ppermute | solution.py:308
  56.1 2.0 collective-permute-start.14
  60.2 6.1 %pool.1 = (bf16[320,384]{1,0:T(8,128)(2,1)}, f32[128,128]{1,0:T(8,128)S(1)}, f32[80,128]{1,0:T(8,128)S(1)}) custom-call(s32[3]{0:T(128)S(1)} %pad_add_fusion.1.info, s32[1281]{0:T(1024)S(1)} %pad_add_fusion.starts, bf16[640,128]{1,0:T(8,128)(2,1)S(1)} %pad_maximum_fusion.2.refs_0_, bf16[640,128]{1,0:T(8,128)(2,1)S(1)} %collective-permute-done.8.refs_1_, ...), custom_call_target="tpu_custom_call" | custom-call | flops 1000 | bytes 1000 | tf_op jit(solution)/shard_map/pool/pallas_call | solution.py:382
  67.5 8.7 %pair.2 = bf16[4,2,2,16,32,128]{5,4,3,2,1,0:T(8,128)(2,1)} custom-call(s32[4]{0:T(128)S(1)} %pad_add_fusion.3.info, bf16[32,32,128]{2,1,0:T(8,128)(2,1)S(1)} %bitcast.46, bf16[32,32,128]{2,1,0:T(8,128)(2,1)S(1)} %collective-permute-done.5.refs_1_, bf16[32,32,128]{2,1,0:T(8,128)(2,1)S(1)} %collective-permute-done.6.refs_2_, ...), custom_call_target="tpu_custom_call" | custom-call | flops 1000 | bytes 1000 | tf_op jit(solution)/shard_map/pair/pallas_call | solution.py:434
  76.2 4.6 %all-to-all-start = ((bf16[4,2,2,16,32,128]{5,4,3,2,1,0:T(8,128)(2,1)}), bf16[4,2,2,16,32,128]{5,4,3,2,1,0:T(8,128)(2,1)}, u32[]{:S(2)}, u32[]{:S(2)}) async-start(bf16[4,2,2,16,32,128]{5,4,3,2,1,0:T(8,128)(2,1)} %pair.2), calls=%async_computation | async-start | bytes 4194304 | tf_op jit(solution)/shard_map/all_to_all | solution.py:323
  80.8 7.7 %collective-permute-done.13.refs_2_ = bf16[48,32,128]{2,1,0:T(8,128)(2,1)} collective-permute-done((bf16[48,32,128]{2,1,0:T(8,128)(2,1)}, bf16[48,32,128]{2,1,0:T(8,128)(2,1)}, u32[]{:S(2)}, u32[]{:S(2)}) %collective-permute-start.13) | collective-permute-done | bytes 393248 | tf_op jit(solution)/shard_map/ppermute | solution.py:308
  88.5 2.9 %collective-permute-done.14.refs_3_ = bf16[48,32,128]{2,1,0:T(8,128)(2,1)} collective-permute-done((bf16[48,32,128]{2,1,0:T(8,128)(2,1)}, bf16[48,32,128]{2,1,0:T(8,128)(2,1)}, u32[]{:S(2)}, u32[]{:S(2)}) %collective-permute-start.14) | collective-permute-done | bytes 393248 | tf_op jit(solution)/shard_map/ppermute | solution.py:308
  91.4 12.4 %pair.3 = (bf16[4,1,2,16,48,128]{5,4,3,2,1,0:T(8,128)(2,1)}, bf16[1,1,2,16,48,128]{5,4,3,2,1,0:T(8,128)(2,1)S(1)}, bf16[1,1,2,16,48,128]{5,4,3,2,1,0:T(8,128)(2,...) custom-call(s32[4]{0:T(128)S(1)} %pad_add_fusion.3.info, ...), custom_call_target="tpu_custom_call" | custom-call | flops 30000001024 | bytes 1000000 | tf_op jit(solution)/shard_map/pair/pallas_call | solution.py:434
  105.9 3.7 %all-to-all-start.1 = ((bf16[4,1,2,16,48,128]{5,4,3,2,1,0:T(8,128)(2,1)}), bf16[4,1,2,16,48,128]{5,4,3,2,1,0:T(8,128)(2,1)S(1)}, u32[]{:S(2)}, u32[]{:S(2)}) async-start(bf16[4,1,2,16,48,128]{5,4,3,2,1,0:T(8,128)(2,1)} %get-tuple-element.96), calls=%async_computation.1 | async-start | bytes 3145728 | tf_op jit(solution)/shard_map/all_to_all | solution.py:323
  109.6 19.0 %all-to-all-done.1.refs_1_ = bf16[4,1,2,16,48,128]{5,4,3,2,1,0:T(8,128)(2,1)S(1)} async-done(((bf16[4,1,2,16,48,128]{5,4,3,2,1,0:T(8,128)(2,1)}), bf16[4,1,2,16,48,128]{5,4,3,2,1,0:T(8,128)(2,1)S(1)}, u32[]{:S(2)}, u32[]{:S(2)}) %all-to-all-start.1) | async-done | bytes 1572896 | tf_op jit(solution)/shard_map/all_to_all | solution.py:323
  132.2 3.2 %triangle.2 = (bf16[32,16,256]{2,1,0:T(8,128)(2,1)S(1)}, bf16[32,16,256]{2,1,0:T(8,128)(2,1)S(1)}, bf16[32,16,256]{2,1,0:T(8,128)(2,1)S(1)}, bf16[32,16,256]{2,1,0:T(8,128)(2,1)S(1)}) custom-call(s32[3]{0:T(128)S(1)} %pad_add_fusion.1.info, bf16[4,2,2,16,32,128]{5,4,3,2,1,0:T(8,128)(2,1)} %all-to-all-done.refs_0_, ...), custom_call_target="tpu_custom_call" | custom-call | flops 335544320 | bytes 10000000 | tf_op jit(solution)/shard_map/triangle/pallas_call | solution.py:506
  135.9 4.7 %collective-permute-done.18.refs_2_ = bf16[1,1,2,16,48,128]{5,4,3,2,1,0:T(8,128)(2,1)S(1)} collective-permute-done((bf16[1,1,2,16,48,128]{5,4,3,2,1,0:T(8,128)(2,1)S(1)}, bf16[1,1,2,16,48,128]{5,4,3,2,1,0:T(8,128)(2,1)S(1)}, u32[]{:S(2)}, u32[]{:S(2)}) %collective-permute-start.18) | collective-permute-done | bytes 393248 | tf_op jit(solution)/shard_map/ppermute | solution.py:311
  140.6 9.2 %collective-permute-done.19.refs_3_ = bf16[1,1,2,16,48,128]{5,4,3,2,1,0:T(8,128)(2,1)S(1)} collective-permute-done((bf16[1,1,2,16,48,128]{5,4,3,2,1,0:T(8,128)(2,1)S(1)}, bf16[1,1,2,16,48,128]{5,4,3,2,1,0:T(8,128)(2,1)S(1)}, u32[]{:S(2)}, u32[]{:S(2)}) %collective-permute-start.19) | collective-permute-done | bytes 393248 | tf_op jit(solution)/shard_map/ppermute | solution.py:311
  150.2 1.9 collective-permute-start.22
  153.5 3.2 %triangle.3 = (bf16[32,16,256]{2,1,0:T(8,128)(2,1)S(1)}, bf16[32,16,256]{2,1,0:T(8,128)(2,1)S(1)}, bf16[32,16,256]{2,1,0:T(8,128)(2,1)S(1)}, bf16[32,16,256]{2,1,0:T(8,128)(2,1)S(1)}) custom-call(s32[3]{0:T(128)S(1)} %pad_add_fusion.1.info, bf16[4,2,2,16,32,128]{5,4,3,2,1,0:T(8,128)(2,1)} %all-to-all-done.refs_0_, ...), custom_call_target="tpu_custom_call" | custom-call | flops 335544320 | bytes 10000000 | tf_op jit(solution)/shard_map/triangle/pallas_call | solution.py:506
  156.9 3.4 %collective-permute-start.25 = (bf16[32,16,256]{2,1,0:T(8,128)(2,1)S(1)}, bf16[32,16,256]{2,1,0:T(8,128)(2,1)S(1)}, u32[]{:S(2)}, u32[]{:S(2)}) collective-permute-start(bf16[32,16,256]{2,1,0:T(8,128)(2,1)S(1)} %get-tuple-element.112), channel_id=1, source_target_pairs={{0,16},{4,20},{8,24},{12,28},{16,0},{20,4},{24,8},{28,12},{1,17},{... | collective-permute-start | bytes 786440 | tf_op jit(solution)/shard_map/ppermute | solution.py:308
  160.3 10.8 %collective-permute-done.22.refs_3_ = bf16[32,16,256]{2,1,0:T(8,128)(2,1)S(1)} collective-permute-done((bf16[32,16,256]{2,1,0:T(8,128)(2,1)S(1)}, bf16[32,16,256]{2,1,0:T(8,128)(2,1)S(1)}, u32[]{:S(2)}, u32[]{:S(2)}) %collective-permute-start.22) | collective-permute-done | bytes 262176 | tf_op jit(solution)/shard_map/ppermute | solution.py:308
  172.1 3.4 %all-to-all-start.2 = ((bf16[4,16,16,128]{3,2,1,0:T(8,128)(2,1)}), bf16[4,16,16,128]{3,2,1,0:T(8,128)(2,1)S(1)}, u32[]{:S(2)}, u32[]{:S(2)}) async-start(bf16[4,16,16,128]{3,2,1,0:T(8,128)(2,1)} %gather.2), calls=%async_computation.2 | async-start | bytes 524288 | tf_op jit(solution)/shard_map/all_to_all | solution.py:323
  175.5 9.8 %collective-permute-done.25.refs_2_ = bf16[32,16,256]{2,1,0:T(8,128)(2,1)S(1)} collective-permute-done((bf16[32,16,256]{2,1,0:T(8,128)(2,1)S(1)}, bf16[32,16,256]{2,1,0:T(8,128)(2,1)S(1)}, u32[]{:S(2)}, u32[]{:S(2)}) %collective-permute-start.25) | collective-permute-done | bytes 262176 | tf_op jit(solution)/shard_map/ppermute | solution.py:308
  185.4 1.6 collective-permute-done.26.refs_3_
  187.3 8.3 %all_to_all.20.second = bf16[4,16,16,128]{3,2,1,0:T(8,128)(2,1)S(1)} all-to-all(bf16[4,16,16,128]{3,2,1,0:T(8,128)(2,1)S(1)} %gather.3), channel_id=1, replica_groups=mesh['row'=8,'col'=4] {'col'}, dimensions={0} | all-to-all | bytes 524288 | tf_op jit(solution)/shard_map/all_to_all | solution.py:323
  195.7 1.9 finish.1
  (123 shorter events, 34.2 us)
Async XLA Ops:
  1.4 17.3 %collective-permute-start = (bf16[48,128]{1,0:T(8,128)(2,1)S(1)}, bf16[48,128]{1,0:T(8,128)(2,1)S(1)}, u32[]{:S(2)}, u32[]{:S(2)}) collective-permute-start(bf16[48,128]{1,0:T(8,128)(2,1)S(1)} %get-tuple-element.125), channel_id=1, source_target_pairs={{0,1},{1,2},{2,3},{3,4},{4,5},{5,6},{6,7},{7,8},{8,9},{9,10},{10,1... | collective-permute-start | bytes 36872 | tf_op jit(solution)/shard_map/ppermute | solution.py:303
  4.8 13.9 %collective-permute-start.1 = (bf16[48,128]{1,0:T(8,128)(2,1)S(1)}, bf16[48,128]{1,0:T(8,128)(2,1)S(1)}, u32[]{:S(2)}, u32[]{:S(2)}) collective-permute-start(bf16[48,128]{1,0:T(8,128)(2,1)S(1)} %get-tuple-element.124), channel_id=1, source_target_pairs={{1,0},{2,1},{3,2},{4,3},{5,4},{6,5},{7,6},{8,7},{9,8},{10,9},{11,1... | collective-permute-start | bytes 36872 | tf_op jit(solution)/shard_map/ppermute | solution.py:304
  11.0 19.9 %collective-permute-start.5 = (bf16[32,32,128]{2,1,0:T(8,128)(2,1)}, bf16[32,32,128]{2,1,0:T(8,128)(2,1)S(1)}, u32[]{:S(2)}, u32[]{:S(2)}) collective-permute-start(bf16[32,32,128]{2,1,0:T(8,128)(2,1)} %bitcast.43), channel_id=1, source_target_pairs={{0,8},{4,12},{8,16},{12,20},{16,24},{20,28},{24,0},{28,4},{1,9},{5... | collective-permute-start | bytes 786440 | tf_op jit(solution)/shard_map/ppermute | solution.py:308
  13.4 21.1 %collective-permute-start.6 = (bf16[32,32,128]{2,1,0:T(8,128)(2,1)}, bf16[32,32,128]{2,1,0:T(8,128)(2,1)S(1)}, u32[]{:S(2)}, u32[]{:S(2)}) collective-permute-start(bf16[32,32,128]{2,1,0:T(8,128)(2,1)} %bitcast.42), channel_id=1, source_target_pairs={{0,16},{4,20},{8,24},{12,28},{16,0},{20,4},{24,8},{28,12},{1,17},{... | collective-permute-start | bytes 786440 | tf_op jit(solution)/shard_map/ppermute | solution.py:308
  15.2 20.9 %collective-permute-start.7 = (bf16[32,32,128]{2,1,0:T(8,128)(2,1)}, bf16[32,32,128]{2,1,0:T(8,128)(2,1)S(1)}, u32[]{:S(2)}, u32[]{:S(2)}) collective-permute-start(bf16[32,32,128]{2,1,0:T(8,128)(2,1)} %bitcast.41), channel_id=1, source_target_pairs={{0,24},{4,28},{8,0},{12,4},{16,8},{20,12},{24,16},{28,20},{1,25},{... | collective-permute-start | bytes 786440 | tf_op jit(solution)/shard_map/ppermute | solution.py:308
  20.9 5.0 %collective-permute-start.4 = (bf16[160,128]{1,0:T(8,128)(2,1)S(1)}, bf16[160,128]{1,0:T(8,128)(2,1)S(1)}, u32[]{:S(2)}, u32[]{:S(2)}) collective-permute-start(bf16[160,128]{1,0:T(8,128)(2,1)S(1)} %atoms.1), channel_id=1, source_target_pairs={{0,3},{1,2},{2,1},{3,0},{4,7},{5,6},{6,5},{7,4},{8,11},{9,10},{10,... | collective-permute-start | bytes 122888 | tf_op jit(solution)/shard_map/ppermute | solution.py:311
  21.8 6.6 %collective-permute-start.3 = (bf16[160,128]{1,0:T(8,128)(2,1)S(1)}, bf16[160,128]{1,0:T(8,128)(2,1)S(1)}, u32[]{:S(2)}, u32[]{:S(2)}) collective-permute-start(bf16[160,128]{1,0:T(8,128)(2,1)S(1)} %atoms.1), channel_id=1, source_target_pairs={{0,2},{1,3},{2,0},{3,1},{4,6},{5,7},{6,4},{7,5},{8,10},{9,11},{10,... | collective-permute-start | bytes 122888 | tf_op jit(solution)/shard_map/ppermute | solution.py:311
  25.9 4.0 %collective-permute-start.2 = (bf16[160,128]{1,0:T(8,128)(2,1)S(1)}, bf16[160,128]{1,0:T(8,128)(2,1)S(1)}, u32[]{:S(2)}, u32[]{:S(2)}) collective-permute-start(bf16[160,128]{1,0:T(8,128)(2,1)S(1)} %atoms.1), channel_id=1, source_target_pairs={{0,1},{1,0},{2,3},{3,2},{4,5},{5,4},{6,7},{7,6},{8,9},{9,8},{10,11... | collective-permute-start | bytes 122888 | tf_op jit(solution)/shard_map/ppermute | solution.py:311
  28.0 25.5 %copy-start.20 = (s32[1280]{0:T(1024)S(1)}, s32[1280]{0:T(1024)}, u32[]{:S(2)}) copy-start(s32[1280]{0:T(1024)} %get-tuple-element.114) | copy-start | bytes 15364
  28.0 31.2 %copy-start.6 = (bf16[128,384]{1,0:T(8,128)(2,1)S(1)}, bf16[128,384]{1,0:T(8,128)(2,1)}, u32[]{:S(2)}) copy-start(bf16[128,384]{1,0:T(8,128)(2,1)} %refs_7_.1) | copy-start | bytes 294916
  36.9 7.1 %collective-permute-start.8 = (bf16[640,128]{1,0:T(8,128)(2,1)S(1)}, bf16[640,128]{1,0:T(8,128)(2,1)S(1)}, u32[]{:S(2)}, u32[]{:S(2)}) collective-permute-start(bf16[640,128]{1,0:T(8,128)(2,1)S(1)} %pad_maximum_fusion.2.refs_0_), channel_id=1, source_target_pairs={{0,8},{4,12},{8,16},{12,20},{16,24},{20,28},{24,0},{28,4},{1,9},{5... | collective-permute-start | bytes 491528 | tf_op jit(solution)/shard_map/ppermute | solution.py:308
  36.9 14.5 %collective-permute-start.9 = (bf16[640,128]{1,0:T(8,128)(2,1)S(1)}, bf16[640,128]{1,0:T(8,128)(2,1)S(1)}, u32[]{:S(2)}, u32[]{:S(2)}) collective-permute-start(bf16[640,128]{1,0:T(8,128)(2,1)S(1)} %pad_maximum_fusion.2.refs_0_), channel_id=1, source_target_pairs={{0,16},{4,20},{8,24},{12,28},{16,0},{20,4},{24,8},{28,12},{1,17},{... | collective-permute-start | bytes 491528 | tf_op jit(solution)/shard_map/ppermute | solution.py:308
  38.5 13.8 %collective-permute-start.10 = (bf16[640,128]{1,0:T(8,128)(2,1)S(1)}, bf16[640,128]{1,0:T(8,128)(2,1)S(1)}, u32[]{:S(2)}, u32[]{:S(2)}) collective-permute-start(bf16[640,128]{1,0:T(8,128)(2,1)S(1)} %pad_maximum_fusion.2.refs_0_), channel_id=1, source_target_pairs={{0,24},{4,28},{8,0},{12,4},{16,8},{20,12},{24,16},{28,20},{1,25},{... | collective-permute-start | bytes 491528 | tf_op jit(solution)/shard_map/ppermute | solution.py:308
  53.4 5.8 %collective-permute-start.11 = (bf16[2560,128]{1,0:T(8,128)(2,1)}, bf16[2560,128]{1,0:T(8,128)(2,1)S(1)}, u32[]{:S(2)}, u32[]{:S(2)}) collective-permute-start(bf16[2560,128]{1,0:T(8,128)(2,1)} %pad_maximum_fusion.1), channel_id=1, source_target_pairs={{0,4},{4,0},{8,12},{12,8},{16,20},{20,16},{24,28},{28,24},{1,5},{5... | collective-permute-start | bytes 1966088 | tf_op jit(solution)/shard_map/ppermute | solution.py:314
  53.6 27.2 %collective-permute-start.12 = (bf16[48,32,128]{2,1,0:T(8,128)(2,1)}, bf16[48,32,128]{2,1,0:T(8,128)(2,1)}, u32[]{:S(2)}, u32[]{:S(2)}) collective-permute-start(bf16[48,32,128]{2,1,0:T(8,128)(2,1)} %get-tuple-element.83), channel_id=1, source_target_pairs={{0,8},{4,12},{8,16},{12,20},{16,24},{20,28},{24,0},{28,4},{1,9},{5... | collective-permute-start | bytes 1179656 | tf_op jit(solution)/shard_map/ppermute | solution.py:308
  53.6 34.9 %collective-permute-start.13 = (bf16[48,32,128]{2,1,0:T(8,128)(2,1)}, bf16[48,32,128]{2,1,0:T(8,128)(2,1)}, u32[]{:S(2)}, u32[]{:S(2)}) collective-permute-start(bf16[48,32,128]{2,1,0:T(8,128)(2,1)} %get-tuple-element.84), channel_id=1, source_target_pairs={{0,16},{4,20},{8,24},{12,28},{16,0},{20,4},{24,8},{28,12},{1,17},{... | collective-permute-start | bytes 1179656 | tf_op jit(solution)/shard_map/ppermute | solution.py:308
  56.1 35.3 %collective-permute-start.14 = (bf16[48,32,128]{2,1,0:T(8,128)(2,1)}, bf16[48,32,128]{2,1,0:T(8,128)(2,1)}, u32[]{:S(2)}, u32[]{:S(2)}) collective-permute-start(bf16[48,32,128]{2,1,0:T(8,128)(2,1)} %get-tuple-element.85), channel_id=1, source_target_pairs={{0,24},{4,28},{8,0},{12,4},{16,8},{20,12},{24,16},{28,20},{1,25},{... | collective-permute-start | bytes 1179656 | tf_op jit(solution)/shard_map/ppermute | solution.py:308
  76.2 29.7 %all-to-all-start = ((bf16[4,2,2,16,32,128]{5,4,3,2,1,0:T(8,128)(2,1)}), bf16[4,2,2,16,32,128]{5,4,3,2,1,0:T(8,128)(2,1)}, u32[]{:S(2)}, u32[]{:S(2)}) async-start(bf16[4,2,2,16,32,128]{5,4,3,2,1,0:T(8,128)(2,1)} %pair.2), calls=%async_computation | async-start | bytes 4194304 | tf_op jit(solution)/shard_map/all_to_all | solution.py:323
  105.9 22.8 %all-to-all-start.1 = ((bf16[4,1,2,16,48,128]{5,4,3,2,1,0:T(8,128)(2,1)}), bf16[4,1,2,16,48,128]{5,4,3,2,1,0:T(8,128)(2,1)S(1)}, u32[]{:S(2)}, u32[]{:S(2)}) async-start(bf16[4,1,2,16,48,128]{5,4,3,2,1,0:T(8,128)(2,1)} %get-tuple-element.96), calls=%async_computation.1 | async-start | bytes 3145728 | tf_op jit(solution)/shard_map/all_to_all | solution.py:323
  109.6 22.6 %collective-permute-start.15 = (bf16[4,2,2,16,32,128]{5,4,3,2,1,0:T(8,128)(2,1)}, bf16[4,2,2,16,32,128]{5,4,3,2,1,0:T(8,128)(2,1)}, u32[]{:S(2)}, u32[]{:S(2)}) collective-permute-start(bf16[4,2,2,16,32,128]{5,4,3,2,1,0:T(8,128)(2,1)} %all-to-all-done.refs_0_), channel_id=1, source_target_pairs={{0,4},{4,0},{8,12},{12,8},{16,20},{20,16},{24,28},{28,24},{1,5},{5... | collective-permute-start | bytes 6291464 | tf_op jit(solution)/shard_map/ppermute | solution.py:314
  128.7 3.5 %collective-permute-start.16 = (bf16[4,1,2,16,48,128]{5,4,3,2,1,0:T(8,128)(2,1)S(1)}, bf16[4,1,2,16,48,128]{5,4,3,2,1,0:T(8,128)(2,1)S(1)}, u32[]{:S(2)}, u32[]{:S(2)}) collective-permute-start(bf16[4,1,2,16,48,128]{5,4,3,2,1,0:T(8,128)(2,1)S(1)} %all-to-all-done.1.refs_1_), channel_id=1, source_target_pairs={{0,4},{4,0},{8,12},{12,8},{16,20},{20,16},{24,28},{28,24},{1,5},{5... | collective-permute-start | bytes 4718600 | tf_op jit(solution)/shard_map/ppermute | solution.py:314
  128.7 11.9 %collective-permute-start.18 = (bf16[1,1,2,16,48,128]{5,4,3,2,1,0:T(8,128)(2,1)S(1)}, bf16[1,1,2,16,48,128]{5,4,3,2,1,0:T(8,128)(2,1)S(1)}, u32[]{:S(2)}, u32[]{:S(2)}) collective-permute-start(bf16[1,1,2,16,48,128]{5,4,3,2,1,0:T(8,128)(2,1)S(1)} %copy-done.15), channel_id=1, source_target_pairs={{0,1},{1,0},{2,3},{3,2},{4,5},{5,4},{6,7},{7,6},{8,9},{9,8},{10,11... | collective-permute-start | bytes 1179656 | tf_op jit(solution)/shard_map/ppermute | solution.py:311
  130.1 19.7 %collective-permute-start.19 = (bf16[1,1,2,16,48,128]{5,4,3,2,1,0:T(8,128)(2,1)S(1)}, bf16[1,1,2,16,48,128]{5,4,3,2,1,0:T(8,128)(2,1)S(1)}, u32[]{:S(2)}, u32[]{:S(2)}) collective-permute-start(bf16[1,1,2,16,48,128]{5,4,3,2,1,0:T(8,128)(2,1)S(1)} %copy-done.13), channel_id=1, source_target_pairs={{0,2},{1,3},{2,0},{3,1},{4,6},{5,7},{6,4},{7,5},{8,10},{9,11},{10,... | collective-permute-start | bytes 1179656 | tf_op jit(solution)/shard_map/ppermute | solution.py:311
  130.7 19.1 %collective-permute-start.20 = (bf16[1,1,2,16,48,128]{5,4,3,2,1,0:T(8,128)(2,1)S(1)}, bf16[1,1,2,16,48,128]{5,4,3,2,1,0:T(8,128)(2,1)S(1)}, u32[]{:S(2)}, u32[]{:S(2)}) collective-permute-start(bf16[1,1,2,16,48,128]{5,4,3,2,1,0:T(8,128)(2,1)S(1)} %get-tuple-element.102), channel_id=1, source_target_pairs={{0,3},{1,2},{2,1},{3,0},{4,7},{5,6},{6,5},{7,4},{8,11},{9,10},{10,... | collective-permute-start | bytes 1179656 | tf_op jit(solution)/shard_map/ppermute | solution.py:311
  135.4 14.4 %collective-permute-start.21 = (bf16[32,16,256]{2,1,0:T(8,128)(2,1)S(1)}, bf16[32,16,256]{2,1,0:T(8,128)(2,1)S(1)}, u32[]{:S(2)}, u32[]{:S(2)}) collective-permute-start(bf16[32,16,256]{2,1,0:T(8,128)(2,1)S(1)} %get-tuple-element.103), channel_id=1, source_target_pairs={{0,16},{4,20},{8,24},{12,28},{16,0},{20,4},{24,8},{28,12},{1,17},{... | collective-permute-start | bytes 786440 | tf_op jit(solution)/shard_map/ppermute | solution.py:308
  150.0 3.5 %collective-permute-start.23 = (bf16[4,1,2,16,48,128]{5,4,3,2,1,0:T(8,128)(2,1)S(1)}, bf16[4,1,2,16,48,128]{5,4,3,2,1,0:T(8,128)(2,1)S(1)}, u32[]{:S(2)}, u32[]{:S(2)}) collective-permute-start(bf16[4,1,2,16,48,128]{5,4,3,2,1,0:T(8,128)(2,1)S(1)} %pad_maximum_fusion), channel_id=1, source_target_pairs={{0,4},{4,0},{8,12},{12,8},{16,20},{20,16},{24,28},{28,24},{1,5},{5... | collective-permute-start | bytes 4718600 | tf_op jit(solution)/shard_map/ppermute | solution.py:314
  150.1 10.2 %collective-permute-start.17 = (bf16[32,16,256]{2,1,0:T(8,128)(2,1)S(1)}, bf16[32,16,256]{2,1,0:T(8,128)(2,1)S(1)}, u32[]{:S(2)}, u32[]{:S(2)}) collective-permute-start(bf16[32,16,256]{2,1,0:T(8,128)(2,1)S(1)} %get-tuple-element.98), channel_id=1, source_target_pairs={{0,8},{4,12},{8,16},{12,20},{16,24},{20,28},{24,0},{28,4},{1,9},{5... | collective-permute-start | bytes 786440 | tf_op jit(solution)/shard_map/ppermute | solution.py:308
  150.2 20.8 %collective-permute-start.22 = (bf16[32,16,256]{2,1,0:T(8,128)(2,1)S(1)}, bf16[32,16,256]{2,1,0:T(8,128)(2,1)S(1)}, u32[]{:S(2)}, u32[]{:S(2)}) collective-permute-start(bf16[32,16,256]{2,1,0:T(8,128)(2,1)S(1)} %get-tuple-element.105), channel_id=1, source_target_pairs={{0,24},{4,28},{8,0},{12,4},{16,8},{20,12},{24,16},{28,20},{1,25},{... | collective-permute-start | bytes 786440 | tf_op jit(solution)/shard_map/ppermute | solution.py:308
  156.7 18.8 %collective-permute-start.24 = (bf16[32,16,256]{2,1,0:T(8,128)(2,1)S(1)}, bf16[32,16,256]{2,1,0:T(8,128)(2,1)S(1)}, u32[]{:S(2)}, u32[]{:S(2)}) collective-permute-start(bf16[32,16,256]{2,1,0:T(8,128)(2,1)S(1)} %get-tuple-element.111), channel_id=1, source_target_pairs={{0,8},{4,12},{8,16},{12,20},{16,24},{20,28},{24,0},{28,4},{1,9},{5... | collective-permute-start | bytes 786440 | tf_op jit(solution)/shard_map/ppermute | solution.py:308
  156.9 28.5 %collective-permute-start.25 = (bf16[32,16,256]{2,1,0:T(8,128)(2,1)S(1)}, bf16[32,16,256]{2,1,0:T(8,128)(2,1)S(1)}, u32[]{:S(2)}, u32[]{:S(2)}) collective-permute-start(bf16[32,16,256]{2,1,0:T(8,128)(2,1)S(1)} %get-tuple-element.112), channel_id=1, source_target_pairs={{0,16},{4,20},{8,24},{12,28},{16,0},{20,4},{24,8},{28,12},{1,17},{... | collective-permute-start | bytes 786440 | tf_op jit(solution)/shard_map/ppermute | solution.py:308
  160.3 26.7 %collective-permute-start.26 = (bf16[32,16,256]{2,1,0:T(8,128)(2,1)S(1)}, bf16[32,16,256]{2,1,0:T(8,128)(2,1)S(1)}, u32[]{:S(2)}, u32[]{:S(2)}) collective-permute-start(bf16[32,16,256]{2,1,0:T(8,128)(2,1)S(1)} %get-tuple-element.113), channel_id=1, source_target_pairs={{0,24},{4,28},{8,0},{12,4},{16,8},{20,12},{24,16},{28,20},{1,25},{... | collective-permute-start | bytes 786440 | tf_op jit(solution)/shard_map/ppermute | solution.py:308
  172.1 15.2 %all-to-all-start.2 = ((bf16[4,16,16,128]{3,2,1,0:T(8,128)(2,1)}), bf16[4,16,16,128]{3,2,1,0:T(8,128)(2,1)S(1)}, u32[]{:S(2)}, u32[]{:S(2)}) async-start(bf16[4,16,16,128]{3,2,1,0:T(8,128)(2,1)} %gather.2), calls=%async_computation.2 | async-start | bytes 524288 | tf_op jit(solution)/shard_map/all_to_all | solution.py:323
  (23 other events, 213.0 us)
